TPU v7x, 512 devices: a whole 4x8x8 slice. The times are simulated.
512 devices in a mesh: ctx: 32 (over x, y), ts: 16 (over z, core).
Axes of the slice: x: 4, y: 8, z: 8, core: 2. Of those that a mesh axis runs over, the one named last changes fastest.
Arguments:
- projected: bfloat16 [65536, 12288], P(('ctx', 'ts')), may hold values from -6 to 6
- doc_lengths: int32 [16], replicated, may hold values from 1 to 16384, 65536 in all
- short_taps: float32 [3, 7, 256], replicated, may hold values from -2.4 to 2.4
- medium_taps: float32 [128, 256], replicated, may hold values from -0.5 to 0.5
- decay_rates: float32 [16, 256], replicated, may hold values from 3.8146973e-06 to 0.03
- residues: float32 [16, 256], replicated, may hold values from -1.5 to 1.5
- skip_gain: float32 [4096], replicated, may hold values from -3 to 3
Outputs:
- hyena_out: bfloat16 [65536, 4096], P(('ctx', 'ts'))
Inputs may be any that keep to these rules, and one draw needn't show every extreme that they name: `doc_lengths`: the lengths sum to 65536; the largest is exactly 16384.
All inputs are finite; a program needn't handle non-finite values.
Results may differ from a plain program's by a relative error of at most 0.01.
Values may be sent and summed in bfloat16 or wider, within the bound.
No kernel may reach another device: no remote copies, remote signals or barrier semaphores. Data moves between devices by JAX's collectives and lax.ppermute only.
A program may use at most 128 MiB of HBM per device.

v0:
```python
import jax
import jax.numpy as jnp
from jax import lax
from jax.sharding import PartitionSpec as P

GROUP = 16
SHORT = 7
MEDIUM = 128
MODES = 16


HIGHEST = lax.Precision.HIGHEST


def from_behind(value, axis, by):
    length = lax.axis_size(axis)
    pairs = [(i, i + by) for i in range(length) if 0 <= i + by < length]
    return lax.ppermute(value, axis, pairs)


def copy_for_each(value, axis):
    copies = jnp.broadcast_to(value, (lax.axis_size(axis), *value.shape))
    return lax.all_to_all(copies, axis, split_axis=0, concat_axis=0, tiled=True)


def collected_together(value, axis):
    leaves = jax.tree.leaves(value)
    order = sorted(range(len(leaves)), key=lambda k: -leaves[k].size)
    width = (1, *leaves[order[0]].shape)[-1]
    lines = [
        jnp.pad(leaves[k].reshape(-1), (0, -leaves[k].size % width)).reshape(-1, width)
        for k in order
    ]
    both, at, found = (copy_for_each(jnp.concatenate(lines), axis), 0, {})
    for k, line in zip(order, lines):
        section = both[:, at : at + len(line)].reshape(len(both), -1)
        found[k] = section[:, : leaves[k].size].reshape(-1, *leaves[k].shape)
        at += len(line)
    numbers = iter(range(len(leaves)))
    return jax.tree.map(lambda _: found[next(numbers)], value)


def folded_in_pairs(pieces, combine):
    while len(jax.tree.leaves(pieces)[0]) > 1:
        pieces = jax.vmap(combine)(
            *(jax.tree.map(lambda part: part[side::2], pieces) for side in (0, 1))
        )
    return jax.tree.map(lambda part: part[0], pieces)


def entering(value, axis, combine, identity):
    length, position = (lax.axis_size(axis), lax.axis_index(axis))
    passed = jnp.arange(length) < position

    def kept(part, zero, own):
        part = jnp.where(
            passed.reshape(-1, *(1 for _ in own.shape)), part, jnp.asarray(zero, own.dtype)
        )
        return part

    pieces = collected_together(value, axis)
    return folded_in_pairs(jax.tree.map(kept, pieces, identity, value), combine)


def starts_for(positions, doc_lengths):
    doc_ends = jnp.cumsum(doc_lengths)
    doc_begins = doc_ends - doc_lengths
    inside = doc_begins[None, :] <= positions[:, None]
    return jnp.max(jnp.where(inside, doc_begins[None, :], 0), axis=1)


def featurize(window, positions, row_start, tap_table):
    row_count = positions.shape[0]
    summed = jnp.zeros((row_count,) + window.shape[1:], jnp.float32)
    for offset in range(SHORT):
        in_doc = positions - offset >= row_start
        shifted = window[SHORT - 1 - offset : SHORT - 1 - offset + row_count]
        summed = summed + jnp.where(
            in_doc[:, None, None], shifted * tap_table[:, offset][None], 0.0
        )
    return summed


def filter_tables(decay_rates, residues):
    scaled = residues * jnp.sqrt(-jnp.expm1(-2.0 * decay_rates))
    steps_f = jnp.arange(MEDIUM).astype(jnp.float32)
    long_table = jnp.sum(
        scaled[None] * jnp.exp(-decay_rates[None] * steps_f[:, None, None]), axis=1
    )
    return (scaled, long_table)


def band_matrix(medium_taps, long_table, row_pos, col_pos, block_begin):
    distance = row_pos[:, None] - col_pos[None, :]
    in_band = (distance >= 0) & (distance < MEDIUM)
    lag_index = jnp.clip(distance, 0, MEDIUM - 1)
    same_block = (col_pos >= block_begin)[None, :, None]
    tap_values = medium_taps[lag_index] + jnp.where(same_block, long_table[lag_index], 0.0)
    return jnp.where(in_band[:, :, None], tap_values, 0.0)


def split_pieces(matrix):
    upper = matrix.astype(jnp.bfloat16)
    rest = matrix - upper.astype(jnp.float32)
    middle = rest.astype(jnp.bfloat16)
    lower = (rest - middle.astype(jnp.float32)).astype(jnp.bfloat16)
    return jnp.stack([upper, middle, lower], axis=0)


def combine(earlier, later):
    return (earlier[0] * later[0], later[0] * earlier[1] + later[1])


def per_device(projected, doc_lengths, short_taps, medium_taps, decay_rates, residues, skip_gain):
    ts_count = lax.axis_size("ts")
    ts_index = lax.axis_index("ts")
    ctx_index = lax.axis_index("ctx")
    tok_rows = projected.shape[0]
    width = projected.shape[1] // 3
    span_rows = tok_rows * ts_count
    local_width = width // ts_count
    local_groups = local_width // GROUP
    blocks_dev = span_rows // MEDIUM
    group_begin = ts_index * local_groups
    my_medium = lax.dynamic_slice_in_dim(medium_taps, group_begin, local_groups, 1)
    my_rates = lax.dynamic_slice_in_dim(decay_rates, group_begin, local_groups, 1)
    my_residues = lax.dynamic_slice_in_dim(residues, group_begin, local_groups, 1)
    my_skip = lax.dynamic_slice_in_dim(skip_gain, ts_index * local_width, local_width, 0)
    scaled, long_table = filter_tables(my_rates, my_residues)
    span_begin = ctx_index * span_rows
    chan_pos = span_begin + jnp.arange(span_rows, dtype=jnp.int32)
    chan_start = starts_for(chan_pos, doc_lengths)
    stacked = projected.reshape(tok_rows, 3, width)
    switched = lax.all_to_all(stacked, "ts", split_axis=2, concat_axis=0, tiled=True)
    edge_raw = from_behind(switched[span_rows - (SHORT - 1) :], "ctx", 1)
    my_short = jnp.repeat(
        lax.dynamic_slice_in_dim(short_taps, group_begin, local_groups, 2), GROUP, axis=2
    )
    window = jnp.concatenate([edge_raw, switched], axis=0).astype(jnp.float32)
    feature = featurize(window, chan_pos, chan_start, my_short)
    query = feature[:, 0]
    product = (feature[:, 1] * feature[:, 2]).astype(jnp.bfloat16)
    edge_rows = from_behind(product[span_rows - MEDIUM :], "ctx", 1)
    extended = jnp.concatenate([edge_rows, product], axis=0)
    rel_rows = MEDIUM + jnp.arange(MEDIUM, dtype=jnp.int32)
    rel_cols = jnp.arange(2 * MEDIUM, dtype=jnp.int32)
    pieces = split_pieces(band_matrix(my_medium, long_table, rel_rows, rel_cols, MEDIUM))
    local_f = jnp.arange(MEDIUM).astype(jnp.float32)
    decay_rows = scaled[None] * jnp.exp(-my_rates[None] * (local_f + 1.0)[:, None, None])
    tail_power = jnp.exp(-my_rates[None] * (MEDIUM - 1.0 - local_f)[:, None, None])
    block_decay = jnp.exp(-my_rates * MEDIUM)
    product_f = product.astype(jnp.float32).reshape(blocks_dev, MEDIUM, local_width)
    start_rows = chan_start.reshape(blocks_dev, MEDIUM)
    pos_rows = chan_pos.reshape(blocks_dev, MEDIUM)
    begins_dev = pos_rows[:, 0]
    last_start = start_rows[:, MEDIUM - 1]
    kept_rows = jnp.where((pos_rows >= last_start[:, None])[:, :, None], product_f, 0.0)
    kept_rows = kept_rows.reshape(blocks_dev, MEDIUM, local_groups, GROUP)
    contribution = jnp.einsum("umg,bugc->bmgc", tail_power, kept_rows, precision=HIGHEST).reshape(
        blocks_dev, MODES, local_width
    )
    factors = jnp.where((last_start < begins_dev)[:, None, None], block_decay[None], 0.0)
    factors = jnp.repeat(factors, GROUP, axis=2)

    def local_step(carry_pair, inputs):
        decay_acc, state_acc = carry_pair
        factor, term = inputs
        decay_acc = factor * decay_acc
        state_acc = factor * state_acc + term
        return ((decay_acc, state_acc), (decay_acc, state_acc))

    ones_state = jnp.ones((MODES, local_width), jnp.float32)
    zero_state = jnp.zeros((MODES, local_width), jnp.float32)
    finals, stacks = lax.scan(local_step, (ones_state, zero_state), (factors, contribution))
    decay_cum, state_loc = stacks
    total_decay = decay_cum[blocks_dev - 1]
    total_state = state_loc[blocks_dev - 1]

    def block_filter(block_idx):
        block_begin = span_begin + block_idx * MEDIUM
        row_pos = block_begin + jnp.arange(MEDIUM, dtype=jnp.int32)
        row_start = starts_for(row_pos, doc_lengths)
        col_pos = block_begin - MEDIUM + rel_cols
        allowed = col_pos[None, :] >= row_start[:, None]
        masked = jnp.where(allowed[None, :, :, None], pieces, jnp.zeros((), jnp.bfloat16))
        window_x = lax.dynamic_slice_in_dim(extended, block_idx * MEDIUM, 2 * MEDIUM, 0)
        window_x = window_x.reshape(2 * MEDIUM, local_groups, GROUP)
        return jnp.einsum(
            "ptug,ugc->tgc", masked, window_x, preferred_element_type=jnp.float32
        ).reshape(MEDIUM, local_width)

    banded = lax.map(block_filter, jnp.arange(blocks_dev, dtype=jnp.int32))
    prefix = entering((total_decay, total_state), "ctx", combine, (ones_state, zero_state))
    state_in = prefix[1]
    previous_states = jnp.concatenate([zero_state[None], state_loc[: blocks_dev - 1]], axis=0)
    previous_states = (
        previous_states
        + jnp.concatenate([ones_state[None], decay_cum[: blocks_dev - 1]], axis=0) * state_in[None]
    )
    carried_part = jnp.einsum(
        "tmg,bmgc->btgc",
        decay_rows,
        previous_states.reshape(blocks_dev, MODES, local_groups, GROUP),
        precision=HIGHEST,
    )
    carried_part = carried_part.reshape(blocks_dev, MEDIUM, local_width)
    carried_part = jnp.where((start_rows < begins_dev[:, None])[:, :, None], carried_part, 0.0)
    filtered = (
        (banded + carried_part + my_skip[None, None, :] * product_f)
        .reshape(span_rows, local_width)
        .astype(jnp.bfloat16)
    )
    outgoing = (query * filtered.astype(jnp.float32)).astype(jnp.bfloat16)
    returned = lax.all_to_all(outgoing, "ts", split_axis=0, concat_axis=1, tiled=True)
    return returned


def solution(mesh):
    return jax.shard_map(
        per_device,
        mesh=mesh,
        in_specs=(P(("ctx", "ts"), None), P(), P(), P(), P(), P(), P()),
        out_specs=P(("ctx", "ts"), None),
        check_vma=False,
    )
```

profile of v0, /device:TPU:1, one launch (start us, length us, event | category | flops | bytes accessed | tf_op | source)
XLA Modules:
  0.0 498.9 jit_solution(17720436163595369607)
XLA Ops:
  0.0 3.5 copy.123
  3.5 20.6 %copy.124 = bf16[128,3,4096]{0,1,2:T(4,128)(2,1)} copy(bf16[128,3,4096]{0,2,1:T(8,128)(2,1)S(1)} %bitcast.116) | data formatting | bytes 6291456 | tf_op jit(solution)/shard_map/reshape | solution.py:133
  24.1 12.0 %all-to-all-start = ((bf16[128,3,4096]{0,1,2:T(4,128)(2,1)}), bf16[128,3,4096]{0,1,2:T(4,128)(2,1)}, u32[]{:S(2)}, u32[]{:S(2)}) async-start(bf16[128,3,4096]{0,1,2:T(4,128)(2,1)} %copy.124), calls=%async_computation | async-start | bytes 8388608 | tf_op jit(solution)/shard_map/all_to_all | solution.py:134
  38.0 109.0 %gather_fusion.1 = f32[32768,16]{1,0:T(8,128)} fusion(f32[128,16]{1,0:T(8,128)S(1)} %copy.129, s32[32768]{0:T(1024)S(1)} %broadcast_clamp_fusion), kind=kCustom, calls=%fused_computation.1 | custom fusion | bytes 4325376 | tf_op jit(solution)/shard_map/gather | solution.py:98
  147.0 9.8 %copy.130 = f32[1,128,256,16]{2,3,1,0:T(8,128)S(1)} copy(f32[1,128,256,16]{3,2,1,0:T(8,128)} %bitcast.110) | data formatting | bytes 4194304 | tf_op jit(solution)/shard_map/gather | solution.py:98
  156.9 109.0 %gather_fusion = f32[32768,16]{1,0:T(8,128)} fusion(f32[128,16]{1,0:T(8,128)S(1)} %constant_dynamic-slice_fusion.1, s32[32768]{0:T(1024)S(1)} %broadcast_clamp_fusion), kind=kCustom, calls=%fused_computation | custom fusion | bytes 4325376 | tf_op jit(solution)/shard_map/gather | solution.py:98
  265.9 10.6 %copy.131 = f32[1,128,256,16]{2,3,1,0:T(8,128)} copy(f32[1,128,256,16]{3,2,1,0:T(8,128)} %bitcast.109) | data formatting | bytes 4194304 | tf_op jit(solution)/shard_map/gather | solution.py:98
  278.0 2.3 fusion.47
  284.8 4.3 copy.125
  289.1 4.7 copy.126
  293.8 1.3 slice.198
  295.1 3.8 collective-permute-start
  300.0 2.0 broadcast_in_dim.255
  302.0 2.4 reshape.406
  304.4 1.3 dynamic_slice.39
  305.9 2.5 maximum_convert_fusion
  308.5 8.2 %fusion.5 = f32[2048,3,256]{2,0,1:T(8,128)S(1)} fusion(f32[2054,3,256]{2,0,1:T(8,128)S(1)} %maximum_convert_fusion, f32[3,256]{1,0:T(4,128)S(1)} %copy-done.10, f32[3,256]{1,0:T(4,128)S(1)} %copy-done.11, f32[3,256]{1,0:T(4,128)S(1)} %copy-done.12, f32[3,256]{1,0:T(4,128)S(1)} %copy-done.13, f32[3,256]{1,0:T(4,128)S(1)} %copy-done.14, ...), kind=kLoop, calls=%fused_computation.19 | loop fusion | flops 31457280 | bytes 50367488 | tf_op jit(solution)/shard_map/add | solution.py:78
  316.7 2.7 fusion.48
  319.4 2.7 copy.134
  322.0 2.0 copy.158
  324.7 3.9 fusion.22
  328.6 3.2 copy.136
  331.8 3.1 reshape.407
  334.8 21.4 %while.33 = (s32[]{:T(128)}, f32[16,256]{1,0:T(8,128)S(1)}, f32[16,256]{1,0:T(8,128)S(1)}, f32[16,16,256]{2,1,0:T(8,128)}, f32[16,16,256]{2,1,0:T(8,128)}, /*index=5*/f32[16,16,256]{2,1,0:T(8,128)S(1)}, f32[16,16,256]{2,1,0:T(8,128)}) while((s32[]{:T(128)}, f32[16,256]{1,0:T(8,128)S(1)}, f32[16,256]{1,0:T(8,128)S(1)}, ...), condition=%wide.region_8.9_spmd.clone.clone, body=%wide.region_7.8_spmd.clone.sunk.clone | while | flops 20483 | bytes 131671 | solution.py:174
  334.8 1.3 bitcast_dynamic-update-slice_fusion.4
  336.2 1.3 bitcast_dynamic-update-slice_fusion.4
  337.5 1.3 bitcast_dynamic-update-slice_fusion.4
  338.9 1.3 bitcast_dynamic-update-slice_fusion.4
  340.2 1.3 bitcast_dynamic-update-slice_fusion.4
  341.5 1.3 bitcast_dynamic-update-slice_fusion.4
  342.9 1.3 bitcast_dynamic-update-slice_fusion.4
  344.2 1.3 bitcast_dynamic-update-slice_fusion.4
  345.5 1.3 bitcast_dynamic-update-slice_fusion.4
  346.9 1.3 bitcast_dynamic-update-slice_fusion.4
  348.2 1.3 bitcast_dynamic-update-slice_fusion.4
  349.5 1.3 bitcast_dynamic-update-slice_fusion.4
  350.9 1.3 bitcast_dynamic-update-slice_fusion.4
  352.2 1.3 bitcast_dynamic-update-slice_fusion.4
  353.6 1.3 bitcast_dynamic-update-slice_fusion.4
  354.9 1.3 bitcast_dynamic-update-slice_fusion.4
  356.9 1.6 slice.169
  359.3 1.7 slice.170
  361.8 2.8 collective-permute-start.1
  364.6 1.1 broadcast_in_dim.259
  365.7 8.4 %all-to-all-start.1 = ((f32[32,32,256]{2,1,0:T(8,128)}), f32[32,32,256]{2,1,0:T(8,128)}, u32[]{:S(2)}, u32[]{:S(2)}) async-start(f32[32,32,256]{2,1,0:T(8,128)} %broadcast_in_dim.259), calls=%async_computation.1 | async-start | bytes 2097152 | tf_op jit(solution)/shard_map/all_to_all | solution.py:23
  374.1 2.3 pad_maximum_fusion.1
  376.4 72.1 %while.32 = (s32[]{:T(128)}, f32[16,128,256]{2,1,0:T(8,128)}, s32[16]{0:T(128)S(1)}, bf16[2176,256]{1,0:T(8,128)(2,1)}, s32[]{:T(128)}, /*index=5*/s32[1,16]{1,0...) while((s32[]{:T(128)}, f32[16,128,256]{2,1,0:T(8,128)}, s32[16]{0:T(128)S(1)}, ...), condition=%wide.region_6.7_spmd.clone.clone, body=%wide.region_3.6_spmd.clone.sunk.clone | while | flops 21010696 | bytes 6623987 | solution.py:192
  377.7 0.9 constant_dynamic-slice_fusion.5
  382.1 0.9 constant_dynamic-slice_fusion.5
  386.7 0.9 constant_dynamic-slice_fusion.5
  391.2 0.9 constant_dynamic-slice_fusion.5
  395.7 0.9 constant_dynamic-slice_fusion.5
  400.2 0.9 constant_dynamic-slice_fusion.5
  404.7 0.9 constant_dynamic-slice_fusion.5
  409.2 0.9 constant_dynamic-slice_fusion.5
  413.7 0.9 constant_dynamic-slice_fusion.5
  418.2 0.9 constant_dynamic-slice_fusion.5
  431.7 0.9 constant_dynamic-slice_fusion.5
  448.5 1.4 slice_select_fusion.1
  450.9 3.8 fusion.25
  455.0 1.9 copy.139
  456.9 3.7 multiply_convert_fusion
  460.6 36.3 %all_to_all.39 = bf16[16,128,256]{2,1,0:T(8,128)(2,1)S(1)} all-to-all(bf16[16,128,256]{2,1,0:T(8,128)(2,1)S(1)} %multiply_convert_fusion), channel_id=1, replica_groups=mesh['ctx'=32,'ts'=16] {'ts'}, dimensions={0} | all-to-all | bytes 2097152 | tf_op jit(solution)/shard_map/all_to_all | solution.py:214
  497.6 1.3 copy.142
  (300 shorter events, 64.3 us)
Async XLA Ops:
  0.0 156.8 %copy-start = (f32[128,256]{1,0:T(8,128)S(1)}, f32[128,256]{1,0:T(8,128)}, u32[]{:S(2)}) copy-start(f32[128,256]{1,0:T(8,128)} %param.14) | copy-start | bytes 393220
  24.1 12.0 %copy-start.26 = (f32[3,7,256]{2,1,0:T(8,128)S(1)}, f32[3,7,256]{2,1,0:T(8,128)}, u32[]{:S(2)}) copy-start(f32[3,7,256]{2,1,0:T(8,128)} %param.13) | copy-start | bytes 64516
  24.1 12.3 %copy-start.33 = (s32[16]{0:T(128)S(1)}, s32[16]{0:T(128)}, u32[]{:S(2)}) copy-start(s32[16]{0:T(128)} %param.12) | copy-start | bytes 196
  24.1 12.6 %copy-start.27 = (f32[16,256]{1,0:T(8,128)S(1)}, f32[16,256]{1,0:T(8,128)}, u32[]{:S(2)}) copy-start(f32[16,256]{1,0:T(8,128)} %param.15) | copy-start | bytes 49156
  24.1 12.6 %copy-start.28 = (f32[16,256]{1,0:T(8,128)S(1)}, f32[16,256]{1,0:T(8,128)}, u32[]{:S(2)}) copy-start(f32[16,256]{1,0:T(8,128)} %param.16) | copy-start | bytes 49156
  24.1 260.7 %all-to-all-start = ((bf16[128,3,4096]{0,1,2:T(4,128)(2,1)}), bf16[128,3,4096]{0,1,2:T(4,128)(2,1)}, u32[]{:S(2)}, u32[]{:S(2)}) async-start(bf16[128,3,4096]{0,1,2:T(4,128)(2,1)} %copy.124), calls=%async_computation | async-start | bytes 8388608 | tf_op jit(solution)/shard_map/all_to_all | solution.py:134
  36.7 239.9 %copy-start.34 = (s32[16]{0:T(128)}, s32[16]{0:T(128)S(1)}, u32[]{:S(2)}) copy-start(s32[16]{0:T(128)S(1)} %sub.106) | copy-start | bytes 196
  36.9 0.6 copy-start.5
  36.9 0.6 copy-start.8
  295.1 10.8 %collective-permute-start = (bf16[6,3,256]{2,0,1:T(8,128)(2,1)}, bf16[6,3,256]{2,0,1:T(8,128)(2,1)}, u32[]{:S(2)}, u32[]{:S(2)}) collective-permute-start(bf16[6,3,256]{2,0,1:T(8,128)(2,1)} %slice.198), channel_id=1, source_target_pairs={{0,16},{16,32},{32,48},{48,64},{64,80},{80,96},{96,112},{112,128},... | collective-permute-start | bytes 27656 | tf_op jit(solution)/shard_map/ppermute | solution.py:18
  305.7 2.6 copy-start.10
  305.7 2.6 copy-start.11
  305.7 2.7 copy-start.12
  305.7 2.7 copy-start.13
  305.7 2.7 copy-start.14
  305.8 2.7 copy-start.15
  305.8 2.7 copy-start.16
  305.8 2.7 copy-start.17
  305.8 2.7 copy-start.18
  305.8 2.7 copy-start.19
  305.8 2.7 copy-start.20
  305.8 2.7 copy-start.21
  305.8 2.7 copy-start.22
  305.8 2.7 copy-start.23
  322.0 2.0 copy-start.24
  324.0 0.7 copy-start.6
  324.0 0.7 copy-start.32
  331.8 3.1 copy-start.4
  361.8 12.3 %collective-permute-start.1 = (bf16[128,256]{1,0:T(8,128)(2,1)S(1)}, bf16[128,256]{1,0:T(8,128)(2,1)S(1)}, u32[]{:S(2)}, u32[]{:S(2)}) collective-permute-start(bf16[128,256]{1,0:T(8,128)(2,1)S(1)} %slice_bitcast_fusion), channel_id=1, source_target_pairs={{0,16},{16,32},{32,48},{48,64},{64,80},{80,96},{96,112},{112,128},... | collective-permute-start | bytes 196616 | tf_op jit(solution)/shard_map/ppermute | solution.py:18
  365.7 10.7 %copy-start.35 = (s32[16]{0:T(128)S(1)}, s32[16]{0:T(128)}, u32[]{:S(2)}) copy-start(s32[16]{0:T(128)} %copy-done.34) | copy-start | bytes 196
  365.7 82.8 %all-to-all-start.1 = ((f32[32,32,256]{2,1,0:T(8,128)}), f32[32,32,256]{2,1,0:T(8,128)}, u32[]{:S(2)}, u32[]{:S(2)}) async-start(f32[32,32,256]{2,1,0:T(8,128)} %broadcast_in_dim.259), calls=%async_computation.1 | async-start | bytes 2097152 | tf_op jit(solution)/shard_map/all_to_all | solution.py:23
  376.4 72.1 %copy-start.30 = (pred[32]{0:T(512)(128)(4,1)S(1)}, pred[32]{0:T(512)(128)(4,1)}, u32[]{:S(2)}) copy-start(pred[32]{0:T(512)(128)(4,1)} %iota_compare_fusion.1) | copy-start | bytes 100
  448.5 1.7 copy-start.2
  448.5 1.7 copy-start.3
  450.1 0.8 copy-start.7
  450.1 0.8 copy-start.9
  450.1 0.8 copy-start.31
  454.9 2.0 copy-start.25
  454.9 1.9 copy-start.29
  496.9 2.0 copy-start.1
where the time goes:
time: 502 us; the launch traced here: 499 us
  local copies, waits for them, and re-layouts  343 us (68%)
  other arithmetic  66.1 us (13%)
  blocking collectives  36.3 us (7%)
  starting transfers between devices  26.9 us (5%)
  matrix products  14.1 us (3%)
  loops' own time  11.4 us (2%)
    gather x2, local copies, waits for them, and re-layouts, band_matrix(): medium_taps[lag_index] + jnp.where(same_block, long_table[lag_index], 0.0)  120 us
    gather x2, local copies, waits for them, and re-layouts, band_matrix(): long_table[lag_index]  119 us
    all_to_all x1, blocking collectives, per_device(): lax.all_to_all(outgoing, 'ts', split_axis=0, concat_axis=1, tiled=True)  36.3 us
    dynamic_update_slice x16, other arithmetic, per_device(): lax.scan(local_step, (ones_state, zero_state), (factors, contribution))  21.4 us
    reshape x1, local copies, waits for them, and re-layouts, per_device(): stacked = projected.reshape(tok_rows, 3, width)  20.6 us
    dynamic_slice x32, local copies, waits for them, and re-layouts, block_filter(): lax.dynamic_slice_in_dim(extended, block_idx * MEDIUM, 2 * MEDIUM, 0)  16.3 us
    reduce_sum x16, other arithmetic, block_filter(): jnp.einsum('ptug,ugc->tgc', masked, window_x, preferred_element_type=jnp....  13.4 us
    dynamic_update_slice x32, local copies, waits for them, and re-layouts, per_device(): banded = lax.map(block_filter, jnp.arange(blocks_dev, dtype=jnp.int32))  12.4 us
  transfers between devices with their start and end apart: 4, of which 0 were waited for; matrix products, arithmetic and copies ran while one was open for 64% of the time, Pallas kernels for 0%

commit v1 on v0

v1 whole, which is shorter than its diff:
```python
import jax
import jax.numpy as jnp
from jax import lax
from jax.experimental import pallas as pl
from jax.experimental.pallas import tpu as pltpu
from jax.sharding import PartitionSpec as P

GROUP = 16
SHORT = 7
BLOCK = 128
MODES = 16
LANES = 128
DOCS = 16
SPAN = 4
PER_TILE = LANES // GROUP
FLAT = ("ctx", "ts")
HIGHEST = lax.Precision.HIGHEST
f32 = jnp.float32
bf16 = jnp.bfloat16
i32 = jnp.int32


def iota(shape, dim):
    return lax.broadcasted_iota(i32, shape, dim)


def tile_at(i):
    return pl.ds(pl.multiple_of(i * LANES, LANES), LANES)


def in_vmem():
    return pl.BlockSpec(memory_space=pltpu.VMEM)


def in_smem():
    return pl.BlockSpec(memory_space=pltpu.SMEM)


def params():
    return pltpu.CompilerParams(vmem_limit_bytes=48 << 20)


def dot_nt(a, b, precision=None):
    return lax.dot_general(
        a, b, (((1,), (1,)), ((), ())), precision=precision, preferred_element_type=f32
    )


def tables_kernel(
    base_ref, docs_ref, taps_ref, rates_ref, scaled_ref, medium_ref,
    srel_ref, live_ref, tapsx_ref, ratesx_ref, dec_ref, tail_ref, own_ref, med_ref,
    stack_ref,
):
    base = base_ref[0]
    first = base_ref[1]
    row = iota((BLOCK, LANES), 0)
    lane = iota((BLOCK, LANES), 1)
    pos = base + row
    starts = jnp.zeros((BLOCK, LANES), i32)
    ends = first + row * BLOCK + (BLOCK - 1)
    lasts = jnp.zeros((BLOCK, LANES), i32)
    begin = jnp.int32(0)
    for d in range(DOCS):
        starts = jnp.where(pos >= begin, begin, starts)
        lasts = jnp.where(ends >= begin, begin, lasts)
        begin = begin + docs_ref[d]
    srel_ref[...] = starts - base
    live = jnp.where(lasts < ends - (BLOCK - 1), 1.0, 0.0)
    live_ref[...] = live[: live_ref.shape[0]]
    stack_ref[...] = jnp.zeros(stack_ref.shape, f32)
    for p in range(3):
        stack_ref[8 * p : 8 * p + SHORT] = taps_ref[p]
    stack_ref[24:40] = rates_ref[...]
    stack_ref[40:56] = scaled_ref[...]
    whole = stack_ref[...]
    upper = whole.astype(bf16)
    rest = whole - upper.astype(f32)
    middle = rest.astype(bf16)
    lower = (rest - middle.astype(f32)).astype(bf16)
    pieces = jnp.concatenate([upper, middle, lower], axis=0)
    flip = jnp.where(row + lane == BLOCK - 1, 1.0, 0.0)
    med_ref[...] = jnp.dot(
        medium_ref[...].T, flip, precision=HIGHEST, preferred_element_type=f32
    )
    old = starts < base
    groups = medium_ref.shape[1]
    g_row = iota((groups, LANES), 0)
    g_lane = iota((groups, LANES), 1) // GROUP
    own_mode = iota((MODES, LANES), 0) == iota((MODES, LANES), 1) % MODES
    own_group = iota((PER_TILE, LANES), 0) == iota((PER_TILE, LANES), 1) // MODES
    ahead = (row + 1).astype(f32)
    behind = (BLOCK - 1 - row).astype(f32)

    def step(i, carry):
        hot = jnp.where(g_lane + i * PER_TILE == g_row, 1.0, 0.0).astype(bf16)
        spread = jnp.dot(pieces, hot, preferred_element_type=f32)
        spread = spread[0:56] + spread[56:112] + spread[112:168]
        tapsx_ref[:, tile_at(i)] = spread[0:24]
        ratesx_ref[:, tile_at(i)] = spread[24:40]
        rate = jnp.sum(jnp.where(own_mode, spread[24:40], 0.0), axis=0, keepdims=True)
        scale = jnp.sum(jnp.where(own_mode, spread[40:56], 0.0), axis=0, keepdims=True)
        decay = jnp.where(old, scale * jnp.exp(-rate * ahead), 0.0)
        dec_ref[:, tile_at(i)] = decay.astype(bf16)
        power = jnp.exp(-rate * behind)
        tail_ref[tile_at(i), :] = power.T.astype(bf16)
        picked = jnp.where(own_group, scale, 0.0)
        rows = pl.ds(pl.multiple_of(i * PER_TILE, PER_TILE), PER_TILE)
        own_ref[rows, :] = med_ref[rows, :] + dot_nt(picked, power, HIGHEST)
        return carry

    lax.fori_loop(0, tapsx_ref.shape[1] // LANES, step, 0)


def make_tables(place, doc_lengths, short_taps, medium_taps, decay_rates, scaled, width):
    groups = medium_taps.shape[1]
    shape = jax.ShapeDtypeStruct
    return pl.pallas_call(
        tables_kernel,
        out_shape=(
            shape((BLOCK, LANES), i32),
            shape((4 * DOCS, LANES), f32),
            shape((24, width), f32),
            shape((MODES, width), f32),
            shape((BLOCK, width), bf16),
            shape((width, BLOCK), bf16),
            shape((groups, BLOCK), f32),
            shape((groups, BLOCK), f32),
        ),
        in_specs=[in_smem(), in_smem()] + [in_vmem()] * 4,
        out_specs=tuple([in_vmem()] * 8),
        scratch_shapes=[pltpu.VMEM((56, groups), f32)],
        compiler_params=params(),
        name="tables",
    )(place, doc_lengths, short_taps, decay_rates, scaled, medium_taps)


def feature_of(raw_ref, halo_ref, taps_ref, part, i, rel, window_ref):
    window_ref[0:8] = halo_ref[:, tile_at(i)].astype(f32)
    window_ref[8 : 8 + BLOCK] = raw_ref[:, tile_at(i)].astype(f32)
    summed = jnp.zeros((BLOCK, LANES), f32)
    for offset in range(SHORT):
        tap = taps_ref[8 * part + offset : 8 * part + offset + 1, tile_at(i)]
        term = window_ref[8 - offset : 8 - offset + BLOCK] * tap
        if offset:
            term = jnp.where(rel >= offset, term, 0.0)
        summed = summed + term
    return summed


def product_kernel(
    k_ref, v_ref, hk_ref, hv_ref, taps_ref, srel_ref, tail_ref,
    product_ref, contrib_ref,
    wk_ref, wv_ref,
):
    row = iota((BLOCK, LANES), 0)
    rel = row - srel_ref[...]
    kept = jnp.where(row >= srel_ref[BLOCK - 1 : BLOCK], 1.0, 0.0).astype(bf16)
    lane_group = iota((MODES, LANES), 1) // GROUP

    def step(i, carry):
        key = feature_of(k_ref, hk_ref, taps_ref, 1, i, rel, wk_ref)
        value = feature_of(v_ref, hv_ref, taps_ref, 2, i, rel, wv_ref)
        product = (key * value).astype(bf16)
        product_ref[:, tile_at(i)] = product
        all_modes = jnp.dot(
            tail_ref[tile_at(i), :], product * kept, preferred_element_type=f32
        )
        contrib = all_modes[0:MODES]
        for g in range(1, PER_TILE):
            contrib = jnp.where(
                lane_group == g, all_modes[g * MODES : (g + 1) * MODES], contrib
            )
        contrib_ref[0, i] = contrib[0:8].astype(bf16)
        contrib_ref[1, i] = contrib[8:16].astype(bf16)
        return carry

    lax.fori_loop(0, product_ref.shape[1] // LANES, step, 0)


def make_product(projected, halo, tapsx, srel, tail):
    width = projected.shape[1] // 3
    shape = jax.ShapeDtypeStruct
    return pl.pallas_call(
        product_kernel,
        grid=(1,),
        out_shape=(
            shape((BLOCK, width), bf16),
            shape((2, width // LANES, 8, LANES), bf16),
        ),
        in_specs=[
            pl.BlockSpec((BLOCK, width), lambda _: (0, 1)),
            pl.BlockSpec((BLOCK, width), lambda _: (0, 2)),
            pl.BlockSpec((8, width), lambda _: (0, 1)),
            pl.BlockSpec((8, width), lambda _: (0, 2)),
            in_vmem(),
            in_vmem(),
            in_vmem(),
        ],
        out_specs=(in_vmem(), in_vmem()),
        scratch_shapes=[pltpu.VMEM((8 + BLOCK, LANES), f32)] * 2,
        compiler_params=params(),
        name="product",
    )(projected, projected, halo, halo, tapsx, srel, tail)


def band_sum(i, x_ref, taps_ref, mask, acc):
    lane_group = iota((1, LANES), 1) // GROUP
    even = jnp.where(lane_group % 2 == 0, 1.0, 0.0).astype(bf16)
    odd = jnp.where(lane_group % 2 == 1, 1.0, 0.0).astype(bf16)
    x = x_ref[:, tile_at(i)]
    both = jnp.concatenate([x * even, x * odd], axis=0)
    pair_of = iota((BLOCK, LANES), 1) // (2 * GROUP)
    taps = taps_ref[pl.ds(pl.multiple_of(i * PER_TILE, PER_TILE), PER_TILE), :]
    for pair in range(PER_TILE // 2):
        bands = []
        for side in range(2):
            g = 2 * pair + side
            line = jnp.broadcast_to(taps[g : g + 1], (BLOCK, BLOCK))
            ring = pltpu.roll(line, 1, 1, stride=1, stride_axis=0)
            bands.append((ring * mask).astype(bf16))
        out = jnp.dot(
            jnp.concatenate(bands, axis=1), both, preferred_element_type=f32
        )
        acc = jnp.where(pair_of == pair, acc + out, acc)
    return acc


def own_kernel(
    q_ref, hq_ref, taps_ref, srel_ref, x_ref, own_ref, skip_ref,
    query_ref, acc_ref,
    wq_ref, mask_ref,
):
    row = iota((BLOCK, LANES), 0)
    lane = iota((BLOCK, LANES), 1)
    rel = row - srel_ref[...]
    mask_ref[...] = jnp.where((lane <= row) & (lane >= srel_ref[...]), 1.0, 0.0)

    def step(i, carry):
        query_ref[:, tile_at(i)] = feature_of(q_ref, hq_ref, taps_ref, 0, i, rel, wq_ref)
        acc = skip_ref[:, tile_at(i)] * x_ref[:, tile_at(i)].astype(f32)
        acc_ref[:, tile_at(i)] = band_sum(i, x_ref, own_ref, mask_ref[...], acc)
        return carry

    lax.fori_loop(0, acc_ref.shape[1] // LANES, step, 0)


def make_own(projected, halo, tapsx, srel, product, own, skip):
    width = product.shape[1]
    shape = jax.ShapeDtypeStruct
    return pl.pallas_call(
        own_kernel,
        grid=(1,),
        out_shape=(shape((BLOCK, width), f32), shape((BLOCK, width), f32)),
        in_specs=[
            pl.BlockSpec((BLOCK, width), lambda _: (0, 0)),
            pl.BlockSpec((8, width), lambda _: (0, 0)),
        ]
        + [in_vmem()] * 5,
        out_specs=(in_vmem(), in_vmem()),
        scratch_shapes=[
            pltpu.VMEM((8 + BLOCK, LANES), f32),
            pltpu.VMEM((BLOCK, LANES), f32),
        ],
        compiler_params=params(),
        name="own",
    )(projected, halo, tapsx, srel, product, own, skip)


def earlier_kernel(x_ref, taps_ref, srel_ref, acc_ref, out_ref, mask_ref):
    row = iota((BLOCK, LANES), 0)
    lane = iota((BLOCK, LANES), 1)
    inside = (lane > row) & (lane - BLOCK >= srel_ref[...])
    mask_ref[...] = jnp.where(inside, 1.0, 0.0)

    def step(i, carry):
        acc = acc_ref[:, tile_at(i)]
        out_ref[:, tile_at(i)] = band_sum(i, x_ref, taps_ref, mask_ref[...], acc)
        return carry

    lax.fori_loop(0, out_ref.shape[1] // LANES, step, 0)


def make_earlier(before, med, srel, acc):
    return pl.pallas_call(
        earlier_kernel,
        out_shape=jax.ShapeDtypeStruct(acc.shape, f32),
        in_specs=[in_vmem()] * 4,
        out_specs=in_vmem(),
        scratch_shapes=[pltpu.VMEM((BLOCK, LANES), f32)],
        compiler_params=params(),
        name="earlier",
    )(before, med, srel, acc)


def totals_kernel(which_ref, terms_ref, rates_ref, live_ref, out_ref):
    decay = jnp.exp(-rates_ref[...] * float(BLOCK))
    state = jnp.zeros((8, LANES), f32)
    kept = jnp.ones((8, LANES), f32)
    for b in range(terms_ref.shape[0]):
        factor = live_ref[b : b + 1] * decay
        state = factor * state + terms_ref[b].astype(f32)
        kept = factor * kept
    out_ref[0] = state
    out_ref[1] = kept


def item_spec(tiles):
    return pl.BlockSpec((8, LANES), lambda _, which: (which[0] // tiles, which[0] % tiles))


def make_totals(which, terms, ratesx, live):
    tiles = ratesx.shape[1] // LANES
    return pl.pallas_call(
        totals_kernel,
        out_shape=jax.ShapeDtypeStruct((2, 8, LANES), f32),
        grid_spec=pltpu.PrefetchScalarGridSpec(
            num_scalar_prefetch=1,
            grid=(1,),
            in_specs=[in_vmem(), item_spec(tiles), in_vmem()],
            out_specs=in_vmem(),
        ),
        compiler_params=params(),
        name="totals",
    )(which, terms, ratesx, live)


def states_kernel(which_ref, terms_ref, rates_ref, live_ref, one_ref, two_ref, out_ref):
    decay = jnp.exp(-rates_ref[...] * float(BLOCK))
    state = one_ref[0] + one_ref[1] * two_ref[...]
    for b in range(terms_ref.shape[0]):
        out_ref[b] = state.astype(bf16)
        state = live_ref[b : b + 1] * decay * state + terms_ref[b].astype(f32)


def make_states(which, terms, ratesx, live, one, two):
    tiles = ratesx.shape[1] // LANES
    return pl.pallas_call(
        states_kernel,
        out_shape=jax.ShapeDtypeStruct(terms.shape, bf16),
        grid_spec=pltpu.PrefetchScalarGridSpec(
            num_scalar_prefetch=1,
            grid=(1,),
            in_specs=[in_vmem(), item_spec(tiles)] + [in_vmem()] * 3,
            out_specs=in_vmem(),
        ),
        compiler_params=params(),
        name="states",
    )(which, terms, ratesx, live, one, two)


def final_kernel(acc_ref, query_ref, dec_ref, state_ref, out_ref):
    same = iota((LANES, LANES), 0) // MODES == iota((LANES, LANES), 1) // GROUP
    keep = jnp.where(same, 1.0, 0.0).astype(bf16)

    def step(i, carry):
        one = jnp.concatenate([state_ref[0, i], state_ref[1, i]], axis=0)
        spread = jnp.concatenate([one] * PER_TILE, axis=0) * keep
        carried = jnp.dot(dec_ref[:, tile_at(i)], spread, preferred_element_type=f32)
        filtered = (acc_ref[:, tile_at(i)] + carried).astype(bf16).astype(f32)
        out_ref[:, tile_at(i)] = (query_ref[:, tile_at(i)] * filtered).astype(bf16)
        return carry

    lax.fori_loop(0, out_ref.shape[1] // LANES, step, 0)


def make_final(acc, query, dec, state):
    return pl.pallas_call(
        final_kernel,
        out_shape=jax.ShapeDtypeStruct(acc.shape, bf16),
        in_specs=[in_vmem()] * 4,
        out_specs=in_vmem(),
        compiler_params=params(),
        name="final",
    )(acc, query, dec, state)


def per_device(projected, doc_lengths, short_taps, medium_taps, decay_rates, residues, skip_gain):
    ts_count = lax.axis_size("ts")
    ctx_count = lax.axis_size("ctx")
    count = ts_count * ctx_count
    ctx = lax.axis_index("ctx")
    index = ctx * ts_count + lax.axis_index("ts")
    size = SPAN * ts_count
    which = (index % size).astype(i32)
    groups = [[s * size + j for j in range(size)] for s in range(count // size)]
    onward = [(i, i + 1) for i in range(count - 1)]
    width = projected.shape[1] // 3

    def from_ctx(value, by):
        return lax.ppermute(value, "ctx", [(i, i + by) for i in range(ctx_count - by)])

    halo = lax.ppermute(projected[BLOCK - 8 :], FLAT, onward)
    place = jnp.stack([index * BLOCK, (index - which) * BLOCK]).astype(i32)
    scaled = residues * jnp.sqrt(-jnp.expm1(-2.0 * decay_rates))
    srel, live, tapsx, ratesx, dec, tail, own, med = make_tables(
        place, doc_lengths, short_taps, medium_taps, decay_rates, scaled, width
    )
    product, contrib = make_product(projected, halo, tapsx, srel, tail)
    items = contrib.reshape(size, 8, LANES)
    terms = lax.all_to_all(
        items, FLAT, split_axis=0, concat_axis=0, tiled=True, axis_index_groups=groups
    )
    before = lax.ppermute(product, FLAT, onward)
    query, acc = make_own(projected, halo, tapsx, srel, product, own, skip_gain.reshape(1, -1))
    ours = which.reshape(1)
    totals = make_totals(ours, terms, ratesx, live)
    one = from_ctx(totals, SPAN)
    two = from_ctx(totals[0], 2 * SPAN)
    states = make_states(ours, terms, ratesx, live, one, two)
    back = lax.all_to_all(
        states, FLAT, split_axis=0, concat_axis=0, tiled=True, axis_index_groups=groups
    )
    acc = make_earlier(before, med, srel, acc)
    return make_final(acc, query, dec, back.reshape(2, width // LANES, 8, LANES))


def solution(mesh):
    return jax.shard_map(
        per_device,
        mesh=mesh,
        in_specs=(P(FLAT, None), P(), P(), P(), P(), P(), P()),
        out_specs=P(FLAT, None),
        check_vma=False,
    )
```

time: 502 us -> 113 us (0.23)
  local copies, waits for them, and re-layouts: 343 us -> 8.76 us
  other arithmetic: 66.1 us -> 0.83 us
  Pallas kernels: 0 us -> 52.8 us
  matrix products: 14.1 us -> 0 us
  blocking collectives: 36.3 us -> 23.9 us
  loops' own time: 11.4 us -> 0 us
    gather x4 -> x0, local copies, waits for them, and re-layouts: 238 us -> none  [the longest x2 120 us: band_matrix(): medium_taps[lag_index] + jnp.where(same_block, long_table[lag_index], 0.0)]
    pallas_call x0 -> x7, Pallas kernels: none -> 52.8 us  [the longest x1 14.3 us: make_tables(): pl.pallas_call(tables_kernel, out_shape=(shape((BLOCK, LANES), i32), shap...]
    reshape x8 -> x0, local copies, waits for them, and re-layouts: 30.2 us -> none  [the longest x1 20.6 us: per_device(): stacked = projected.reshape(tok_rows, 3, width)]
    dynamic_slice x51 -> x0, local copies, waits for them, and re-layouts: 27.1 us -> none  [the longest x32 16.3 us: block_filter(): lax.dynamic_slice_in_dim(extended, block_idx * MEDIUM, 2 * MEDIUM, 0)]
    dynamic_update_slice x16 -> x0, other arithmetic: 21.4 us -> none  [per_device(): lax.scan(local_step, (ones_state, zero_state), (factors, contribution))]
    dot_general x18 -> x0, matrix products: 14.1 us -> none  [the longest x16 6.41 us: block_filter(): jnp.einsum('ptug,ugc->tgc', masked, window_x, preferred_element_type=jnp....]
    reduce_sum x17 -> x0, other arithmetic: 13.5 us -> none  [the longest x16 13.4 us: block_filter(): jnp.einsum('ptug,ugc->tgc', masked, window_x, preferred_element_type=jnp....]
    all_to_all x1, blocking collectives: 36.3 us -> 23.9 us  [per_device(): lax.all_to_all(items, FLAT, split_axis=0, concat_axis=0, tiled=True, axis...]
  transfers between devices with their start and end apart: 4 -> 5, of which waited for: 0 -> 1; matrix products, arithmetic and copies ran while one was open for 64% -> 1% of each run, Pallas kernels for 0% -> 35%
where the time goes in v1:
time: 113 us; the launch traced here: 112 us
  Pallas kernels  52.8 us (47%)
  starting transfers between devices  25 us (22%)
  blocking collectives  23.9 us (21%)
  local copies, waits for them, and re-layouts  8.76 us (8%)
    all_to_all x1, blocking collectives, per_device(): lax.all_to_all(items, FLAT, split_axis=0, concat_axis=0, tiled=True, axis...  23.9 us
    pallas_call x1, Pallas kernels, make_tables(): pl.pallas_call(tables_kernel, out_shape=(shape((BLOCK, LANES), i32), shap...  14.3 us
    pallas_call x1, Pallas kernels, make_own(): pl.pallas_call(own_kernel, grid=(1,), out_shape=(shape((BLOCK, width), f3...  11.8 us
    pallas_call x1, Pallas kernels, make_earlier(): pl.pallas_call(earlier_kernel, out_shape=jax.ShapeDtypeStruct(acc.shape,...  11.7 us
    ppermute x2, starting transfers between devices, from_ctx(): lax.ppermute(value, 'ctx', [(i, i + by) for i in range(ctx_count - by)])  9.63 us
    pallas_call x1, Pallas kernels, make_product(): pl.pallas_call(product_kernel, grid=(1,), out_shape=(shape((BLOCK, width)...  8.38 us
    all_to_all x1, starting transfers between devices, per_device(): lax.all_to_all(states, FLAT, split_axis=0, concat_axis=0, tiled=True, axi...  8.08 us
    unnamed x16, local copies, waits for them, and re-layouts  7.82 us
  transfers between devices with their start and end apart: 5, of which 1 were waited for; matrix products, arithmetic and copies ran while one was open for 1% of the time, Pallas kernels for 35%

profile of v1, /device:TPU:1, one launch (start us, length us, event | category | flops | bytes accessed | tf_op | source)
XLA Modules:
  0.0 112.2 jit_solution(4223321351856889430)
XLA Ops:
  0.0 0.9 slice.6
  0.9 5.4 %collective-permute-start = (bf16[8,12288]{1,0:T(8,128)(2,1)S(1)}, bf16[8,12288]{1,0:T(8,128)(2,1)S(1)}, u32[]{:S(2)}, u32[]{:S(2)}) collective-permute-start(bf16[8,12288]{1,0:T(8,128)(2,1)S(1)} %slice.6), channel_id=1, source_target_pairs={{0,1},{1,2},{2,3},{3,4},{4,5},{5,6},{6,7},{7,8},{8,9},{9,10},{10,1... | collective-permute-start | bytes 589832 | tf_op jit(solution)/shard_map/ppermute | solution.py:392
  6.3 0.1 pad_add_fusion.base_ref
  6.4 0.8 sqrt_multiply_fusion.scaled_ref
  7.2 0.0 copy-start.3
  7.2 0.9 copy-done.3
  8.1 0.0 copy-start.4
  8.1 0.7 copy-done.4
  8.8 0.0 copy-start.5
  8.8 0.7 copy-done.5
  9.5 0.0 copy-start.7
  9.5 0.7 copy-done.7
  10.2 14.3 %tables.1 = (s32[128,128]{1,0:T(8,128)S(1)}, f32[64,128]{1,0:T(8,128)S(1)}, f32[24,4096]{1,0:T(8,128)S(1)}, f32[16,4096]{1,0:T(8,128)S(1)}, bf16[128,4096]{1,0:T...) custom-call(s32[2]{0:T(128)S(1)} %pad_add_fusion.base_ref, ...), custom_call_target="tpu_custom_call" | custom-call | tf_op jit(solution)/shard_map/tables/pallas_call | solution.py:117
  24.5 0.0 collective-permute-done.hk_ref.hv_ref.hq_ref
  24.5 0.0 copy-start
  24.5 1.9 %copy-done = bf16[128,12288]{1,0:T(8,128)(2,1)S(1)} copy-done((bf16[128,12288]{1,0:T(8,128)(2,1)S(1)}, bf16[128,12288]{1,0:T(8,128)(2,1)}, u32[]{:S(2)}) %copy-start) | copy-done | bytes 3145752
  26.4 0.0 copy-start.6
  26.4 8.4 %product.1 = (bf16[128,4096]{1,0:T(8,128)(2,1)S(1)}, bf16[2,32,8,128]{3,2,1,0:T(8,128)(2,1)S(1)}) custom-call(bf16[128,12288]{1,0:T(8,128)(2,1)S(1)} %copy-done, bf16[128,12288]{1,0:T(8,128)(2,1)S(1)} %copy-done, bf16[8,12288]{1,0:T(8,128)(2,1)S(1)} %collective-permute-done.hk_ref.hv_ref.hq_ref, ...), custom_call_target="tpu_custom_call" | custom-call | tf_op jit(solution)/shard_map/product/pallas_call | solution.py:183
  34.8 1.9 %collective-permute-start.1 = (bf16[128,4096]{1,0:T(8,128)(2,1)S(1)}, bf16[128,4096]{1,0:T(8,128)(2,1)}, u32[]{:S(2)}, u32[]{:S(2)}) collective-permute-start(bf16[128,4096]{1,0:T(8,128)(2,1)S(1)} %get-tuple-element.20.x_ref), channel_id=1, source_target_pairs={{0,1},{1,2},{2,3},{3,4},{4,5},{5,6},{6,7},{7,8},{8,9},{9,10},{10,1... | collective-permute-start | bytes 3145736 | tf_op jit(solution)/shard_map/ppermute | solution.py:403
  36.7 23.9 %all_to_all.10.terms_ref = bf16[64,8,128]{2,1,0:T(8,128)(2,1)S(1)} all-to-all(bf16[64,8,128]{2,1,0:T(8,128)(2,1)S(1)} %bitcast.9), channel_id=1, replica_groups={{0,1,2,3,4,5,6,7,8,9,10,11,12,13,14,15,16,17,18,19,20,21,22,23,24,25,26..., dimensions={0} | all-to-all | bytes 262144 | tf_op jit(solution)/shard_map/all_to_all | solution.py:400
  60.6 0.1 totals.1
  60.8 6.5 %collective-permute-start.2 = (f32[2,8,128]{2,1,0:T(8,128)S(1)}, f32[2,8,128]{2,1,0:T(8,128)S(1)}, u32[]{:S(2)}, u32[]{:S(2)}) collective-permute-start(f32[2,8,128]{2,1,0:T(8,128)S(1)} %totals.1), channel_id=1, source_target_pairs={{0,64},{16,80},{32,96},{48,112},{64,128},{80,144},{96,160},{112,17... | collective-permute-start | bytes 24584 | tf_op jit(solution)/shard_map/ppermute | solution.py:390
  67.3 3.1 %collective-permute-start.3 = (f32[8,128]{1,0:T(8,128)S(1)}, f32[8,128]{1,0:T(8,128)S(1)}, u32[]{:S(2)}, u32[]{:S(2)}) collective-permute-start(f32[8,128]{1,0:T(8,128)S(1)} %slice_bitcast_fusion), channel_id=1, source_target_pairs={{0,128},{16,144},{32,160},{48,176},{64,192},{80,208},{96,224},{112... | collective-permute-start | bytes 12296 | tf_op jit(solution)/shard_map/ppermute | solution.py:390
  70.4 0.7 collective-permute-done.3.two_ref
  71.2 0.0 collective-permute-done.2.one_ref
  71.2 0.8 states.1
  72.0 8.1 %all-to-all-start.1 = ((bf16[64,8,128]{2,1,0:T(8,128)(2,1)}), bf16[64,8,128]{2,1,0:T(8,128)(2,1)S(1)}, u32[]{:S(2)}, u32[]{:S(2)}) async-start(bf16[64,8,128]{2,1,0:T(8,128)(2,1)} %states.1), calls=%async_computation.1 | async-start | bytes 262144 | tf_op jit(solution)/shard_map/all_to_all | solution.py:410
  80.1 0.0 copy-done.6
  80.1 11.8 %own.1 = (f32[128,4096]{1,0:T(8,128)S(1)}, f32[128,4096]{1,0:T(8,128)S(1)}) custom-call(bf16[128,12288]{1,0:T(8,128)(2,1)} %q_ref.1, bf16[8,12288]{1,0:T(8,128)(2,1)S(1)} %collective-permute-done.hk_ref.hv_ref.hq_ref, f32[24,4096]{1,0:T(8,128)S(1)} %get-tuple-element.17.taps_ref, s32[128,128]{1,0:T(8,128)S(1)} %get-tuple-element.18.srel_ref, ...), custom_call_target="tpu_custom_call" | custom-call | tf_op jit(solution)/shard_map/own/pallas_call | solution.py:250
  91.9 0.0 copy-start.1
  91.9 1.3 %copy-done.1 = f32[128,4096]{1,0:T(8,128)} copy-done((f32[128,4096]{1,0:T(8,128)}, f32[128,4096]{1,0:T(8,128)S(1)}, u32[]{:S(2)}) %copy-start.1) | copy-done | bytes 2097176
  93.2 0.0 collective-permute-done.1.x_ref
  93.2 11.7 %earlier.1.acc_ref = f32[128,4096]{1,0:T(8,128)S(1)} custom-call(bf16[128,4096]{1,0:T(8,128)(2,1)} %collective-permute-done.1.x_ref, f32[256,128]{1,0:T(8,128)S(1)} %get-tuple-element.21.taps_ref, s32[128,128]{1,0:T(8,128)S(1)} %get-tuple-element.18.srel_ref, f32[128,4096]{1,0:T(8,128)S(1)} %get-tuple-element.23.acc_ref), custom_call_target="tpu_custom_call" | custom-call | tf_op jit(solution)/shard_map/earlier/pallas_call | solution.py:284
  104.9 0.0 all-to-all-done.1
  104.9 0.0 copy-start.2
  104.9 1.6 %copy-done.2 = f32[128,4096]{1,0:T(8,128)S(1)} copy-done((f32[128,4096]{1,0:T(8,128)S(1)}, f32[128,4096]{1,0:T(8,128)}, u32[]{:S(2)}) %copy-start.2) | copy-done | bytes 2097176
  106.5 5.7 %final.1 = bf16[128,4096]{1,0:T(8,128)(2,1)} custom-call(f32[128,4096]{1,0:T(8,128)S(1)} %earlier.1.acc_ref, f32[128,4096]{1,0:T(8,128)S(1)} %copy-done.2, bf16[128,4096]{1,0:T(8,128)(2,1)S(1)} %get-tuple-element.25.dec_ref, bf16[2,32,8,128]{3,2,1,0:T(8,128)(2,1)S(1)} %bitcast.8), custom_call_target="tpu_custom_call" | custom-call | tf_op jit(solution)/shard_map/final/pallas_call | solution.py:367
  (1 shorter events, 0.0 us)
Async XLA Ops:
  0.9 23.6 %collective-permute-start = (bf16[8,12288]{1,0:T(8,128)(2,1)S(1)}, bf16[8,12288]{1,0:T(8,128)(2,1)S(1)}, u32[]{:S(2)}, u32[]{:S(2)}) collective-permute-start(bf16[8,12288]{1,0:T(8,128)(2,1)S(1)} %slice.6), channel_id=1, source_target_pairs={{0,1},{1,2},{2,3},{3,4},{4,5},{5,6},{6,7},{7,8},{8,9},{9,10},{10,1... | collective-permute-start | bytes 589832 | tf_op jit(solution)/shard_map/ppermute | solution.py:392
  7.2 0.9 copy-start.3
  8.1 0.7 copy-start.4
  8.8 0.7 copy-start.5
  9.5 0.7 copy-start.7
  24.5 1.9 %copy-start = (bf16[128,12288]{1,0:T(8,128)(2,1)S(1)}, bf16[128,12288]{1,0:T(8,128)(2,1)}, u32[]{:S(2)}) copy-start(bf16[128,12288]{1,0:T(8,128)(2,1)} %q_ref.1) | copy-start | bytes 9437188
  26.4 53.6 %copy-start.6 = (f32[4096]{0:T(1024)S(1)}, f32[4096]{0:T(1024)}, u32[]{:S(2)}) copy-start(f32[4096]{0:T(1024)} %param.13) | copy-start | bytes 49156
  34.8 58.4 %collective-permute-start.1 = (bf16[128,4096]{1,0:T(8,128)(2,1)S(1)}, bf16[128,4096]{1,0:T(8,128)(2,1)}, u32[]{:S(2)}, u32[]{:S(2)}) collective-permute-start(bf16[128,4096]{1,0:T(8,128)(2,1)S(1)} %get-tuple-element.20.x_ref), channel_id=1, source_target_pairs={{0,1},{1,2},{2,3},{3,4},{4,5},{5,6},{6,7},{7,8},{8,9},{9,10},{10,1... | collective-permute-start | bytes 3145736 | tf_op jit(solution)/shard_map/ppermute | solution.py:403
  60.8 10.4 %collective-permute-start.2 = (f32[2,8,128]{2,1,0:T(8,128)S(1)}, f32[2,8,128]{2,1,0:T(8,128)S(1)}, u32[]{:S(2)}, u32[]{:S(2)}) collective-permute-start(f32[2,8,128]{2,1,0:T(8,128)S(1)} %totals.1), channel_id=1, source_target_pairs={{0,64},{16,80},{32,96},{48,112},{64,128},{80,144},{96,160},{112,17... | collective-permute-start | bytes 24584 | tf_op jit(solution)/shard_map/ppermute | solution.py:390
  67.3 3.9 %collective-permute-start.3 = (f32[8,128]{1,0:T(8,128)S(1)}, f32[8,128]{1,0:T(8,128)S(1)}, u32[]{:S(2)}, u32[]{:S(2)}) collective-permute-start(f32[8,128]{1,0:T(8,128)S(1)} %slice_bitcast_fusion), channel_id=1, source_target_pairs={{0,128},{16,144},{32,160},{48,176},{64,192},{80,208},{96,224},{112... | collective-permute-start | bytes 12296 | tf_op jit(solution)/shard_map/ppermute | solution.py:390
  72.0 32.9 %all-to-all-start.1 = ((bf16[64,8,128]{2,1,0:T(8,128)(2,1)}), bf16[64,8,128]{2,1,0:T(8,128)(2,1)S(1)}, u32[]{:S(2)}, u32[]{:S(2)}) async-start(bf16[64,8,128]{2,1,0:T(8,128)(2,1)} %states.1), calls=%async_computation.1 | async-start | bytes 262144 | tf_op jit(solution)/shard_map/all_to_all | solution.py:410
  91.9 1.3 %copy-start.1 = (f32[128,4096]{1,0:T(8,128)}, f32[128,4096]{1,0:T(8,128)S(1)}, u32[]{:S(2)}) copy-start(f32[128,4096]{1,0:T(8,128)S(1)} %get-tuple-element.24.query_ref) | copy-start | bytes 6291460
  104.9 1.6 %copy-start.2 = (f32[128,4096]{1,0:T(8,128)S(1)}, f32[128,4096]{1,0:T(8,128)}, u32[]{:S(2)}) copy-start(f32[128,4096]{1,0:T(8,128)} %copy-done.1) | copy-start | bytes 6291460

commit v2 on v1

v2 whole, which is shorter than its diff:
```python
import jax
import jax.numpy as jnp
from jax import lax
from jax.experimental import pallas as pl
from jax.experimental.pallas import tpu as pltpu
from jax.sharding import PartitionSpec as P

GROUP = 16
SHORT = 7
BLOCK = 128
MODES = 16
LANES = 128
DOCS = 16
SPAN = 4
PER_TILE = LANES // GROUP
FLAT = ("ctx", "ts")
HIGHEST = lax.Precision.HIGHEST
f32 = jnp.float32
bf16 = jnp.bfloat16
i32 = jnp.int32


def iota(shape, dim):
    return lax.broadcasted_iota(i32, shape, dim)


TILES = 4
WIDE = TILES * LANES


def tile(j):
    return slice(j * LANES, (j + 1) * LANES)


def in_vmem():
    return pl.BlockSpec(memory_space=pltpu.VMEM)


def in_smem():
    return pl.BlockSpec(memory_space=pltpu.SMEM)


def columns(rows, first=0):
    return pl.BlockSpec((rows, WIDE), lambda j: (0, first + j))


def rows_of(count):
    return pl.BlockSpec((count, LANES), lambda j: (j, 0))


def fixed(shape):
    return pl.BlockSpec(shape, lambda j: (0,) * len(shape))


def hbm(*values):
    return [pltpu.with_memory_space_constraint(value, pltpu.HBM) for value in values]


def params(mib=12):
    return pltpu.CompilerParams(vmem_limit_bytes=mib << 20)


def spread_kernel(
    place_ref, stack_ref,
    srel_ref, live_ref, tapsx_ref, ratesx_ref, scalex_ref, tail_ref,
    pieces_ref,
):
    step = pl.program_id(0)
    row = iota((BLOCK, LANES), 0)

    @pl.when(step == 0)
    def _():
        base = place_ref[0]
        pos = base + row
        starts = jnp.zeros((BLOCK, LANES), i32)
        ends = place_ref[1] + row[: live_ref.shape[0]] * BLOCK + (BLOCK - 1)
        lasts = jnp.zeros(live_ref.shape, i32)
        begin = jnp.int32(0)
        for d in range(DOCS):
            starts = jnp.where(pos >= begin, begin, starts)
            lasts = jnp.where(ends >= begin, begin, lasts)
            begin = begin + place_ref[2 + d]
        srel_ref[...] = starts - base
        live_ref[...] = jnp.where(lasts < ends - (BLOCK - 1), 1.0, 0.0)
        whole = stack_ref[...]
        upper = whole.astype(bf16)
        rest = whole - upper.astype(f32)
        middle = rest.astype(bf16)
        pieces_ref[0] = upper
        pieces_ref[1] = middle
        pieces_ref[2] = (rest - middle.astype(f32)).astype(bf16)

    groups = stack_ref.shape[1]
    pieces = jnp.concatenate([pieces_ref[0], pieces_ref[1], pieces_ref[2]], axis=0)
    ahead = iota((groups, LANES), 0) - iota((groups, LANES), 1) // GROUP
    own_mode = iota((MODES, LANES), 0) == iota((MODES, LANES), 1) % MODES
    behind = (BLOCK - 1 - row).astype(f32)
    for j in range(TILES):
        first = (step * TILES + j) * PER_TILE
        hot = jnp.where(ahead == first, 1.0, 0.0).astype(bf16)
        spread = jnp.dot(pieces, hot, preferred_element_type=f32)
        spread = spread[0:64] + spread[64:128] + spread[128:192]
        tapsx_ref[:, tile(j)] = spread[0:24]
        ratesx_ref[:, tile(j)] = spread[24:40]
        scalex_ref[:, tile(j)] = spread[40:56]
        rate = jnp.sum(jnp.where(own_mode, spread[24:40], 0.0), axis=0, keepdims=True)
        tail_ref[tile(j), :] = jnp.exp(-rate * behind).T.astype(bf16)


def make_spread(place, stack, width):
    shape = pltpu.HBM
    return pl.pallas_call(
        spread_kernel,
        grid=(width // WIDE,),
        out_shape=(
            shape((BLOCK, LANES), i32),
            shape((4 * DOCS, LANES), f32),
            shape((24, width), f32),
            shape((MODES, width), f32),
            shape((MODES, width), f32),
            shape((width, BLOCK), bf16),
        ),
        in_specs=[in_smem(), fixed(stack.shape)],
        out_specs=(
            fixed((BLOCK, LANES)),
            fixed((4 * DOCS, LANES)),
            columns(24),
            columns(MODES),
            columns(MODES),
            rows_of(WIDE),
        ),
        scratch_shapes=[pltpu.VMEM((3, *stack.shape), bf16)],
        compiler_params=params(),
        name="spread",
    )(place, stack)


def tables_kernel(
    srel_ref, ratesx_ref, scalex_ref, medium_ref,
    dec_ref, own_ref, med_ref,
    long_ref,
):
    step = pl.program_id(0)
    row = iota((BLOCK, LANES), 0)
    lane = iota((BLOCK, LANES), 1)
    old = srel_ref[...] < 0
    own_mode = iota((MODES, LANES), 0) == iota((MODES, LANES), 1) % MODES
    ahead = (row + 1).astype(f32)
    behind = (BLOCK - 1 - row).astype(f32)
    steps_each = LANES // (TILES * PER_TILE)

    @pl.when(step % steps_each == 0)
    def _():
        long_ref[step // steps_each] = jnp.zeros((BLOCK, LANES), f32)

    total = long_ref[step // steps_each]
    for j in range(TILES):
        rate = jnp.sum(jnp.where(own_mode, ratesx_ref[:, tile(j)], 0.0), axis=0, keepdims=True)
        scale = jnp.sum(jnp.where(own_mode, scalex_ref[:, tile(j)], 0.0), axis=0, keepdims=True)
        decay = jnp.where(old, scale * jnp.exp(-rate * ahead), 0.0)
        dec_ref[:, tile(j)] = decay.astype(bf16)
        power = scale * jnp.exp(-rate * behind)
        upper = power.astype(bf16)
        lower = (power - upper.astype(f32)).astype(bf16)
        first = (step % steps_each * TILES + j) * PER_TILE
        hot = jnp.where(lane - row // MODES == first, 1.0, 0.0).astype(bf16)
        total = total + jnp.dot(
            jnp.concatenate([upper, lower], axis=1),
            jnp.concatenate([hot, hot], axis=0),
            preferred_element_type=f32,
        )
    long_ref[step // steps_each] = total

    @pl.when(step == pl.num_programs(0) - 1)
    def _():
        flip = jnp.where(row + lane == BLOCK - 1, 1.0, 0.0)
        for h in range(long_ref.shape[0]):
            medium = jnp.dot(
                flip, medium_ref[:, tile(h)], precision=HIGHEST, preferred_element_type=f32
            )
            med_ref[tile(h), :] = medium.T
            own_ref[tile(h), :] = (medium + long_ref[h]).T


def make_tables(srel, ratesx, scalex, medium_taps):
    width = ratesx.shape[1]
    groups = medium_taps.shape[1]
    shape = pltpu.HBM
    return pl.pallas_call(
        tables_kernel,
        grid=(width // WIDE,),
        out_shape=(
            shape((BLOCK, width), bf16),
            shape((groups, BLOCK), f32),
            shape((groups, BLOCK), f32),
        ),
        in_specs=[
            fixed((BLOCK, LANES)),
            columns(MODES),
            columns(MODES),
            fixed(medium_taps.shape),
        ],
        out_specs=(columns(BLOCK), fixed((groups, BLOCK)), fixed((groups, BLOCK))),
        scratch_shapes=[pltpu.VMEM((groups // LANES, BLOCK, LANES), f32)],
        compiler_params=params(),
        name="tables",
    )(*hbm(srel, ratesx, scalex, medium_taps))


def feature_of(raw_ref, halo_ref, taps_ref, part, j, rel, window_ref):
    window_ref[0:8] = halo_ref[:, tile(j)].astype(f32)
    window_ref[8 : 8 + BLOCK] = raw_ref[:, tile(j)].astype(f32)
    summed = window_ref[8 : 8 + BLOCK] * taps_ref[8 * part : 8 * part + 1, tile(j)]
    for offset in range(1, SHORT):
        tap = taps_ref[8 * part + offset : 8 * part + offset + 1, tile(j)]
        term = window_ref[8 - offset : 8 - offset + BLOCK] * tap
        summed = summed + jnp.where(rel >= offset, term, 0.0)
    return summed


def product_kernel(
    k_ref, v_ref, hq_ref, hk_ref, hv_ref, taps_ref, srel_ref, tail_ref,
    product_ref, contrib_ref, edge_ref,
    wk_ref, wv_ref,
):
    row = iota((BLOCK, LANES), 0)
    rel = row - srel_ref[...]
    kept = jnp.where(row >= srel_ref[BLOCK - 1 : BLOCK], 1.0, 0.0).astype(bf16)
    lane_group = iota((MODES, LANES), 1) // GROUP
    edge_ref[...] = hq_ref[...]
    for j in range(TILES):
        key = feature_of(k_ref, hk_ref, taps_ref, 1, j, rel, wk_ref.at[j])
        value = feature_of(v_ref, hv_ref, taps_ref, 2, j, rel, wv_ref.at[j])
        product = (key * value).astype(bf16)
        product_ref[:, tile(j)] = product
        all_modes = jnp.dot(
            tail_ref[tile(j), :], product * kept, preferred_element_type=f32
        )
        contrib = all_modes[0:MODES]
        for g in range(1, PER_TILE):
            contrib = jnp.where(
                lane_group == g, all_modes[g * MODES : (g + 1) * MODES], contrib
            )
        contrib_ref[0, j] = contrib[0:8].astype(bf16)
        contrib_ref[1, j] = contrib[8:16].astype(bf16)


def make_product(projected, halo, tapsx, srel, tail):
    width = projected.shape[1] // 3
    steps = width // WIDE
    shape = pltpu.HBM
    return pl.pallas_call(
        product_kernel,
        grid=(steps,),
        out_shape=(
            shape((BLOCK, width), bf16),
            shape((2, width // LANES, 8, LANES), bf16),
            shape((8, width), bf16),
        ),
        in_specs=[
            columns(BLOCK, steps),
            columns(BLOCK, 2 * steps),
            columns(8),
            columns(8, steps),
            columns(8, 2 * steps),
            columns(24),
            fixed((BLOCK, LANES)),
            rows_of(WIDE),
        ],
        out_specs=(
            columns(BLOCK),
            pl.BlockSpec((2, TILES, 8, LANES), lambda j: (0, j, 0, 0)),
            columns(8),
        ),
        scratch_shapes=[pltpu.VMEM((TILES, 8 + BLOCK, LANES), f32)] * 2,
        compiler_params=params(),
        name="product",
    )(*hbm(projected, projected), halo, halo, halo, *hbm(tapsx, srel, tail))


def band_sum(j, x_ref, taps_ref, mask_ref, acc):
    lane_group = iota((1, LANES), 1) // GROUP
    even = jnp.where(lane_group % 2 == 0, 1.0, 0.0).astype(bf16)
    odd = jnp.where(lane_group % 2 == 1, 1.0, 0.0).astype(bf16)
    x = x_ref[:, tile(j)]
    both = jnp.concatenate([x * even, x * odd], axis=0)
    pair_of = iota((BLOCK, LANES), 1) // (2 * GROUP)
    pairs = []
    for pair in range(PER_TILE // 2):
        bands = []
        for side in range(2):
            g = j * PER_TILE + 2 * pair + side
            line = jnp.broadcast_to(taps_ref[g : g + 1], (8, BLOCK))
            ring = pltpu.roll(line, 1, 1, stride=1, stride_axis=0)
            parts = [ring] + [pltpu.roll(ring, 8 * k, 1) for k in range(1, BLOCK // 8)]
            bands.append((jnp.concatenate(parts, axis=0) * mask_ref[...]).astype(bf16))
        pairs.append(jnp.concatenate(bands, axis=1))
    out = jnp.dot(jnp.concatenate(pairs, axis=0), both, preferred_element_type=f32)
    picked = out[0:BLOCK]
    for pair in range(1, PER_TILE // 2):
        picked = jnp.where(pair_of == pair, out[pair * BLOCK : (pair + 1) * BLOCK], picked)
    return acc + picked


def own_kernel(
    q_ref, hq_ref, taps_ref, srel_ref, x_ref, own_ref, skip_ref,
    query_ref, acc_ref, zero_ref,
    wq_ref, mask_ref,
):
    row = iota((BLOCK, LANES), 0)
    lane = iota((BLOCK, LANES), 1)
    rel = row - srel_ref[...]
    zero_ref[...] = jnp.zeros(zero_ref.shape, f32)

    @pl.when(pl.program_id(0) == 0)
    def _():
        mask_ref[...] = jnp.where((lane <= row) & (lane >= srel_ref[...]), 1.0, 0.0)

    for j in range(TILES):
        query_ref[:, tile(j)] = feature_of(q_ref, hq_ref, taps_ref, 0, j, rel, wq_ref.at[j])
        acc = skip_ref[:, tile(j)] * x_ref[:, tile(j)].astype(f32)
        acc_ref[:, tile(j)] = band_sum(j, x_ref, own_ref, mask_ref, acc)


def make_own(projected, halo, tapsx, srel, product, own, skip):
    width = product.shape[1]
    shape = pltpu.HBM
    return pl.pallas_call(
        own_kernel,
        grid=(width // WIDE,),
        out_shape=(
            shape((BLOCK, width), f32),
            shape((BLOCK, width), f32),
            shape((8, LANES), f32),
        ),
        in_specs=[
            columns(BLOCK),
            columns(8),
            columns(24),
            fixed((BLOCK, LANES)),
            columns(BLOCK),
            rows_of(WIDE // GROUP),
            columns(1),
        ],
        out_specs=(columns(BLOCK), columns(BLOCK), fixed((8, LANES))),
        scratch_shapes=[
            pltpu.VMEM((TILES, 8 + BLOCK, LANES), f32),
            pltpu.VMEM((BLOCK, LANES), f32),
        ],
        compiler_params=params(),
        name="own",
    )(*hbm(projected, halo, tapsx, srel, product, own, skip))


def earlier_kernel(x_ref, taps_ref, srel_ref, acc_ref, out_ref, mask_ref):
    row = iota((BLOCK, LANES), 0)
    lane = iota((BLOCK, LANES), 1)

    @pl.when(pl.program_id(0) == 0)
    def _():
        inside = (lane > row) & (lane - BLOCK >= srel_ref[...])
        mask_ref[...] = jnp.where(inside, 1.0, 0.0)

    for j in range(TILES):
        out_ref[:, tile(j)] = band_sum(j, x_ref, taps_ref, mask_ref, acc_ref[:, tile(j)])


def make_earlier(before, med, srel, acc):
    return pl.pallas_call(
        earlier_kernel,
        grid=(acc.shape[1] // WIDE,),
        out_shape=pltpu.HBM(acc.shape, f32),
        in_specs=[
            columns(BLOCK),
            rows_of(WIDE // GROUP),
            fixed((BLOCK, LANES)),
            columns(BLOCK),
        ],
        out_specs=columns(BLOCK),
        scratch_shapes=[pltpu.VMEM((BLOCK, LANES), f32)],
        compiler_params=params(),
        name="earlier",
    )(before, *hbm(med, srel, acc))


def totals_kernel(which_ref, terms_ref, rates_ref, live_ref, zero_ref, out_ref):
    decay = jnp.exp(-rates_ref[...] * float(BLOCK))
    state = zero_ref[...]
    kept = jnp.ones((8, LANES), f32)
    for b in range(terms_ref.shape[0]):
        factor = live_ref[b : b + 1] * decay
        state = factor * state + terms_ref[b].astype(f32)
        kept = factor * kept
    out_ref[0] = state
    out_ref[1] = kept


def whole(value):
    return pl.BlockSpec(value.shape, lambda *_: (0,) * value.ndim)


def item_spec(tiles):
    return pl.BlockSpec((8, LANES), lambda _, which: (which[0] // tiles, which[0] % tiles))


def make_totals(which, terms, ratesx, live, zero):
    tiles = ratesx.shape[1] // LANES
    return pl.pallas_call(
        totals_kernel,
        out_shape=jax.ShapeDtypeStruct((2, 8, LANES), f32),
        grid_spec=pltpu.PrefetchScalarGridSpec(
            num_scalar_prefetch=1,
            grid=(1,),
            in_specs=[in_vmem(), item_spec(tiles), whole(live), whole(zero)],
            out_specs=in_vmem(),
        ),
        compiler_params=params(),
        name="totals",
    )(which, terms, *hbm(ratesx, live, zero))


def states_kernel(which_ref, terms_ref, rates_ref, live_ref, one_ref, two_ref, out_ref):
    decay = jnp.exp(-rates_ref[...] * float(BLOCK))
    state = one_ref[0] + one_ref[1] * two_ref[...]
    for b in range(terms_ref.shape[0]):
        out_ref[b] = state.astype(bf16)
        state = live_ref[b : b + 1] * decay * state + terms_ref[b].astype(f32)


def make_states(which, terms, ratesx, live, one, two):
    tiles = ratesx.shape[1] // LANES
    return pl.pallas_call(
        states_kernel,
        out_shape=pltpu.HBM(terms.shape, bf16),
        grid_spec=pltpu.PrefetchScalarGridSpec(
            num_scalar_prefetch=1,
            grid=(1,),
            in_specs=[in_vmem(), item_spec(tiles), whole(live), in_vmem(), in_vmem()],
            out_specs=whole(terms),
        ),
        compiler_params=params(),
        name="states",
    )(which, terms, *hbm(ratesx, live), one, two)


def final_kernel(acc_ref, query_ref, dec_ref, state_ref, out_ref):
    same = iota((LANES, LANES), 0) // MODES == iota((LANES, LANES), 1) // GROUP
    keep = jnp.where(same, 1.0, 0.0).astype(bf16)
    for j in range(TILES):
        one = jnp.concatenate([state_ref[0, j], state_ref[1, j]], axis=0)
        spread = jnp.concatenate([one] * PER_TILE, axis=0) * keep
        carried = jnp.dot(dec_ref[:, tile(j)], spread, preferred_element_type=f32)
        filtered = (acc_ref[:, tile(j)] + carried).astype(bf16).astype(f32)
        out_ref[:, tile(j)] = (query_ref[:, tile(j)] * filtered).astype(bf16)


def make_final(acc, query, dec, state):
    return pl.pallas_call(
        final_kernel,
        grid=(acc.shape[1] // WIDE,),
        out_shape=pltpu.HBM(acc.shape, bf16),
        in_specs=[
            columns(BLOCK),
            columns(BLOCK),
            columns(BLOCK),
            pl.BlockSpec((2, TILES, 8, LANES), lambda j: (0, j, 0, 0)),
        ],
        out_specs=columns(BLOCK),
        compiler_params=params(),
        name="final",
    )(*hbm(acc, query, dec), state)


def per_device(projected, doc_lengths, short_taps, medium_taps, decay_rates, residues, skip_gain):
    ts_count = lax.axis_size("ts")
    ctx_count = lax.axis_size("ctx")
    count = ts_count * ctx_count
    ctx = lax.axis_index("ctx")
    index = ctx * ts_count + lax.axis_index("ts")
    size = SPAN * ts_count
    which = (index % size).astype(i32)
    groups = [[s * size + j for j in range(size)] for s in range(count // size)]
    onward = [(i, i + 1) for i in range(count - 1)]
    width = projected.shape[1] // 3

    def from_ctx(value, by):
        return lax.ppermute(value, "ctx", [(i, i + by) for i in range(ctx_count - by)])

    halo = lax.ppermute(projected[BLOCK - 8 :], FLAT, onward)
    place = jnp.concatenate(
        [jnp.stack([index * BLOCK, (index - which) * BLOCK]).astype(i32), doc_lengths]
    )
    scaled = residues * jnp.sqrt(-jnp.expm1(-2.0 * decay_rates))
    taps = jnp.pad(short_taps, ((0, 0), (0, 1), (0, 0))).reshape(24, -1)
    stack = jnp.concatenate([taps, decay_rates, scaled, jnp.zeros_like(taps[:8])], axis=0)
    srel, live, tapsx, ratesx, scalex, tail = make_spread(place, stack, width)
    product, contrib, edge = make_product(projected, halo, tapsx, srel, tail)
    items = contrib.reshape(size, 8, LANES)
    terms = lax.all_to_all(
        items, FLAT, split_axis=0, concat_axis=0, tiled=True, axis_index_groups=groups
    )
    before = lax.ppermute(product, FLAT, onward)
    dec, own, med = make_tables(srel, ratesx, scalex, medium_taps)
    query, acc, zero = make_own(projected, edge, tapsx, srel, product, own, skip_gain.reshape(1, -1))
    ours = which.reshape(1)
    totals = make_totals(ours, terms, ratesx, live, zero)
    one = from_ctx(totals, SPAN)
    two = from_ctx(totals[0], 2 * SPAN)
    states = make_states(ours, terms, ratesx, live, one, two)
    back = lax.all_to_all(
        states, FLAT, split_axis=0, concat_axis=0, tiled=True, axis_index_groups=groups
    )
    acc = make_earlier(before, med, srel, acc)
    return make_final(acc, query, dec, back.reshape(2, width // LANES, 8, LANES))


def solution(mesh):
    return jax.shard_map(
        per_device,
        mesh=mesh,
        in_specs=(P(FLAT, None), P(), P(), P(), P(), P(), P()),
        out_specs=P(FLAT, None),
        check_vma=False,
    )
```

time: 113 us -> 98.7 us (0.87)
  the two profiles are of different devices: /device:TPU:1 before, /device:TPU:59 now
where the time goes in v2:
time: 98.7 us; the launch traced here: 97.1 us
  Pallas kernels  51 us (52%)
  starting transfers between devices  40.4 us (41%)
  other arithmetic  2.28 us (2%)
  local copies, waits for them, and re-layouts  1.76 us (2%)
  waiting for transfers between devices  1.53 us (2%)
    all_to_all x1, starting transfers between devices, per_device(): lax.all_to_all(items, FLAT, split_axis=0, concat_axis=0, tiled=True, axis...  13.5 us
    all_to_all x1, starting transfers between devices, per_device(): lax.all_to_all(states, FLAT, split_axis=0, concat_axis=0, tiled=True, axi...  12.2 us
    pallas_call x1, Pallas kernels, make_own(): pl.pallas_call(own_kernel, grid=(width // WIDE,), out_shape=(shape((BLOCK...  11.9 us
    pallas_call x1, Pallas kernels, make_earlier(): pl.pallas_call(earlier_kernel, grid=(acc.shape[1] // WIDE,), out_shape=pl...  10.1 us
    pallas_call x1, Pallas kernels, make_product(): pl.pallas_call(product_kernel, grid=(steps,), out_shape=(shape((BLOCK, wi...  8.21 us
    ppermute x2, starting transfers between devices, from_ctx(): lax.ppermute(value, 'ctx', [(i, i + by) for i in range(ctx_count - by)])  8.19 us
    pallas_call x1, Pallas kernels, make_final(): pl.pallas_call(final_kernel, grid=(acc.shape[1] // WIDE,), out_shape=pltp...  6.63 us
    pallas_call x1, Pallas kernels, make_tables(): pl.pallas_call(tables_kernel, grid=(width // WIDE,), out_shape=(shape((BL...  6.5 us
  transfers between devices with their start and end apart: 6, of which 1 were waited for; matrix products, arithmetic and copies ran while one was open for 3% of the time, Pallas kernels for 37%

profile of v2, /device:TPU:59, one launch (start us, length us, event | category | flops | bytes accessed | tf_op | source)
XLA Modules:
  0.0 97.1 jit_solution(5272110571040981405)
XLA Ops:
  0.0 0.9 slice.6
  0.9 4.6 %collective-permute-start = (bf16[8,12288]{1,0:T(8,128)(2,1)S(1)}, bf16[8,12288]{1,0:T(8,128)(2,1)S(1)}, u32[]{:S(2)}, u32[]{:S(2)}) collective-permute-start(bf16[8,12288]{1,0:T(8,128)(2,1)S(1)} %slice.6), channel_id=1, source_target_pairs={{0,1},{1,2},{2,3},{3,4},{4,5},{5,6},{6,7},{7,8},{8,9},{9,10},{10,1... | collective-permute-start | bytes 589832 | tf_op jit(solution)/shard_map/ppermute | solution.py:489
  5.5 0.7 pad_bitcast_fusion
  6.3 0.8 sqrt_multiply_fusion
  7.0 0.1 pad.8.clone
  7.1 0.7 pad_add_fusion.place_ref
  7.8 0.8 maximum_maximum_fusion.stack_ref
  8.6 5.2 %spread.1 = (s32[128,128]{1,0:T(8,128)}, f32[64,128]{1,0:T(8,128)}, f32[24,4096]{1,0:T(8,128)}, f32[16,4096]{1,0:T(8,128)}, f32[16,4096]{1,0:T(8,128)}, /*index=5*/bf16[4096,128]{1,0:T(8,128)(2,1)}) custom-call(s32[18]{0:T(128)S(1)} %pad_add_fusion.place_ref, f32[64,256]{1,0:T(8,128)S(1)} %maximum_maximum_fusion.stack_ref), custom_call_target="tpu_custom_call" | custom-call | tf_op jit(solution)/shard_map/spread/pallas_call | solution.py:112
  13.9 0.0 collective-permute-done.hq_ref.hk_ref.hv_ref
  13.9 8.2 %product.1 = (bf16[128,4096]{1,0:T(8,128)(2,1)}, bf16[2,32,8,128]{3,2,1,0:T(8,128)(2,1)}, bf16[8,4096]{1,0:T(8,128)(2,1)}) custom-call(bf16[128,12288]{1,0:T(8,128)(2,1)} %q_ref.1, bf16[128,12288]{1,0:T(8,128)(2,1)} %q_ref.1, bf16[8,12288]{1,0:T(8,128)(2,1)S(1)} %collective-permute-done.hq_ref.hk_ref.hv_ref, ...), custom_call_target="tpu_custom_call" | custom-call | tf_op jit(solution)/shard_map/product/pallas_call | solution.py:252
  22.1 1.9 %collective-permute-start.1 = (bf16[128,4096]{1,0:T(8,128)(2,1)}, bf16[128,4096]{1,0:T(8,128)(2,1)S(1)}, u32[]{:S(2)}, u32[]{:S(2)}) collective-permute-start(bf16[128,4096]{1,0:T(8,128)(2,1)} %get-tuple-element.23.x_ref), channel_id=1, source_target_pairs={{0,1},{1,2},{2,3},{3,4},{4,5},{5,6},{6,7},{7,8},{8,9},{9,10},{10,1... | collective-permute-start | bytes 3145736 | tf_op jit(solution)/shard_map/ppermute | solution.py:502
  24.0 13.5 %all-to-all-start = ((bf16[64,8,128]{2,1,0:T(8,128)(2,1)}), bf16[64,8,128]{2,1,0:T(8,128)(2,1)S(1)}, u32[]{:S(2)}, u32[]{:S(2)}) async-start(bf16[64,8,128]{2,1,0:T(8,128)(2,1)} %bitcast.11), calls=%async_computation | async-start | bytes 262144 | tf_op jit(solution)/shard_map/all_to_all | solution.py:499
  37.6 6.5 %tables.1 = (bf16[128,4096]{1,0:T(8,128)(2,1)}, f32[256,128]{1,0:T(8,128)}, f32[256,128]{1,0:T(8,128)}) custom-call(s32[128,128]{1,0:T(8,128)} %get-tuple-element.21.srel_ref, f32[16,4096]{1,0:T(8,128)} %get-tuple-element.24.ratesx_ref.rates_ref, f32[16,4096]{1,0:T(8,128)} %get-tuple-element.25.scalex_ref, f32[128,256]{1,0:T(8,128)} %medium_ref.1), custom_call_target="tpu_custom_call" | custom-call | tf_op jit(solution)/shard_map/tables/pallas_call | solution.py:189
  44.1 11.9 %own.1 = (f32[128,4096]{1,0:T(8,128)}, f32[128,4096]{1,0:T(8,128)}, f32[8,128]{1,0:T(8,128)}) custom-call(bf16[128,12288]{1,0:T(8,128)(2,1)} %q_ref.1, bf16[8,4096]{1,0:T(8,128)(2,1)} %get-tuple-element.27.hq_ref, f32[24,4096]{1,0:T(8,128)} %get-tuple-element.20.taps_ref, s32[128,128]{1,0:T(8,128)} %get-tuple-element.21.srel_ref, ...), custom_call_target="tpu_custom_call" | custom-call | tf_op jit(solution)/shard_map/own/pallas_call | solution.py:328
  56.0 0.0 all-to-all-done.terms_ref
  56.0 0.9 totals.1
  56.9 5.4 %collective-permute-start.2 = (f32[2,8,128]{2,1,0:T(8,128)S(1)}, f32[2,8,128]{2,1,0:T(8,128)S(1)}, u32[]{:S(2)}, u32[]{:S(2)}) collective-permute-start(f32[2,8,128]{2,1,0:T(8,128)S(1)} %totals.1), channel_id=1, source_target_pairs={{0,64},{16,80},{32,96},{48,112},{64,128},{80,144},{96,160},{112,17... | collective-permute-start | bytes 24584 | tf_op jit(solution)/shard_map/ppermute | solution.py:487
  62.3 2.8 %collective-permute-start.3 = (f32[8,128]{1,0:T(8,128)S(1)}, f32[8,128]{1,0:T(8,128)S(1)}, u32[]{:S(2)}, u32[]{:S(2)}) collective-permute-start(f32[8,128]{1,0:T(8,128)S(1)} %slice_bitcast_fusion), channel_id=1, source_target_pairs={{0,128},{16,144},{32,160},{48,176},{64,192},{80,208},{96,224},{112... | collective-permute-start | bytes 12296 | tf_op jit(solution)/shard_map/ppermute | solution.py:487
  65.1 1.5 %collective-permute-done.3.two_ref = f32[8,128]{1,0:T(8,128)S(1)} collective-permute-done((f32[8,128]{1,0:T(8,128)S(1)}, f32[8,128]{1,0:T(8,128)S(1)}, u32[]{:S(2)}, u32[]{:S(2)}) %collective-permute-start.3) | collective-permute-done | bytes 4128 | tf_op jit(solution)/shard_map/ppermute | solution.py:487
  66.6 0.0 collective-permute-done.2.one_ref
  66.6 1.6 %states.1 = bf16[64,8,128]{2,1,0:T(8,128)(2,1)} custom-call(s32[1]{0:T(128)} %bitcast.4.which_ref, bf16[64,8,128]{2,1,0:T(8,128)(2,1)S(1)} %all-to-all-done.terms_ref, f32[16,4096]{1,0:T(8,128)} %get-tuple-element.24.ratesx_ref.rates_ref, f32[64,128]{1,0:T(8,128)} %get-tuple-element.33.live_ref, f32[2,8,128]{2,1,0:T(8,128)S(1)} %collective-permute-done.2.one_ref, ...), custom_call_target="tpu_custom_call" | custom-call | tf_op jit(solution)/shard_map/states/pallas_call | solution.py:432
  68.2 12.2 %all-to-all-start.1 = ((bf16[64,8,128]{2,1,0:T(8,128)(2,1)}), bf16[64,8,128]{2,1,0:T(8,128)(2,1)S(1)}, u32[]{:S(2)}, u32[]{:S(2)}) async-start(bf16[64,8,128]{2,1,0:T(8,128)(2,1)} %states.1), calls=%async_computation.1 | async-start | bytes 262144 | tf_op jit(solution)/shard_map/all_to_all | solution.py:510
  80.3 0.0 collective-permute-done.1.x_ref
  80.4 10.1 %earlier.1.acc_ref = f32[128,4096]{1,0:T(8,128)} custom-call(bf16[128,4096]{1,0:T(8,128)(2,1)S(1)} %collective-permute-done.1.x_ref, f32[256,128]{1,0:T(8,128)} %get-tuple-element.26.taps_ref, s32[128,128]{1,0:T(8,128)} %get-tuple-element.21.srel_ref, f32[128,4096]{1,0:T(8,128)} %get-tuple-element.29.acc_ref), custom_call_target="tpu_custom_call" | custom-call | tf_op jit(solution)/shard_map/earlier/pallas_call | solution.py:369
  90.5 0.0 all-to-all-done.1
  90.5 6.6 %final.1 = bf16[128,4096]{1,0:T(8,128)(2,1)} custom-call(f32[128,4096]{1,0:T(8,128)} %earlier.1.acc_ref, f32[128,4096]{1,0:T(8,128)} %get-tuple-element.30.query_ref, bf16[128,4096]{1,0:T(8,128)(2,1)} %get-tuple-element.31.dec_ref, bf16[2,32,8,128]{3,2,1,0:T(8,128)(2,1)S(1)} %bitcast.10), custom_call_target="tpu_custom_call" | custom-call | tf_op jit(solution)/shard_map/final/pallas_call | solution.py:458
  (2 shorter events, 0.0 us)
Async XLA Ops:
  0.9 12.9 %collective-permute-start = (bf16[8,12288]{1,0:T(8,128)(2,1)S(1)}, bf16[8,12288]{1,0:T(8,128)(2,1)S(1)}, u32[]{:S(2)}, u32[]{:S(2)}) collective-permute-start(bf16[8,12288]{1,0:T(8,128)(2,1)S(1)} %slice.6), channel_id=1, source_target_pairs={{0,1},{1,2},{2,3},{3,4},{4,5},{5,6},{6,7},{7,8},{8,9},{9,10},{10,1... | collective-permute-start | bytes 589832 | tf_op jit(solution)/shard_map/ppermute | solution.py:489
  22.1 58.3 %collective-permute-start.1 = (bf16[128,4096]{1,0:T(8,128)(2,1)}, bf16[128,4096]{1,0:T(8,128)(2,1)S(1)}, u32[]{:S(2)}, u32[]{:S(2)}) collective-permute-start(bf16[128,4096]{1,0:T(8,128)(2,1)} %get-tuple-element.23.x_ref), channel_id=1, source_target_pairs={{0,1},{1,2},{2,3},{3,4},{4,5},{5,6},{6,7},{7,8},{8,9},{9,10},{10,1... | collective-permute-start | bytes 3145736 | tf_op jit(solution)/shard_map/ppermute | solution.py:502
  24.0 32.0 %all-to-all-start = ((bf16[64,8,128]{2,1,0:T(8,128)(2,1)}), bf16[64,8,128]{2,1,0:T(8,128)(2,1)S(1)}, u32[]{:S(2)}, u32[]{:S(2)}) async-start(bf16[64,8,128]{2,1,0:T(8,128)(2,1)} %bitcast.11), calls=%async_computation | async-start | bytes 262144 | tf_op jit(solution)/shard_map/all_to_all | solution.py:499
  56.9 9.7 %collective-permute-start.2 = (f32[2,8,128]{2,1,0:T(8,128)S(1)}, f32[2,8,128]{2,1,0:T(8,128)S(1)}, u32[]{:S(2)}, u32[]{:S(2)}) collective-permute-start(f32[2,8,128]{2,1,0:T(8,128)S(1)} %totals.1), channel_id=1, source_target_pairs={{0,64},{16,80},{32,96},{48,112},{64,128},{80,144},{96,160},{112,17... | collective-permute-start | bytes 24584 | tf_op jit(solution)/shard_map/ppermute | solution.py:487
  62.3 4.4 %collective-permute-start.3 = (f32[8,128]{1,0:T(8,128)S(1)}, f32[8,128]{1,0:T(8,128)S(1)}, u32[]{:S(2)}, u32[]{:S(2)}) collective-permute-start(f32[8,128]{1,0:T(8,128)S(1)} %slice_bitcast_fusion), channel_id=1, source_target_pairs={{0,128},{16,144},{32,160},{48,176},{64,192},{80,208},{96,224},{112... | collective-permute-start | bytes 12296 | tf_op jit(solution)/shard_map/ppermute | solution.py:487
  68.2 22.3 %all-to-all-start.1 = ((bf16[64,8,128]{2,1,0:T(8,128)(2,1)}), bf16[64,8,128]{2,1,0:T(8,128)(2,1)S(1)}, u32[]{:S(2)}, u32[]{:S(2)}) async-start(bf16[64,8,128]{2,1,0:T(8,128)(2,1)} %states.1), calls=%async_computation.1 | async-start | bytes 262144 | tf_op jit(solution)/shard_map/all_to_all | solution.py:510

commit v3 on v1

v3 whole, which is shorter than its diff:
```python
import jax
import jax.numpy as jnp
from jax import lax
from jax.experimental import pallas as pl
from jax.experimental.pallas import tpu as pltpu
from jax.sharding import PartitionSpec as P

GROUP = 16
SHORT = 7
BLOCK = 128
MODES = 16
LANES = 128
DOCS = 16
SPAN = 4
PER_TILE = LANES // GROUP
FLAT = ("ctx", "ts")
HIGHEST = lax.Precision.HIGHEST
f32 = jnp.float32
bf16 = jnp.bfloat16
i32 = jnp.int32


def iota(shape, dim):
    return lax.broadcasted_iota(i32, shape, dim)


TILES = 4
CHUNK = 8
WIDE = CHUNK * LANES


def tile(j):
    if isinstance(j, int):
        return slice(j * LANES, (j + 1) * LANES)
    return pl.ds(pl.multiple_of(j * LANES, LANES), LANES)


def for_tiles(count, body):
    def step(i, carry):
        for j in range(TILES):
            body(i * TILES + j)
        return carry

    lax.fori_loop(0, count // TILES, step, 0)


def in_hbm():
    return pl.BlockSpec(memory_space=pltpu.HBM)


def in_vmem():
    return pl.BlockSpec(memory_space=pltpu.VMEM)


def in_smem():
    return pl.BlockSpec(memory_space=pltpu.SMEM)


def columns(rows, first=0):
    return pl.BlockSpec((rows, WIDE), lambda j: (0, first + j))


def rows_of(count):
    return pl.BlockSpec((count, LANES), lambda j: (j, 0))


def fixed(shape):
    return pl.BlockSpec(shape, lambda j: (0,) * len(shape))


def hbm(*values):
    return [pltpu.with_memory_space_constraint(value, pltpu.HBM) for value in values]


def params(mib=12):
    return pltpu.CompilerParams(vmem_limit_bytes=mib << 20)


def front_kernel(
    place_ref, docs_ref, taps_ref, rates_ref, raw_ref,
    srel_ref, live_ref, tapsx_ref, tail_ref, product_ref, head_ref,
    stack_ref, pieces_ref, raws_ref, wk_ref, wv_ref, sems,
):
    width = product_ref.shape[1]
    copies = [
        pltpu.make_async_copy(
            raw_ref.at[:, pl.ds(width * (1 + p), width)], raws_ref.at[p], sems.at[p]
        )
        for p in range(2)
    ]
    for copy in copies:
        copy.start()
    row = iota((BLOCK, LANES), 0)
    base = place_ref[0]
    pos = base + row
    starts = jnp.zeros((BLOCK, LANES), i32)
    ends = place_ref[1] + row[: live_ref.shape[0]] * BLOCK + (BLOCK - 1)
    lasts = jnp.zeros(live_ref.shape, i32)
    begin = jnp.int32(0)
    for d in range(DOCS):
        starts = jnp.where(pos >= begin, begin, starts)
        lasts = jnp.where(ends >= begin, begin, lasts)
        begin = begin + docs_ref[d]
    srel_ref[...] = starts - base
    live_ref[...] = jnp.where(lasts < ends - (BLOCK - 1), 1.0, 0.0)
    stack_ref[...] = jnp.zeros(stack_ref.shape, f32)
    for p in range(3):
        stack_ref[8 * p : 8 * p + SHORT] = taps_ref[p]
    stack_ref[24:40] = rates_ref[...]
    split_into(pieces_ref, stack_ref[...])
    own_mode = iota((MODES, LANES), 0) == iota((MODES, LANES), 1) % MODES
    behind = (BLOCK - 1 - row).astype(f32)

    def expand(j):
        spread = expanded(pieces_ref, j)
        tapsx_ref[:, tile(j)] = spread[0:24]
        rate = jnp.sum(jnp.where(own_mode, spread[24:40], 0.0), axis=0, keepdims=True)
        tail_ref[tile(j), :] = jnp.exp(-rate * behind).astype(bf16).T

    for_tiles(width // LANES, expand)
    for copy in copies:
        copy.wait()
    rel = row - (starts - base)
    nothing = jnp.zeros((8, LANES), f32)

    def multiply(j):
        slot = lax.rem(j, TILES)
        key = feature_of(raws_ref.at[0], nothing, tapsx_ref, 1, j, rel, wk_ref.at[slot])
        value = feature_of(raws_ref.at[1], nothing, tapsx_ref, 2, j, rel, wv_ref.at[slot])
        product_ref[:, tile(j)] = (key * value).astype(bf16)

    for_tiles(width // LANES, multiply)
    head_ref[0] = raws_ref[0, 0:8]
    head_ref[1] = raws_ref[1, 0:8]


def split_into(pieces_ref, whole):
    upper = whole.astype(bf16)
    rest = whole - upper.astype(f32)
    middle = rest.astype(bf16)
    pieces_ref[0] = upper
    pieces_ref[1] = middle
    pieces_ref[2] = (rest - middle.astype(f32)).astype(bf16)


def expanded(pieces_ref, j):
    _, lines, groups = pieces_ref.shape
    pieces = jnp.concatenate([pieces_ref[0], pieces_ref[1], pieces_ref[2]], axis=0)
    ahead = iota((groups, LANES), 0) - iota((groups, LANES), 1) // GROUP
    hot = jnp.where(ahead == j * PER_TILE, 1.0, 0.0).astype(bf16)
    spread = jnp.dot(pieces, hot, preferred_element_type=f32)
    return spread[0:lines] + spread[lines : 2 * lines] + spread[2 * lines :]


def make_front(place, doc_lengths, short_taps, decay_rates, projected):
    width = projected.shape[1] // 3
    groups = decay_rates.shape[1]
    shape = jax.ShapeDtypeStruct
    return pl.pallas_call(
        front_kernel,
        grid=(1,),
        out_shape=(
            shape((BLOCK, LANES), i32),
            shape((4 * DOCS, LANES), f32),
            shape((24, width), f32),
            shape((width, BLOCK), bf16),
            shape((BLOCK, width), bf16),
            shape((2, 8, width), bf16),
        ),
        in_specs=[
            in_smem(),
            in_smem(),
            fixed(short_taps.shape),
            fixed(decay_rates.shape),
            in_hbm(),
        ],
        out_specs=tuple([in_vmem()] * 6),
        scratch_shapes=[
            pltpu.VMEM((48, groups), f32),
            pltpu.VMEM((3, 48, groups), bf16),
            pltpu.VMEM((2, BLOCK, width), bf16),
            pltpu.VMEM((TILES, 8 + BLOCK, LANES), f32),
            pltpu.VMEM((TILES, 8 + BLOCK, LANES), f32),
            pltpu.SemaphoreType.DMA((2,)),
        ],
        compiler_params=params(),
        name="front",
    )(place, *hbm(doc_lengths, short_taps, decay_rates, projected))


def edge_kernel(
    main_ref, head_ref, halo_ref, taps_ref, srel_ref, live_ref, tail_ref,
    product_out, contrib_out, edge_ref, tapsq_ref, srel_out, live_out,
    window_ref, product_ref, contrib_ref, sems,
):
    width = main_ref.shape[1]
    row = iota((BLOCK, LANES), 0)
    kept = jnp.where(row >= srel_ref[BLOCK - 1 : BLOCK], 1.0, 0.0).astype(bf16)
    rel = (row - srel_ref[...])[0:8]
    lane_group = iota((MODES, LANES), 1) // GROUP
    edge_ref[...] = halo_ref[:, 0:width]
    tapsq_ref[...] = taps_ref[0:8]
    srel_out[...] = srel_ref[...]
    live_out[...] = live_ref[...]

    def body(j):
        slot = lax.rem(j, TILES)
        values = []
        for p in range(2):
            past = halo_ref[:, tile(j + (1 + p) * (width // LANES))].astype(f32)
            window = window_ref.at[slot, p]
            window[0:8] = past
            window[8:16] = head_ref[p, :, tile(j)].astype(f32)
            line = 8 * (p + 1)
            summed = window[8:16] * taps_ref[line : line + 1, tile(j)]
            for offset in range(1, SHORT):
                term = window[8 - offset : 16 - offset]
                term = term * taps_ref[line + offset : line + offset + 1, tile(j)]
                summed = summed + jnp.where(rel >= offset, term, 0.0)
            values.append(summed)
        first = values[0] * values[1]
        rest = main_ref[0:16, tile(j)].astype(f32)[8:16]
        both = jnp.concatenate([first, rest], axis=0).astype(bf16)
        product = jnp.concatenate([both, main_ref[16:BLOCK, tile(j)]], axis=0)
        product_ref[:, tile(j)] = product
        all_modes = jnp.dot(
            tail_ref[tile(j), :], product * kept, preferred_element_type=f32
        )
        contrib = all_modes[0:MODES]
        for g in range(1, PER_TILE):
            contrib = jnp.where(
                lane_group == g, all_modes[g * MODES : (g + 1) * MODES], contrib
            )
        contrib_ref[0, j] = contrib[0:8].astype(bf16)
        contrib_ref[1, j] = contrib[8:16].astype(bf16)

    def copies(c):
        at = pl.ds(pl.multiple_of(c * WIDE, LANES), WIDE)
        tiles = pl.ds(pl.multiple_of(c * CHUNK, CHUNK), CHUNK)
        return (
            pltpu.make_async_copy(product_ref.at[:, at], product_out.at[:, at], sems.at[0, c]),
            pltpu.make_async_copy(contrib_ref.at[:, tiles], contrib_out.at[:, tiles], sems.at[1, c]),
        )

    def chunk(c, carry):
        def inner(i, more):
            for k in range(TILES):
                body(c * CHUNK + i * TILES + k)
            return more

        lax.fori_loop(0, CHUNK // TILES, inner, 0)
        for copy in copies(c):
            copy.start()
        return carry

    chunks = width // WIDE
    lax.fori_loop(0, chunks, chunk, 0)
    for c in range(chunks):
        for copy in copies(c):
            copy.wait()


def make_edge(main, head, halo, tapsx, srel, live, tail):
    width = main.shape[1]
    shape = pltpu.HBM
    return pl.pallas_call(
        edge_kernel,
        out_shape=(
            shape((BLOCK, width), bf16),
            shape((2, width // LANES, 8, LANES), bf16),
            shape((8, width), bf16),
            shape((8, width), f32),
            shape(srel.shape, i32),
            shape(live.shape, f32),
        ),
        in_specs=[in_vmem()] * 7,
        out_specs=(in_hbm(), in_hbm(), in_vmem(), in_vmem(), in_vmem(), in_vmem()),
        scratch_shapes=[
            pltpu.VMEM((TILES, 2, 16, LANES), f32),
            pltpu.VMEM((BLOCK, width), bf16),
            pltpu.VMEM((2, width // LANES, 8, LANES), bf16),
            pltpu.SemaphoreType.DMA((2, width // WIDE)),
        ],
        compiler_params=params(),
        name="edge",
    )(main, head, halo, tapsx, srel, live, tail)


def tables_kernel(
    srel_ref, rates_ref, scaled_ref, medium_ref,
    dec_ref, own_ref, med_ref, ratesx_ref,
    long_ref, pieces_ref,
):
    row = iota((BLOCK, LANES), 0)
    lane = iota((BLOCK, LANES), 1)
    old = srel_ref[...] < 0
    own_mode = iota((MODES, LANES), 0) == iota((MODES, LANES), 1) % MODES
    ahead = (row + 1).astype(f32)
    behind = (BLOCK - 1 - row).astype(f32)
    each = LANES // PER_TILE
    split_into(pieces_ref, jnp.concatenate([rates_ref[...], scaled_ref[...]], axis=0))
    long_ref[...] = jnp.zeros(long_ref.shape, f32)

    def step(i, carry):
        total = long_ref[(i * TILES) // each]
        for k in range(TILES):
            j = i * TILES + k
            spread = expanded(pieces_ref, j)
            ratesx_ref[:, tile(j)] = spread[0:MODES]
            rate = jnp.sum(jnp.where(own_mode, spread[0:MODES], 0.0), axis=0, keepdims=True)
            scale = jnp.sum(jnp.where(own_mode, spread[MODES:], 0.0), axis=0, keepdims=True)
            decay = jnp.where(old, scale * jnp.exp(-rate * ahead), 0.0)
            dec_ref[:, tile(j)] = decay.astype(bf16)
            power = scale * jnp.exp(-rate * behind)
            upper = power.astype(bf16)
            lower = (power - upper.astype(f32)).astype(bf16)
            first = lax.rem(j, each) * PER_TILE
            hot = jnp.where(lane - row // MODES == first, 1.0, 0.0).astype(bf16)
            total = total + jnp.dot(
                jnp.concatenate([upper, lower], axis=1),
                jnp.concatenate([hot, hot], axis=0),
                preferred_element_type=f32,
            )
        long_ref[(i * TILES) // each] = total
        return carry

    lax.fori_loop(0, dec_ref.shape[1] // (LANES * TILES), step, 0)
    flip = jnp.where(row + lane == BLOCK - 1, 1.0, 0.0)
    for h in range(long_ref.shape[0]):
        medium = jnp.dot(
            flip, medium_ref[:, tile(h)], precision=HIGHEST, preferred_element_type=f32
        )
        med_ref[tile(h), :] = medium.T
        own_ref[tile(h), :] = (medium + long_ref[h]).T


def make_tables(srel, decay_rates, scaled, medium_taps, width):
    groups = medium_taps.shape[1]
    shape = jax.ShapeDtypeStruct
    return pl.pallas_call(
        tables_kernel,
        grid=(1,),
        out_shape=(
            pltpu.HBM((BLOCK, width), bf16),
            shape((groups, BLOCK), f32),
            pltpu.HBM((groups, BLOCK), f32),
            shape((MODES, width), f32),
        ),
        in_specs=[
            fixed((BLOCK, LANES)),
            fixed(decay_rates.shape),
            fixed(scaled.shape),
            fixed(medium_taps.shape),
        ],
        out_specs=tuple([in_vmem()] * 4),
        scratch_shapes=[
            pltpu.VMEM((groups // LANES, BLOCK, LANES), f32),
            pltpu.VMEM((3, 2 * MODES, groups), bf16),
        ],
        compiler_params=params(),
        name="tables",
    )(*hbm(srel, decay_rates, scaled, medium_taps))


def feature_of(raw_ref, past, taps_ref, part, j, rel, window_ref):
    window_ref[0:8] = past
    window_ref[8 : 8 + BLOCK] = raw_ref[:, tile(j)].astype(f32)
    summed = window_ref[8 : 8 + BLOCK] * taps_ref[8 * part : 8 * part + 1, tile(j)]
    for offset in range(1, SHORT):
        tap = taps_ref[8 * part + offset : 8 * part + offset + 1, tile(j)]
        term = window_ref[8 - offset : 8 - offset + BLOCK] * tap
        summed = summed + jnp.where(rel >= offset, term, 0.0)
    return summed


def band_sum(j, x_ref, taps_ref, mask_ref, acc):
    lane_group = iota((1, LANES), 1) // GROUP
    even = jnp.where(lane_group % 2 == 0, 1.0, 0.0).astype(bf16)
    odd = jnp.where(lane_group % 2 == 1, 1.0, 0.0).astype(bf16)
    x = x_ref[:, tile(j)]
    both = jnp.concatenate([x * even, x * odd], axis=0)
    pair_of = iota((BLOCK, LANES), 1) // (2 * GROUP)
    taps = taps_ref[pl.ds(pl.multiple_of(j * PER_TILE, PER_TILE), PER_TILE), :]
    pairs = []
    for pair in range(PER_TILE // 2):
        bands = []
        for side in range(2):
            g = 2 * pair + side
            line = jnp.broadcast_to(taps[g : g + 1], (16, BLOCK))
            ring = pltpu.roll(line, 1, 1, stride=1, stride_axis=0).astype(bf16)
            parts = [ring] + [pltpu.roll(ring, 16 * k, 1) for k in range(1, BLOCK // 16)]
            bands.append(jnp.concatenate(parts, axis=0) * mask_ref[...])
        pairs.append(jnp.concatenate(bands, axis=1))
    out = jnp.dot(jnp.concatenate(pairs, axis=0), both, preferred_element_type=f32)
    picked = out[0:BLOCK]
    for pair in range(1, PER_TILE // 2):
        picked = jnp.where(pair_of == pair, out[pair * BLOCK : (pair + 1) * BLOCK], picked)
    return acc + picked


def own_kernel(
    which_ref, q_ref, hq_ref, taps_ref, srel_ref, x_ref, own_ref, skip_ref, rates_ref, live_ref,
    query_ref, acc_ref, decay_ref, live_out,
    wq_ref, mask_ref,
):
    row = iota((BLOCK, LANES), 0)
    lane = iota((BLOCK, LANES), 1)
    rel = row - srel_ref[...]

    @pl.when(pl.program_id(0) == 0)
    def _():
        mask = (lane <= row) & (lane >= srel_ref[...])
        mask_ref[...] = jnp.where(mask, 1.0, 0.0).astype(bf16)
        decay_ref[...] = jnp.exp(-rates_ref[...] * float(BLOCK))
        live_out[...] = live_ref[...]

    def body(j):
        slot = lax.rem(j, TILES)
        past = hq_ref[:, tile(j)].astype(f32)
        query_ref[:, tile(j)] = feature_of(q_ref, past, taps_ref, 0, j, rel, wq_ref.at[slot])
        acc = skip_ref[:, tile(j)] * x_ref[:, tile(j)].astype(f32)
        acc_ref[:, tile(j)] = band_sum(j, x_ref, own_ref, mask_ref, acc)

    for_tiles(CHUNK, body)


def cols(rows, first=0):
    return pl.BlockSpec((rows, WIDE), lambda j, *_: (0, first + j))


def whole(shape):
    return pl.BlockSpec(shape, lambda *_: (0,) * len(shape))


def make_own(which, projected, edge, tapsq, srel, product, own, skip, ratesx, live):
    width = product.shape[1]
    tiles = width // LANES
    shape = jax.ShapeDtypeStruct
    return pl.pallas_call(
        own_kernel,
        out_shape=(
            pltpu.HBM((BLOCK, width), f32),
            pltpu.HBM((BLOCK, width), f32),
            shape((8, LANES), f32),
            shape(live.shape, f32),
        ),
        grid_spec=pltpu.PrefetchScalarGridSpec(
            num_scalar_prefetch=1,
            grid=(width // WIDE,),
            in_specs=[
                cols(BLOCK),
                cols(8),
                cols(8),
                whole((BLOCK, LANES)),
                cols(BLOCK),
                pl.BlockSpec((WIDE // GROUP, LANES), lambda j, *_: (j, 0)),
                cols(1),
                pl.BlockSpec((8, LANES), lambda _, at: (at[0] // tiles, at[0] % tiles)),
                whole(live.shape),
            ],
            out_specs=(
                cols(BLOCK),
                cols(BLOCK),
                whole((8, LANES)),
                whole(live.shape),
            ),
            scratch_shapes=[
                pltpu.VMEM((TILES, 8 + BLOCK, LANES), f32),
                pltpu.VMEM((BLOCK, LANES), bf16),
            ],
        ),
        compiler_params=params(20),
        name="own",
    )(which, *hbm(projected, edge, tapsq, srel, product), own, *hbm(skip), ratesx, *hbm(live))


def earlier_kernel(
    x_ref, taps_ref, srel_ref, acc_ref, dec_ref,
    out_ref, dec_out,
    mask_ref,
):
    row = iota((BLOCK, LANES), 0)
    lane = iota((BLOCK, LANES), 1)
    dec_out[...] = dec_ref[...]

    @pl.when(pl.program_id(0) == 0)
    def _():
        inside = (lane > row) & (lane - BLOCK >= srel_ref[...])
        mask_ref[...] = jnp.where(inside, 1.0, 0.0).astype(bf16)

    def body(j):
        out_ref[:, tile(j)] = band_sum(j, x_ref, taps_ref, mask_ref, acc_ref[:, tile(j)])

    for_tiles(CHUNK, body)


def make_earlier(before, med, srel, acc, dec):
    width = acc.shape[1]
    shape = jax.ShapeDtypeStruct
    return pl.pallas_call(
        earlier_kernel,
        grid=(width // WIDE,),
        out_shape=(
            shape(acc.shape, f32),
            shape(acc.shape, bf16),
        ),
        in_specs=[
            columns(BLOCK),
            rows_of(WIDE // GROUP),
            fixed((BLOCK, LANES)),
            columns(BLOCK),
            columns(BLOCK),
        ],
        out_specs=(columns(BLOCK), columns(BLOCK)),
        scratch_shapes=[pltpu.VMEM((BLOCK, LANES), bf16)],
        compiler_params=params(20),
        name="earlier",
    )(before, *hbm(med, srel, acc, dec))


def totals_kernel(terms_ref, decay_ref, live_ref, out_ref):
    decay = decay_ref[...]
    state = jnp.zeros((8, LANES), f32)
    kept = jnp.ones((8, LANES), f32)
    for b in range(terms_ref.shape[0]):
        factor = live_ref[b : b + 1] * decay
        state = factor * state + terms_ref[b].astype(f32)
        kept = factor * kept
    out_ref[0] = state
    out_ref[1] = kept


def make_totals(terms, decay, live):
    return pl.pallas_call(
        totals_kernel,
        out_shape=jax.ShapeDtypeStruct((2, 8, LANES), f32),
        in_specs=[in_vmem()] * 3,
        out_specs=in_vmem(),
        compiler_params=params(),
        name="totals",
    )(terms, decay, live)


def states_kernel(terms_ref, decay_ref, live_ref, one_ref, two_ref, out_ref):
    decay = decay_ref[...]
    state = one_ref[0] + one_ref[1] * two_ref[0]
    for b in range(terms_ref.shape[0]):
        out_ref[b] = state.astype(bf16)
        state = live_ref[b : b + 1] * decay * state + terms_ref[b].astype(f32)


def make_states(terms, decay, live, one, two):
    return pl.pallas_call(
        states_kernel,
        out_shape=pltpu.HBM(terms.shape, bf16),
        in_specs=[in_vmem()] * 5,
        out_specs=in_vmem(),
        compiler_params=params(),
        name="states",
    )(terms, decay, live, one, two)


def final_kernel(
    acc_ref, query_hbm, dec_ref, state_ref, out_hbm,
    query_ref, filtered_ref, out_ref, sems,
):
    width = acc_ref.shape[1]
    chunks = width // WIDE

    def span(c):
        return pl.ds(pl.multiple_of(c * WIDE, LANES), WIDE)

    def fetch(c):
        return pltpu.make_async_copy(
            query_hbm.at[:, span(c)], query_ref.at[:, span(c)], sems.at[0, c]
        )

    def send(c):
        return pltpu.make_async_copy(
            out_ref.at[:, span(c)], out_hbm.at[:, span(c)], sems.at[1, c]
        )

    for c in range(chunks):
        fetch(c).start()
    same = iota((LANES, LANES), 0) // MODES == iota((LANES, LANES), 1) // GROUP
    keep = jnp.where(same, 1.0, 0.0).astype(bf16)

    def carry_in(j):
        one = jnp.concatenate([state_ref[0, j], state_ref[1, j]], axis=0)
        spread = jnp.concatenate([one] * PER_TILE, axis=0) * keep
        carried = jnp.dot(dec_ref[:, tile(j)], spread, preferred_element_type=f32)
        filtered_ref[:, tile(j)] = (acc_ref[:, tile(j)] + carried).astype(bf16)

    for_tiles(width // LANES, carry_in)

    def chunk(c, carry):
        fetch(c).wait()

        def inner(i, more):
            at = tile(c * CHUNK + i)
            filtered = filtered_ref[:, at].astype(f32)
            out_ref[:, at] = (query_ref[:, at] * filtered).astype(bf16)
            return more

        lax.fori_loop(0, CHUNK, inner, 0)
        send(c).start()
        return carry

    lax.fori_loop(0, chunks, chunk, 0)
    for c in range(chunks):
        send(c).wait()


def make_final(acc, query, dec, state):
    chunks = acc.shape[1] // WIDE
    return pl.pallas_call(
        final_kernel,
        out_shape=pltpu.HBM(acc.shape, bf16),
        in_specs=[in_vmem(), in_hbm(), in_vmem(), in_vmem()],
        out_specs=in_hbm(),
        scratch_shapes=[
            pltpu.VMEM(acc.shape, f32),
            pltpu.VMEM(acc.shape, bf16),
            pltpu.VMEM(acc.shape, bf16),
            pltpu.SemaphoreType.DMA((2, chunks)),
        ],
        compiler_params=params(),
        name="final",
    )(acc, *hbm(query), dec, state)


def per_device(projected, doc_lengths, short_taps, medium_taps, decay_rates, residues, skip_gain):
    ts_count = lax.axis_size("ts")
    ctx_count = lax.axis_size("ctx")
    count = ts_count * ctx_count
    ctx = lax.axis_index("ctx")
    index = ctx * ts_count + lax.axis_index("ts")
    size = SPAN * ts_count
    which = (index % size).astype(i32)
    groups = [[s * size + j for j in range(size)] for s in range(count // size)]
    onward = [(i, i + 1) for i in range(count - 1)]
    width = projected.shape[1] // 3

    def from_ctx(value, by):
        return lax.ppermute(value, "ctx", [(i, i + by) for i in range(ctx_count - by)])

    halo = lax.ppermute(projected[BLOCK - 8 :], FLAT, onward)
    place = jnp.stack([index * BLOCK, (index - which) * BLOCK]).astype(i32)
    srel, live, tapsx, tail, main, head = make_front(
        place, doc_lengths, short_taps, decay_rates, projected
    )
    product, contrib, edge, tapsq, srel, live = make_edge(
        main, head, halo, tapsx, srel, live, tail
    )
    before = lax.ppermute(product, FLAT, onward)
    items = contrib.reshape(size, 8, LANES)
    terms = lax.all_to_all(
        items, FLAT, split_axis=0, concat_axis=0, tiled=True, axis_index_groups=groups
    )
    scaled = residues * jnp.sqrt(-jnp.expm1(-2.0 * decay_rates))
    dec, own, med, ratesx = make_tables(srel, decay_rates, scaled, medium_taps, width)
    query, acc, decay, near = make_own(
        which.reshape(1), projected, edge, tapsq, srel, product, own,
        skip_gain.reshape(1, -1), ratesx, live,
    )
    totals = make_totals(terms, decay, near)
    one = from_ctx(totals, SPAN)
    two = from_ctx(totals, 2 * SPAN)
    states = make_states(terms, decay, near, one, two)
    back = lax.all_to_all(
        states, FLAT, split_axis=0, concat_axis=0, tiled=True, axis_index_groups=groups
    )
    acc, dec = make_earlier(before, med, srel, acc, dec)
    return make_final(acc, query, dec, back.reshape(2, width // LANES, 8, LANES))


def solution(mesh):
    return jax.shard_map(
        per_device,
        mesh=mesh,
        in_specs=(P(FLAT, None), P(), P(), P(), P(), P(), P()),
        out_specs=P(FLAT, None),
        check_vma=False,
    )
```

time: 113 us -> 84.3 us (0.75)
  blocking collectives: 23.9 us -> 0 us
  starting transfers between devices: 25 us -> 40.5 us
  Pallas kernels: 52.8 us -> 37.9 us
  local copies, waits for them, and re-layouts: 8.76 us -> 3.14 us
    all_to_all x1 -> x0, blocking collectives: 23.9 us -> none  [per_device(): lax.all_to_all(items, FLAT, split_axis=0, concat_axis=0, tiled=True, axis...]
    pallas_call x6 -> x7, Pallas kernels: 52.7 us -> 37.8 us  [the longest x1 9.69 us: make_own(): pl.pallas_call(own_kernel, out_shape=(pltpu.HBM((BLOCK, width), f32), plt...]
    all_to_all x0 -> x1, starting transfers between devices: none -> 13.5 us  [per_device(): lax.all_to_all(items, FLAT, split_axis=0, concat_axis=0, tiled=True, axis...]
    unnamed x16 -> x8, local copies, waits for them, and re-layouts: 7.82 us -> 2.2 us
    all_to_all x1, starting transfers between devices: 8.08 us -> 11.9 us  [per_device(): lax.all_to_all(states, FLAT, split_axis=0, concat_axis=0, tiled=True, axi...]
    ppermute x2, starting transfers between devices: 9.63 us -> 7.86 us  [from_ctx(): lax.ppermute(value, 'ctx', [(i, i + by) for i in range(ctx_count - by)])]
  transfers between devices with their start and end apart: 5 -> 6, of which waited for: 1 -> 2; matrix products, arithmetic and copies ran while one was open for 1% -> 1% of each run, Pallas kernels for 35% -> 38%
where the time goes in v3:
time: 84.3 us; the launch traced here: 83.6 us
  starting transfers between devices  40.5 us (48%)
  Pallas kernels  37.9 us (45%)
  local copies, waits for them, and re-layouts  3.14 us (4%)
  waiting for transfers between devices  1.14 us (1%)
    all_to_all x1, starting transfers between devices, per_device(): lax.all_to_all(items, FLAT, split_axis=0, concat_axis=0, tiled=True, axis...  13.5 us
    all_to_all x1, starting transfers between devices, per_device(): lax.all_to_all(states, FLAT, split_axis=0, concat_axis=0, tiled=True, axi...  11.9 us
    pallas_call x1, Pallas kernels, make_own(): pl.pallas_call(own_kernel, out_shape=(pltpu.HBM((BLOCK, width), f32), plt...  9.69 us
    ppermute x2, starting transfers between devices, from_ctx(): lax.ppermute(value, 'ctx', [(i, i + by) for i in range(ctx_count - by)])  7.86 us
    pallas_call x1, Pallas kernels, make_front(): pl.pallas_call(front_kernel, grid=(1,), out_shape=(shape((BLOCK, LANES),...  7.66 us
    pallas_call x1, Pallas kernels, make_earlier(): pl.pallas_call(earlier_kernel, grid=(width // WIDE,), out_shape=(shape(ac...  7.47 us
    pallas_call x1, Pallas kernels, make_tables(): pl.pallas_call(tables_kernel, grid=(1,), out_shape=(pltpu.HBM((BLOCK, wid...  5.74 us
    ppermute x1, starting transfers between devices, per_device(): halo = lax.ppermute(projected[BLOCK - 8:], FLAT, onward)  5.38 us
  transfers between devices with their start and end apart: 6, of which 2 were waited for; matrix products, arithmetic and copies ran while one was open for 1% of the time, Pallas kernels for 38%

profile of v3, /device:TPU:1, one launch (start us, length us, event | category | flops | bytes accessed | tf_op | source)
XLA Modules:
  0.0 83.6 jit_solution(12088586465347066933)
XLA Ops:
  0.0 0.9 %slice.3 = bf16[8,12288]{1,0:T(8,128)(2,1)S(1)} slice(bf16[128,12288]{1,0:T(8,128)(2,1)} %q_ref.1), slice={[120:128], [0:12288]} | slice | bytes 393216 | tf_op jit(solution)/shard_map/slice | solution.py:647
  0.9 5.4 %collective-permute-start = (bf16[8,12288]{1,0:T(8,128)(2,1)S(1)}, bf16[8,12288]{1,0:T(8,128)(2,1)S(1)}, u32[]{:S(2)}, u32[]{:S(2)}) collective-permute-start(bf16[8,12288]{1,0:T(8,128)(2,1)S(1)} %slice.3), channel_id=1, source_target_pairs={{0,1},{1,2},{2,3},{3,4},{4,5},{5,6},{6,7},{7,8},{8,9},{9,10},{10,1... | collective-permute-start | bytes 589832 | tf_op jit(solution)/shard_map/ppermute | solution.py:647
  6.3 0.1 pad_add_fusion.place_ref
  6.4 7.7 %front.1 = (s32[128,128]{1,0:T(8,128)S(1)}, f32[64,128]{1,0:T(8,128)S(1)}, f32[24,4096]{1,0:T(8,128)S(1)}, bf16[4096,128]{1,0:T(8,128)(2,1)S(1)}, bf16[128,4096]...) custom-call(s32[2]{0:T(128)S(1)} %pad_add_fusion.place_ref, s32[16]{0:T(128)} %docs_ref.1, f32[3,7,256]{2,1,0:T(8,128)} %taps_ref.1, ...), custom_call_target="tpu_custom_call" | custom-call | tf_op jit(solution)/shard_map/front/pallas_call | solution.py:159
  14.1 0.0 copy-start.2
  14.1 0.0 copy-start.3
  14.1 0.0 collective-permute-done.halo_ref
  14.1 3.3 %edge.1 = (bf16[128,4096]{1,0:T(8,128)(2,1)}, bf16[2,32,8,128]{3,2,1,0:T(8,128)(2,1)}, bf16[8,4096]{1,0:T(8,128)(2,1)}, f32[8,4096]{1,0:T(8,128)}, s32[128,128]{1,0:T(8,128)}, /*index=5*/f32[64,128]{1,0:T(8,128)}) custom-call(bf16[128,4096]{1,0:T(8,128)(2,1)S(1)} %get-tuple-element.27.main_ref, bf16[2,8,4096]{2,1,0:T(8,128)(2,1)S(1)} %get-tuple-element.28.head_ref, ...), custom_call_target="tpu_custom_call" | custom-call | tf_op jit(solution)/shard_map/edge/pallas_call | solution.py:266
  17.5 1.9 %collective-permute-start.1 = (bf16[128,4096]{1,0:T(8,128)(2,1)}, bf16[128,4096]{1,0:T(8,128)(2,1)S(1)}, u32[]{:S(2)}, u32[]{:S(2)}) collective-permute-start(bf16[128,4096]{1,0:T(8,128)(2,1)} %get-tuple-element.33.x_ref), channel_id=1, source_target_pairs={{0,1},{1,2},{2,3},{3,4},{4,5},{5,6},{6,7},{7,8},{8,9},{9,10},{10,1... | collective-permute-start | bytes 3145736 | tf_op jit(solution)/shard_map/ppermute | solution.py:655
  19.4 13.5 %all-to-all-start = ((bf16[64,8,128]{2,1,0:T(8,128)(2,1)}), bf16[64,8,128]{2,1,0:T(8,128)(2,1)S(1)}, u32[]{:S(2)}, u32[]{:S(2)}) async-start(bf16[64,8,128]{2,1,0:T(8,128)(2,1)} %bitcast.7), calls=%async_computation | async-start | bytes 262144 | tf_op jit(solution)/shard_map/all_to_all | solution.py:657
  32.9 0.0 copy-done.2
  32.9 0.0 copy-done.3
  32.9 0.6 sqrt_multiply_fusion.scaled_ref
  33.6 5.7 %tables.1 = (bf16[128,4096]{1,0:T(8,128)(2,1)}, f32[256,128]{1,0:T(8,128)S(1)}, f32[256,128]{1,0:T(8,128)}, f32[16,4096]{1,0:T(8,128)S(1)}) custom-call(s32[128,128]{1,0:T(8,128)} %get-tuple-element.34.srel_ref, f32[16,256]{1,0:T(8,128)} %rates_ref.3, f32[16,256]{1,0:T(8,128)} %sqrt_multiply_fusion.scaled_ref, f32[128,256]{1,0:T(8,128)} %medium_ref.1), custom_call_target="tpu_custom_call" | custom-call | tf_op jit(solution)/shard_map/tables/pallas_call | solution.py:340
  39.3 9.7 %own.1 = (f32[128,4096]{1,0:T(8,128)}, f32[128,4096]{1,0:T(8,128)}, f32[8,128]{1,0:T(8,128)S(1)}, f32[64,128]{1,0:T(8,128)S(1)}) custom-call(s32[1]{0:T(128)} %bitcast.2.which_ref, bf16[128,12288]{1,0:T(8,128)(2,1)} %q_ref.1, bf16[8,4096]{1,0:T(8,128)(2,1)} %get-tuple-element.36.hq_ref, f32[8,4096]{1,0:T(8,128)} %get-tuple-element.37.taps_ref, ...), custom_call_target="tpu_custom_call" | custom-call | tf_op jit(solution)/shard_map/own/pallas_call | solution.py:439
  49.0 0.0 all-to-all-done.terms_ref
  49.0 0.1 totals.1
  49.1 4.7 %collective-permute-start.2 = (f32[2,8,128]{2,1,0:T(8,128)S(1)}, f32[2,8,128]{2,1,0:T(8,128)S(1)}, u32[]{:S(2)}, u32[]{:S(2)}) collective-permute-start(f32[2,8,128]{2,1,0:T(8,128)S(1)} %totals.1), channel_id=1, source_target_pairs={{0,64},{16,80},{32,96},{48,112},{64,128},{80,144},{96,160},{112,17... | collective-permute-start | bytes 24584 | tf_op jit(solution)/shard_map/ppermute | solution.py:645
  53.9 3.1 %collective-permute-start.3 = (f32[2,8,128]{2,1,0:T(8,128)S(1)}, f32[2,8,128]{2,1,0:T(8,128)S(1)}, u32[]{:S(2)}, u32[]{:S(2)}) collective-permute-start(f32[2,8,128]{2,1,0:T(8,128)S(1)} %totals.1), channel_id=1, source_target_pairs={{0,128},{16,144},{32,160},{48,176},{64,192},{80,208},{96,224},{112... | collective-permute-start | bytes 24584 | tf_op jit(solution)/shard_map/ppermute | solution.py:645
  57.0 0.0 collective-permute-done.2.one_ref
  57.0 0.8 collective-permute-done.3.two_ref
  57.8 0.8 states.1
  58.6 11.9 %all-to-all-start.1 = ((bf16[64,8,128]{2,1,0:T(8,128)(2,1)}), bf16[64,8,128]{2,1,0:T(8,128)(2,1)S(1)}, u32[]{:S(2)}, u32[]{:S(2)}) async-start(bf16[64,8,128]{2,1,0:T(8,128)(2,1)} %states.1), calls=%async_computation.1 | async-start | bytes 262144 | tf_op jit(solution)/shard_map/all_to_all | solution.py:670
  70.5 0.0 collective-permute-done.1.x_ref
  70.5 0.0 copy-start
  70.5 1.0 %copy-done = bf16[128,4096]{1,0:T(8,128)(2,1)} copy-done((bf16[128,4096]{1,0:T(8,128)(2,1)}, bf16[128,4096]{1,0:T(8,128)(2,1)S(1)}, u32[]{:S(2)}) %copy-start) | copy-done | bytes 1048600
  71.5 0.0 copy-start.1
  71.5 1.2 %copy-done.1 = bf16[128,4096]{1,0:T(8,128)(2,1)S(1)} copy-done((bf16[128,4096]{1,0:T(8,128)(2,1)S(1)}, bf16[128,4096]{1,0:T(8,128)(2,1)}, u32[]{:S(2)}) %copy-start.1) | copy-done | bytes 1048600
  72.7 7.5 %earlier.1 = (f32[128,4096]{1,0:T(8,128)S(1)}, bf16[128,4096]{1,0:T(8,128)(2,1)S(1)}) custom-call(bf16[128,4096]{1,0:T(8,128)(2,1)S(1)} %copy-done.1, f32[256,128]{1,0:T(8,128)} %get-tuple-element.35.taps_ref, s32[128,128]{1,0:T(8,128)} %get-tuple-element.34.srel_ref, f32[128,4096]{1,0:T(8,128)} %get-tuple-element.41.acc_ref, ...), custom_call_target="tpu_custom_call" | custom-call | tf_op jit(solution)/shard_map/earlier/pallas_call | solution.py:500
  80.2 0.4 all-to-all-done.1
  80.5 3.0 %final.1 = bf16[128,4096]{1,0:T(8,128)(2,1)} custom-call(f32[128,4096]{1,0:T(8,128)S(1)} %get-tuple-element.43.acc_ref, f32[128,4096]{1,0:T(8,128)} %get-tuple-element.44.query_hbm, bf16[128,4096]{1,0:T(8,128)(2,1)S(1)} %get-tuple-element.45.dec_ref, bf16[2,32,8,128]{3,2,1,0:T(8,128)(2,1)S(1)} %bitcast.6), custom_call_target="tpu_custom_call" | custom-call | tf_op jit(solution)/shard_map/final/pallas_call | solution.py:616
Async XLA Ops:
  0.9 13.2 %collective-permute-start = (bf16[8,12288]{1,0:T(8,128)(2,1)S(1)}, bf16[8,12288]{1,0:T(8,128)(2,1)S(1)}, u32[]{:S(2)}, u32[]{:S(2)}) collective-permute-start(bf16[8,12288]{1,0:T(8,128)(2,1)S(1)} %slice.3), channel_id=1, source_target_pairs={{0,1},{1,2},{2,3},{3,4},{4,5},{5,6},{6,7},{7,8},{8,9},{9,10},{10,1... | collective-permute-start | bytes 589832 | tf_op jit(solution)/shard_map/ppermute | solution.py:647
  14.1 18.8 %copy-start.2 = (f32[16,256]{1,0:T(8,128)S(1)}, f32[16,256]{1,0:T(8,128)}, u32[]{:S(2)}) copy-start(f32[16,256]{1,0:T(8,128)} %rates_ref.3) | copy-start | bytes 49156
  14.1 18.8 %copy-start.3 = (f32[16,256]{1,0:T(8,128)S(1)}, f32[16,256]{1,0:T(8,128)}, u32[]{:S(2)}) copy-start(f32[16,256]{1,0:T(8,128)} %param.12) | copy-start | bytes 49156
  17.5 53.0 %collective-permute-start.1 = (bf16[128,4096]{1,0:T(8,128)(2,1)}, bf16[128,4096]{1,0:T(8,128)(2,1)S(1)}, u32[]{:S(2)}, u32[]{:S(2)}) collective-permute-start(bf16[128,4096]{1,0:T(8,128)(2,1)} %get-tuple-element.33.x_ref), channel_id=1, source_target_pairs={{0,1},{1,2},{2,3},{3,4},{4,5},{5,6},{6,7},{7,8},{8,9},{9,10},{10,1... | collective-permute-start | bytes 3145736 | tf_op jit(solution)/shard_map/ppermute | solution.py:655
  19.4 29.6 %all-to-all-start = ((bf16[64,8,128]{2,1,0:T(8,128)(2,1)}), bf16[64,8,128]{2,1,0:T(8,128)(2,1)S(1)}, u32[]{:S(2)}, u32[]{:S(2)}) async-start(bf16[64,8,128]{2,1,0:T(8,128)(2,1)} %bitcast.7), calls=%async_computation | async-start | bytes 262144 | tf_op jit(solution)/shard_map/all_to_all | solution.py:657
  49.1 7.9 %collective-permute-start.2 = (f32[2,8,128]{2,1,0:T(8,128)S(1)}, f32[2,8,128]{2,1,0:T(8,128)S(1)}, u32[]{:S(2)}, u32[]{:S(2)}) collective-permute-start(f32[2,8,128]{2,1,0:T(8,128)S(1)} %totals.1), channel_id=1, source_target_pairs={{0,64},{16,80},{32,96},{48,112},{64,128},{80,144},{96,160},{112,17... | collective-permute-start | bytes 24584 | tf_op jit(solution)/shard_map/ppermute | solution.py:645
  53.9 3.9 %collective-permute-start.3 = (f32[2,8,128]{2,1,0:T(8,128)S(1)}, f32[2,8,128]{2,1,0:T(8,128)S(1)}, u32[]{:S(2)}, u32[]{:S(2)}) collective-permute-start(f32[2,8,128]{2,1,0:T(8,128)S(1)} %totals.1), channel_id=1, source_target_pairs={{0,128},{16,144},{32,160},{48,176},{64,192},{80,208},{96,224},{112... | collective-permute-start | bytes 24584 | tf_op jit(solution)/shard_map/ppermute | solution.py:645
  58.6 21.9 %all-to-all-start.1 = ((bf16[64,8,128]{2,1,0:T(8,128)(2,1)}), bf16[64,8,128]{2,1,0:T(8,128)(2,1)S(1)}, u32[]{:S(2)}, u32[]{:S(2)}) async-start(bf16[64,8,128]{2,1,0:T(8,128)(2,1)} %states.1), calls=%async_computation.1 | async-start | bytes 262144 | tf_op jit(solution)/shard_map/all_to_all | solution.py:670
  70.5 1.0 %copy-start = (bf16[128,4096]{1,0:T(8,128)(2,1)}, bf16[128,4096]{1,0:T(8,128)(2,1)S(1)}, u32[]{:S(2)}) copy-start(bf16[128,4096]{1,0:T(8,128)(2,1)S(1)} %collective-permute-done.1.x_ref) | copy-start | bytes 3145732
  71.5 1.2 %copy-start.1 = (bf16[128,4096]{1,0:T(8,128)(2,1)S(1)}, bf16[128,4096]{1,0:T(8,128)(2,1)}, u32[]{:S(2)}) copy-start(bf16[128,4096]{1,0:T(8,128)(2,1)} %copy-done) | copy-start | bytes 3145732

commit v4 on v3

--- a/solution.py
+++ b/solution.py
@@ -11,7 +11,9 @@
 MODES = 16
 LANES = 128
 DOCS = 16
-SPAN = 4
+SPAN = 8
+PARTS = 4
+PART = MODES // PARTS
 PER_TILE = LANES // GROUP
 FLAT = ("ctx", "ts")
 HIGHEST = lax.Precision.HIGHEST
@@ -26,6 +28,7 @@
 
 TILES = 4
 CHUNK = 8
+ROWS = 32
 WIDE = CHUNK * LANES
 
 
@@ -35,13 +38,13 @@
     return pl.ds(pl.multiple_of(j * LANES, LANES), LANES)
 
 
-def for_tiles(count, body):
+def for_tiles(count, body, unroll=TILES):
     def step(i, carry):
-        for j in range(TILES):
-            body(i * TILES + j)
+        for k in range(unroll):
+            body(i * unroll + k, k)
         return carry
 
-    lax.fori_loop(0, count // TILES, step, 0)
+    lax.fori_loop(0, count // unroll, step, 0)
 
 
 def in_hbm():
@@ -79,7 +82,7 @@
 def front_kernel(
     place_ref, docs_ref, taps_ref, rates_ref, raw_ref,
     srel_ref, live_ref, tapsx_ref, tail_ref, product_ref, head_ref,
-    stack_ref, pieces_ref, raws_ref, wk_ref, wv_ref, sems,
+    stack_ref, pieces_ref, raws_ref, wk_ref, wv_ref, rel_ref, near_ref, sems,
 ):
     width = product_ref.shape[1]
     copies = [
@@ -111,7 +114,7 @@
     own_mode = iota((MODES, LANES), 0) == iota((MODES, LANES), 1) % MODES
     behind = (BLOCK - 1 - row).astype(f32)
 
-    def expand(j):
+    def expand(j, k):
         spread = expanded(pieces_ref, j)
         tapsx_ref[:, tile(j)] = spread[0:24]
         rate = jnp.sum(jnp.where(own_mode, spread[24:40], 0.0), axis=0, keepdims=True)
@@ -120,16 +123,24 @@
     for_tiles(width // LANES, expand)
     for copy in copies:
         copy.wait()
-    rel = row - (starts - base)
+    rel_ref[...] = row - (starts - base)
     nothing = jnp.zeros((8, LANES), f32)
 
-    def multiply(j):
-        slot = lax.rem(j, TILES)
-        key = feature_of(raws_ref.at[0], nothing, tapsx_ref, 1, j, rel, wk_ref.at[slot])
-        value = feature_of(raws_ref.at[1], nothing, tapsx_ref, 2, j, rel, wv_ref.at[slot])
-        product_ref[:, tile(j)] = (key * value).astype(bf16)
-
-    for_tiles(width // LANES, multiply)
+    def rows_of_product(at, masked):
+        rows = slice(at, at + ROWS)
+
+        def multiply(j, k):
+            key = feature_of(
+                raws_ref.at[0], nothing, tapsx_ref, 1, j, at, rel_ref, wk_ref.at[k], masked
+            )
+            value = feature_of(
+                raws_ref.at[1], nothing, tapsx_ref, 2, j, at, rel_ref, wv_ref.at[k], masked
+            )
+            product_ref[rows, tile(j)] = (key * value).astype(bf16)
+
+        for_tiles(width // LANES, multiply)
+
+    in_row_parts(rel_ref, near_ref, rows_of_product)
     head_ref[0] = raws_ref[0, 0:8]
     head_ref[1] = raws_ref[1, 0:8]
 
@@ -152,7 +163,7 @@
     return spread[0:lines] + spread[lines : 2 * lines] + spread[2 * lines :]
 
 
-def make_front(place, doc_lengths, short_taps, decay_rates, projected):
+def make_front(place, doc_lengths, short_taps, decay_rates, projected, size):
     width = projected.shape[1] // 3
     groups = decay_rates.shape[1]
     shape = jax.ShapeDtypeStruct
@@ -161,7 +172,7 @@
         grid=(1,),
         out_shape=(
             shape((BLOCK, LANES), i32),
-            shape((4 * DOCS, LANES), f32),
+            shape((size, LANES), f32),
             shape((24, width), f32),
             shape((width, BLOCK), bf16),
             shape((BLOCK, width), bf16),
@@ -179,8 +190,10 @@
             pltpu.VMEM((48, groups), f32),
             pltpu.VMEM((3, 48, groups), bf16),
             pltpu.VMEM((2, BLOCK, width), bf16),
-            pltpu.VMEM((TILES, 8 + BLOCK, LANES), f32),
-            pltpu.VMEM((TILES, 8 + BLOCK, LANES), f32),
+            pltpu.VMEM((TILES, 8 + ROWS, LANES), f32),
+            pltpu.VMEM((TILES, 8 + ROWS, LANES), f32),
+            pltpu.VMEM((BLOCK, LANES), i32),
+            pltpu.SMEM((BLOCK // ROWS,), i32),
             pltpu.SemaphoreType.DMA((2,)),
         ],
         compiler_params=params(),
@@ -203,8 +216,7 @@
     srel_out[...] = srel_ref[...]
     live_out[...] = live_ref[...]
 
-    def body(j):
-        slot = lax.rem(j, TILES)
+    def body(j, slot):
         values = []
         for p in range(2):
             past = halo_ref[:, tile(j + (1 + p) * (width // LANES))].astype(f32)
@@ -231,8 +243,8 @@
             contrib = jnp.where(
                 lane_group == g, all_modes[g * MODES : (g + 1) * MODES], contrib
             )
-        contrib_ref[0, j] = contrib[0:8].astype(bf16)
-        contrib_ref[1, j] = contrib[8:16].astype(bf16)
+        for p in range(PARTS):
+            contrib_ref[p, j] = contrib[p * PART : (p + 1) * PART].astype(bf16)
 
     def copies(c):
         at = pl.ds(pl.multiple_of(c * WIDE, LANES), WIDE)
@@ -245,7 +257,7 @@
     def chunk(c, carry):
         def inner(i, more):
             for k in range(TILES):
-                body(c * CHUNK + i * TILES + k)
+                body(c * CHUNK + i * TILES + k, k)
             return more
 
         lax.fori_loop(0, CHUNK // TILES, inner, 0)
@@ -267,7 +279,7 @@
         edge_kernel,
         out_shape=(
             shape((BLOCK, width), bf16),
-            shape((2, width // LANES, 8, LANES), bf16),
+            shape((PARTS, width // LANES, PART, LANES), bf16),
             shape((8, width), bf16),
             shape((8, width), f32),
             shape(srel.shape, i32),
@@ -278,7 +290,7 @@
         scratch_shapes=[
             pltpu.VMEM((TILES, 2, 16, LANES), f32),
             pltpu.VMEM((BLOCK, width), bf16),
-            pltpu.VMEM((2, width // LANES, 8, LANES), bf16),
+            pltpu.VMEM((PARTS, width // LANES, PART, LANES), bf16),
             pltpu.SemaphoreType.DMA((2, width // WIDE)),
         ],
         compiler_params=params(),
@@ -362,14 +374,36 @@
     )(*hbm(srel, decay_rates, scaled, medium_taps))
 
 
-def feature_of(raw_ref, past, taps_ref, part, j, rel, window_ref):
+def find_near(rel_ref, near_ref):
+    for r in range(BLOCK // ROWS):
+        least = jnp.min(rel_ref[r * ROWS : (r + 1) * ROWS].astype(f32))
+        near_ref[r] = (least < SHORT - 1).astype(i32)
+
+
+def by_rows(near_ref, work):
+    for r in range(BLOCK // ROWS):
+        near = near_ref[r] != 0
+        pl.when(near)(lambda at=r * ROWS: work(at, True))
+        pl.when(jnp.logical_not(near))(lambda at=r * ROWS: work(at, False))
+
+
+def in_row_parts(rel_ref, near_ref, work):
+    find_near(rel_ref, near_ref)
+    by_rows(near_ref, work)
+
+
+def feature_of(raw_ref, past, taps_ref, part, j, at, rel_ref, window_ref, masked):
+    if at:
+        past = raw_ref[at - 16 : at, tile(j)].astype(f32)[8:16]
     window_ref[0:8] = past
-    window_ref[8 : 8 + BLOCK] = raw_ref[:, tile(j)].astype(f32)
-    summed = window_ref[8 : 8 + BLOCK] * taps_ref[8 * part : 8 * part + 1, tile(j)]
+    window_ref[8 : 8 + ROWS] = raw_ref[at : at + ROWS, tile(j)].astype(f32)
+    summed = window_ref[8 : 8 + ROWS] * taps_ref[8 * part : 8 * part + 1, tile(j)]
     for offset in range(1, SHORT):
         tap = taps_ref[8 * part + offset : 8 * part + offset + 1, tile(j)]
-        term = window_ref[8 - offset : 8 - offset + BLOCK] * tap
-        summed = summed + jnp.where(rel >= offset, term, 0.0)
+        term = window_ref[8 - offset : 8 - offset + ROWS] * tap
+        if masked:
+            term = jnp.where(rel_ref[at : at + ROWS] >= offset, term, 0.0)
+        summed = summed + term
     return summed
 
 
@@ -401,27 +435,39 @@
 def own_kernel(
     which_ref, q_ref, hq_ref, taps_ref, srel_ref, x_ref, own_ref, skip_ref, rates_ref, live_ref,
     query_ref, acc_ref, decay_ref, live_out,
-    wq_ref, mask_ref,
+    wq_ref, mask_ref, rel_ref, near_ref,
 ):
     row = iota((BLOCK, LANES), 0)
     lane = iota((BLOCK, LANES), 1)
-    rel = row - srel_ref[...]
 
     @pl.when(pl.program_id(0) == 0)
     def _():
         mask = (lane <= row) & (lane >= srel_ref[...])
         mask_ref[...] = jnp.where(mask, 1.0, 0.0).astype(bf16)
-        decay_ref[...] = jnp.exp(-rates_ref[...] * float(BLOCK))
+        tiles = pl.num_programs(0) * CHUNK
+        upper = lax.rem(which_ref[0] // tiles, 2) == 1
+        rates = jnp.where(upper, rates_ref[PART:8], rates_ref[0:PART])
+        decay_ref[...] = jnp.exp(-rates * float(BLOCK))
         live_out[...] = live_ref[...]
-
-    def body(j):
-        slot = lax.rem(j, TILES)
-        past = hq_ref[:, tile(j)].astype(f32)
-        query_ref[:, tile(j)] = feature_of(q_ref, past, taps_ref, 0, j, rel, wq_ref.at[slot])
+        rel_ref[...] = row - srel_ref[...]
+        find_near(rel_ref, near_ref)
+
+    def rows_of_query(at, masked):
+        def ask(j, k):
+            past = hq_ref[:, tile(j)].astype(f32)
+            query_ref[at : at + ROWS, tile(j)] = feature_of(
+                q_ref, past, taps_ref, 0, j, at, rel_ref, wq_ref.at[k], masked
+            )
+
+        for_tiles(CHUNK, ask, CHUNK)
+
+    by_rows(near_ref, rows_of_query)
+
+    def body(j, k):
         acc = skip_ref[:, tile(j)] * x_ref[:, tile(j)].astype(f32)
         acc_ref[:, tile(j)] = band_sum(j, x_ref, own_ref, mask_ref, acc)
 
-    for_tiles(CHUNK, body)
+    for_tiles(CHUNK, body, CHUNK)
 
 
 def cols(rows, first=0):
@@ -441,7 +487,7 @@
         out_shape=(
             pltpu.HBM((BLOCK, width), f32),
             pltpu.HBM((BLOCK, width), f32),
-            shape((8, LANES), f32),
+            shape((PART, LANES), f32),
             shape(live.shape, f32),
         ),
         grid_spec=pltpu.PrefetchScalarGridSpec(
@@ -455,18 +501,20 @@
                 cols(BLOCK),
                 pl.BlockSpec((WIDE // GROUP, LANES), lambda j, *_: (j, 0)),
                 cols(1),
-                pl.BlockSpec((8, LANES), lambda _, at: (at[0] // tiles, at[0] % tiles)),
+                pl.BlockSpec((8, LANES), lambda _, at: (at[0] // (2 * tiles), at[0] % tiles)),
                 whole(live.shape),
             ],
             out_specs=(
                 cols(BLOCK),
                 cols(BLOCK),
-                whole((8, LANES)),
+                whole((PART, LANES)),
                 whole(live.shape),
             ),
             scratch_shapes=[
-                pltpu.VMEM((TILES, 8 + BLOCK, LANES), f32),
+                pltpu.VMEM((CHUNK, 8 + ROWS, LANES), f32),
                 pltpu.VMEM((BLOCK, LANES), bf16),
+                pltpu.VMEM((BLOCK, LANES), i32),
+                pltpu.SMEM((BLOCK // ROWS,), i32),
             ],
         ),
         compiler_params=params(20),
@@ -488,10 +536,10 @@
         inside = (lane > row) & (lane - BLOCK >= srel_ref[...])
         mask_ref[...] = jnp.where(inside, 1.0, 0.0).astype(bf16)
 
-    def body(j):
+    def body(j, k):
         out_ref[:, tile(j)] = band_sum(j, x_ref, taps_ref, mask_ref, acc_ref[:, tile(j)])
 
-    for_tiles(CHUNK, body)
+    for_tiles(CHUNK, body, CHUNK)
 
 
 def make_earlier(before, med, srel, acc, dec):
@@ -515,25 +563,21 @@
         scratch_shapes=[pltpu.VMEM((BLOCK, LANES), bf16)],
         compiler_params=params(20),
         name="earlier",
-    )(before, *hbm(med, srel, acc, dec))
+    )(*hbm(before, med, srel, acc, dec))
 
 
 def totals_kernel(terms_ref, decay_ref, live_ref, out_ref):
     decay = decay_ref[...]
-    state = jnp.zeros((8, LANES), f32)
-    kept = jnp.ones((8, LANES), f32)
+    state = jnp.zeros((PART, LANES), f32)
     for b in range(terms_ref.shape[0]):
-        factor = live_ref[b : b + 1] * decay
-        state = factor * state + terms_ref[b].astype(f32)
-        kept = factor * kept
-    out_ref[0] = state
-    out_ref[1] = kept
+        state = live_ref[b : b + 1] * decay * state + terms_ref[b].astype(f32)
+    out_ref[...] = state
 
 
 def make_totals(terms, decay, live):
     return pl.pallas_call(
         totals_kernel,
-        out_shape=jax.ShapeDtypeStruct((2, 8, LANES), f32),
+        out_shape=jax.ShapeDtypeStruct((PART, LANES), f32),
         in_specs=[in_vmem()] * 3,
         out_specs=in_vmem(),
         compiler_params=params(),
@@ -541,23 +585,23 @@
     )(terms, decay, live)
 
 
-def states_kernel(terms_ref, decay_ref, live_ref, one_ref, two_ref, out_ref):
+def states_kernel(terms_ref, decay_ref, live_ref, enter_ref, out_ref):
     decay = decay_ref[...]
-    state = one_ref[0] + one_ref[1] * two_ref[0]
+    state = enter_ref[...]
     for b in range(terms_ref.shape[0]):
         out_ref[b] = state.astype(bf16)
         state = live_ref[b : b + 1] * decay * state + terms_ref[b].astype(f32)
 
 
-def make_states(terms, decay, live, one, two):
+def make_states(terms, decay, live, enter):
     return pl.pallas_call(
         states_kernel,
         out_shape=pltpu.HBM(terms.shape, bf16),
-        in_specs=[in_vmem()] * 5,
+        in_specs=[in_vmem()] * 4,
         out_specs=in_vmem(),
         compiler_params=params(),
         name="states",
-    )(terms, decay, live, one, two)
+    )(terms, decay, live, enter)
 
 
 def final_kernel(
@@ -585,8 +629,9 @@
     same = iota((LANES, LANES), 0) // MODES == iota((LANES, LANES), 1) // GROUP
     keep = jnp.where(same, 1.0, 0.0).astype(bf16)
 
-    def carry_in(j):
-        one = jnp.concatenate([state_ref[0, j], state_ref[1, j]], axis=0)
+    def carry_in(j, k):
+        parts = [state_ref[p, j].astype(f32) for p in range(PARTS)]
+        one = jnp.concatenate(parts, axis=0).astype(bf16)
         spread = jnp.concatenate([one] * PER_TILE, axis=0) * keep
         carried = jnp.dot(dec_ref[:, tile(j)], spread, preferred_element_type=f32)
         filtered_ref[:, tile(j)] = (acc_ref[:, tile(j)] + carried).astype(bf16)
@@ -647,13 +692,13 @@
     halo = lax.ppermute(projected[BLOCK - 8 :], FLAT, onward)
     place = jnp.stack([index * BLOCK, (index - which) * BLOCK]).astype(i32)
     srel, live, tapsx, tail, main, head = make_front(
-        place, doc_lengths, short_taps, decay_rates, projected
+        place, doc_lengths, short_taps, decay_rates, projected, size
     )
     product, contrib, edge, tapsq, srel, live = make_edge(
         main, head, halo, tapsx, srel, live, tail
     )
     before = lax.ppermute(product, FLAT, onward)
-    items = contrib.reshape(size, 8, LANES)
+    items = contrib.reshape(size, PART, LANES)
     terms = lax.all_to_all(
         items, FLAT, split_axis=0, concat_axis=0, tiled=True, axis_index_groups=groups
     )
@@ -664,14 +709,13 @@
         skip_gain.reshape(1, -1), ratesx, live,
     )
     totals = make_totals(terms, decay, near)
-    one = from_ctx(totals, SPAN)
-    two = from_ctx(totals, 2 * SPAN)
-    states = make_states(terms, decay, near, one, two)
+    enter = from_ctx(totals, SPAN)
+    states = make_states(terms, decay, near, enter)
     back = lax.all_to_all(
         states, FLAT, split_axis=0, concat_axis=0, tiled=True, axis_index_groups=groups
     )
     acc, dec = make_earlier(before, med, srel, acc, dec)
-    return make_final(acc, query, dec, back.reshape(2, width // LANES, 8, LANES))
+    return make_final(acc, query, dec, back.reshape(PARTS, width // LANES, PART, LANES))
 
 
 def solution(mesh):

time: 84.3 us -> 85.5 us (1.014)
  waiting for transfers between devices: 1.14 us -> 5.46 us
  Pallas kernels: 37.9 us -> 35.1 us
  local copies, waits for them, and re-layouts: 3.14 us -> 1.92 us
  starting transfers between devices: 40.5 us -> 41.5 us
    ppermute x2 -> x1, starting transfers between devices: 7.86 us -> 3.31 us  [from_ctx(): lax.ppermute(value, 'ctx', [(i, i + by) for i in range(ctx_count - by)])]
    all_to_all x1, waiting for transfers between devices: 0.36 us -> 4.73 us  [per_device(): lax.all_to_all(states, FLAT, split_axis=0, concat_axis=0, tiled=True, axi...]
    all_to_all x1, starting transfers between devices: 13.5 us -> 16.5 us  [per_device(): lax.all_to_all(items, FLAT, split_axis=0, concat_axis=0, tiled=True, axis...]
    all_to_all x1, starting transfers between devices: 11.9 us -> 14.4 us  [per_device(): lax.all_to_all(states, FLAT, split_axis=0, concat_axis=0, tiled=True, axi...]
    pallas_call x1, Pallas kernels: 9.69 us -> 8.4 us  [make_own(): pl.pallas_call(own_kernel, out_shape=(pltpu.HBM((BLOCK, width), f32), plt...]
    unnamed x8 -> x6, local copies, waits for them, and re-layouts: 2.2 us -> 0.98 us
    pallas_call x1, Pallas kernels: 7.66 us -> 6.67 us  [make_front(): pl.pallas_call(front_kernel, grid=(1,), out_shape=(shape((BLOCK, LANES),...]
    pallas_call x1, Pallas kernels: 7.47 us -> 6.54 us  [make_earlier(): pl.pallas_call(earlier_kernel, grid=(width // WIDE,), out_shape=(shape(ac...]
  transfers between devices with their start and end apart: 6 -> 5, of which waited for: 2 -> 2; matrix products, arithmetic and copies ran while one was open for 1% -> 1% of each run, Pallas kernels for 38% -> 34%
where the time goes in v4:
time: 85.5 us; the launch traced here: 84.8 us
  starting transfers between devices  41.5 us (49%)
  Pallas kernels  35.1 us (41%)
  waiting for transfers between devices  5.46 us (6%)
  local copies, waits for them, and re-layouts  1.92 us (2%)
    all_to_all x1, starting transfers between devices, per_device(): lax.all_to_all(items, FLAT, split_axis=0, concat_axis=0, tiled=True, axis...  16.5 us
    all_to_all x1, starting transfers between devices, per_device(): lax.all_to_all(states, FLAT, split_axis=0, concat_axis=0, tiled=True, axi...  14.4 us
    pallas_call x1, Pallas kernels, make_own(): pl.pallas_call(own_kernel, out_shape=(pltpu.HBM((BLOCK, width), f32), plt...  8.4 us
    pallas_call x1, Pallas kernels, make_front(): pl.pallas_call(front_kernel, grid=(1,), out_shape=(shape((BLOCK, LANES),...  6.67 us
    pallas_call x1, Pallas kernels, make_earlier(): pl.pallas_call(earlier_kernel, grid=(width // WIDE,), out_shape=(shape(ac...  6.54 us
    pallas_call x1, Pallas kernels, make_tables(): pl.pallas_call(tables_kernel, grid=(1,), out_shape=(pltpu.HBM((BLOCK, wid...  5.75 us
    ppermute x1, starting transfers between devices, per_device(): halo = lax.ppermute(projected[BLOCK - 8:], FLAT, onward)  5.38 us
    all_to_all x1, waiting for transfers between devices, per_device(): lax.all_to_all(states, FLAT, split_axis=0, concat_axis=0, tiled=True, axi...  4.73 us
  transfers between devices with their start and end apart: 5, of which 2 were waited for; matrix products, arithmetic and copies ran while one was open for 1% of the time, Pallas kernels for 34%

profile of v4, /device:TPU:1, one launch (start us, length us, event | category | flops | bytes accessed | tf_op | source)
XLA Modules:
  0.0 84.8 jit_solution(10498651248668602035)
XLA Ops:
  0.0 0.9 %slice.3 = bf16[8,12288]{1,0:T(8,128)(2,1)S(1)} slice(bf16[128,12288]{1,0:T(8,128)(2,1)} %q_ref.1), slice={[120:128], [0:12288]} | slice | bytes 393216 | tf_op jit(solution)/shard_map/slice | solution.py:692
  0.9 5.4 %collective-permute-start = (bf16[8,12288]{1,0:T(8,128)(2,1)S(1)}, bf16[8,12288]{1,0:T(8,128)(2,1)S(1)}, u32[]{:S(2)}, u32[]{:S(2)}) collective-permute-start(bf16[8,12288]{1,0:T(8,128)(2,1)S(1)} %slice.3), channel_id=1, source_target_pairs={{0,1},{1,2},{2,3},{3,4},{4,5},{5,6},{6,7},{7,8},{8,9},{9,10},{10,1... | collective-permute-start | bytes 589832 | tf_op jit(solution)/shard_map/ppermute | solution.py:692
  6.3 0.1 pad_add_fusion.place_ref
  6.4 6.7 %front.1 = (s32[128,128]{1,0:T(8,128)S(1)}, f32[128,128]{1,0:T(8,128)S(1)}, f32[24,4096]{1,0:T(8,128)S(1)}, bf16[4096,128]{1,0:T(8,128)(2,1)S(1)}, bf16[128,4096...) custom-call(s32[2]{0:T(128)S(1)} %pad_add_fusion.place_ref, s32[16]{0:T(128)} %docs_ref.1, f32[3,7,256]{2,1,0:T(8,128)} %taps_ref.1, ...), custom_call_target="tpu_custom_call" | custom-call | tf_op jit(solution)/shard_map/front/pallas_call | solution.py:170
  13.1 0.0 copy-start.1
  13.1 0.0 copy-start.2
  13.1 0.0 collective-permute-done.halo_ref
  13.1 3.4 %edge.1 = (bf16[128,4096]{1,0:T(8,128)(2,1)}, bf16[4,32,4,128]{3,2,1,0:T(4,128)(2,1)}, bf16[8,4096]{1,0:T(8,128)(2,1)}, f32[8,4096]{1,0:T(8,128)}, s32[128,128]{1,0:T(8,128)}, /*index=5*/f32[128,128]{1,0:T(8,128)}) custom-call(bf16[128,4096]{1,0:T(8,128)(2,1)S(1)} %get-tuple-element.27.main_ref, bf16[2,8,4096]{2,1,0:T(8,128)(2,1)S(1)} %get-tuple-element.28.head_ref, ...), custom_call_target="tpu_custom_call" | custom-call | tf_op jit(solution)/shard_map/edge/pallas_call | solution.py:278
  16.6 1.9 %collective-permute-start.1 = (bf16[128,4096]{1,0:T(8,128)(2,1)}, bf16[128,4096]{1,0:T(8,128)(2,1)S(1)}, u32[]{:S(2)}, u32[]{:S(2)}) collective-permute-start(bf16[128,4096]{1,0:T(8,128)(2,1)} %get-tuple-element.33.x_ref), channel_id=1, source_target_pairs={{0,1},{1,2},{2,3},{3,4},{4,5},{5,6},{6,7},{7,8},{8,9},{9,10},{10,1... | collective-permute-start | bytes 3145736 | tf_op jit(solution)/shard_map/ppermute | solution.py:700
  18.5 16.5 %all-to-all-start = ((bf16[128,4,128]{2,1,0:T(4,128)(2,1)}), bf16[128,4,128]{2,1,0:T(4,128)(2,1)S(1)}, u32[]{:S(2)}, u32[]{:S(2)}) async-start(bf16[128,4,128]{2,1,0:T(4,128)(2,1)} %bitcast.7), calls=%async_computation | async-start | bytes 262144 | tf_op jit(solution)/shard_map/all_to_all | solution.py:702
  35.0 0.0 copy-done.1
  35.0 0.0 copy-done.2
  35.0 0.6 sqrt_multiply_fusion.scaled_ref
  35.7 5.7 %tables.1 = (bf16[128,4096]{1,0:T(8,128)(2,1)}, f32[256,128]{1,0:T(8,128)S(1)}, f32[256,128]{1,0:T(8,128)}, f32[16,4096]{1,0:T(8,128)S(1)}) custom-call(s32[128,128]{1,0:T(8,128)} %get-tuple-element.34.srel_ref, f32[16,256]{1,0:T(8,128)} %rates_ref.3, f32[16,256]{1,0:T(8,128)} %sqrt_multiply_fusion.scaled_ref, f32[128,256]{1,0:T(8,128)} %medium_ref.1), custom_call_target="tpu_custom_call" | custom-call | tf_op jit(solution)/shard_map/tables/pallas_call | solution.py:352
  41.4 8.4 %own.1 = (f32[128,4096]{1,0:T(8,128)}, f32[128,4096]{1,0:T(8,128)}, f32[4,128]{1,0:T(4,128)S(1)}, f32[128,128]{1,0:T(8,128)S(1)}) custom-call(s32[1]{0:T(128)} %bitcast.2.which_ref, bf16[128,12288]{1,0:T(8,128)(2,1)} %q_ref.1, bf16[8,4096]{1,0:T(8,128)(2,1)} %get-tuple-element.36.hq_ref, f32[8,4096]{1,0:T(8,128)} %get-tuple-element.37.taps_ref, ...), custom_call_target="tpu_custom_call" | custom-call | tf_op jit(solution)/shard_map/own/pallas_call | solution.py:485
  49.8 0.0 all-to-all-done.terms_ref
  49.8 0.3 totals.1
  50.1 3.3 %collective-permute-start.2 = (f32[4,128]{1,0:T(4,128)S(1)}, f32[4,128]{1,0:T(4,128)S(1)}, u32[]{:S(2)}, u32[]{:S(2)}) collective-permute-start(f32[4,128]{1,0:T(4,128)S(1)} %totals.1), channel_id=1, source_target_pairs={{0,128},{16,144},{32,160},{48,176},{64,192},{80,208},{96,224},{112... | collective-permute-start | bytes 6152 | tf_op jit(solution)/shard_map/ppermute | solution.py:690
  53.4 0.7 collective-permute-done.2.enter_ref
  54.1 0.9 %states.1 = bf16[128,4,128]{2,1,0:T(4,128)(2,1)} custom-call(bf16[128,4,128]{2,1,0:T(4,128)(2,1)S(1)} %all-to-all-done.terms_ref, f32[4,128]{1,0:T(4,128)S(1)} %get-tuple-element.47.decay_ref, f32[128,128]{1,0:T(8,128)S(1)} %get-tuple-element.48.live_ref, f32[4,128]{1,0:T(4,128)S(1)} %collective-permute-done.2.enter_ref), custom_call_target="tpu_custom_call" | custom-call | tf_op jit(solution)/shard_map/states/pallas_call | solution.py:597
  55.1 14.4 %all-to-all-start.1 = ((bf16[128,4,128]{2,1,0:T(4,128)(2,1)}), bf16[128,4,128]{2,1,0:T(4,128)(2,1)S(1)}, u32[]{:S(2)}, u32[]{:S(2)}) async-start(bf16[128,4,128]{2,1,0:T(4,128)(2,1)} %states.1), calls=%async_computation.1 | async-start | bytes 262144 | tf_op jit(solution)/shard_map/all_to_all | solution.py:714
  69.5 0.0 collective-permute-done.1.x_ref
  69.5 0.0 copy-start
  69.5 1.0 %copy-done = bf16[128,4096]{1,0:T(8,128)(2,1)} copy-done((bf16[128,4096]{1,0:T(8,128)(2,1)}, bf16[128,4096]{1,0:T(8,128)(2,1)S(1)}, u32[]{:S(2)}) %copy-start) | copy-done | bytes 1048600
  70.4 6.5 %earlier.1 = (f32[128,4096]{1,0:T(8,128)S(1)}, bf16[128,4096]{1,0:T(8,128)(2,1)S(1)}) custom-call(bf16[128,4096]{1,0:T(8,128)(2,1)} %copy-done, f32[256,128]{1,0:T(8,128)} %get-tuple-element.35.taps_ref, s32[128,128]{1,0:T(8,128)} %get-tuple-element.34.srel_ref, f32[128,4096]{1,0:T(8,128)} %get-tuple-element.41.acc_ref, ...), custom_call_target="tpu_custom_call" | custom-call | tf_op jit(solution)/shard_map/earlier/pallas_call | solution.py:548
  77.0 4.7 %all-to-all-done.1 = bf16[128,4,128]{2,1,0:T(4,128)(2,1)S(1)} async-done(((bf16[128,4,128]{2,1,0:T(4,128)(2,1)}), bf16[128,4,128]{2,1,0:T(4,128)(2,1)S(1)}, u32[]{:S(2)}, u32[]{:S(2)}) %all-to-all-start.1) | async-done | bytes 131104 | tf_op jit(solution)/shard_map/all_to_all | solution.py:714
  81.7 3.1 %final.1 = bf16[128,4096]{1,0:T(8,128)(2,1)} custom-call(f32[128,4096]{1,0:T(8,128)S(1)} %get-tuple-element.43.acc_ref, f32[128,4096]{1,0:T(8,128)} %get-tuple-element.44.query_hbm, bf16[128,4096]{1,0:T(8,128)(2,1)S(1)} %get-tuple-element.45.dec_ref, bf16[4,32,4,128]{3,2,1,0:T(4,128)(2,1)S(1)} %bitcast.6), custom_call_target="tpu_custom_call" | custom-call | tf_op jit(solution)/shard_map/final/pallas_call | solution.py:661
Async XLA Ops:
  0.9 12.2 %collective-permute-start = (bf16[8,12288]{1,0:T(8,128)(2,1)S(1)}, bf16[8,12288]{1,0:T(8,128)(2,1)S(1)}, u32[]{:S(2)}, u32[]{:S(2)}) collective-permute-start(bf16[8,12288]{1,0:T(8,128)(2,1)S(1)} %slice.3), channel_id=1, source_target_pairs={{0,1},{1,2},{2,3},{3,4},{4,5},{5,6},{6,7},{7,8},{8,9},{9,10},{10,1... | collective-permute-start | bytes 589832 | tf_op jit(solution)/shard_map/ppermute | solution.py:692
  13.1 21.9 %copy-start.1 = (f32[16,256]{1,0:T(8,128)S(1)}, f32[16,256]{1,0:T(8,128)}, u32[]{:S(2)}) copy-start(f32[16,256]{1,0:T(8,128)} %rates_ref.3) | copy-start | bytes 49156
  13.1 21.9 %copy-start.2 = (f32[16,256]{1,0:T(8,128)S(1)}, f32[16,256]{1,0:T(8,128)}, u32[]{:S(2)}) copy-start(f32[16,256]{1,0:T(8,128)} %param.12) | copy-start | bytes 49156
  16.6 52.9 %collective-permute-start.1 = (bf16[128,4096]{1,0:T(8,128)(2,1)}, bf16[128,4096]{1,0:T(8,128)(2,1)S(1)}, u32[]{:S(2)}, u32[]{:S(2)}) collective-permute-start(bf16[128,4096]{1,0:T(8,128)(2,1)} %get-tuple-element.33.x_ref), channel_id=1, source_target_pairs={{0,1},{1,2},{2,3},{3,4},{4,5},{5,6},{6,7},{7,8},{8,9},{9,10},{10,1... | collective-permute-start | bytes 3145736 | tf_op jit(solution)/shard_map/ppermute | solution.py:700
  18.5 31.3 %all-to-all-start = ((bf16[128,4,128]{2,1,0:T(4,128)(2,1)}), bf16[128,4,128]{2,1,0:T(4,128)(2,1)S(1)}, u32[]{:S(2)}, u32[]{:S(2)}) async-start(bf16[128,4,128]{2,1,0:T(4,128)(2,1)} %bitcast.7), calls=%async_computation | async-start | bytes 262144 | tf_op jit(solution)/shard_map/all_to_all | solution.py:702
  50.1 4.0 %collective-permute-start.2 = (f32[4,128]{1,0:T(4,128)S(1)}, f32[4,128]{1,0:T(4,128)S(1)}, u32[]{:S(2)}, u32[]{:S(2)}) collective-permute-start(f32[4,128]{1,0:T(4,128)S(1)} %totals.1), channel_id=1, source_target_pairs={{0,128},{16,144},{32,160},{48,176},{64,192},{80,208},{96,224},{112... | collective-permute-start | bytes 6152 | tf_op jit(solution)/shard_map/ppermute | solution.py:690
  55.1 26.6 %all-to-all-start.1 = ((bf16[128,4,128]{2,1,0:T(4,128)(2,1)}), bf16[128,4,128]{2,1,0:T(4,128)(2,1)S(1)}, u32[]{:S(2)}, u32[]{:S(2)}) async-start(bf16[128,4,128]{2,1,0:T(4,128)(2,1)} %states.1), calls=%async_computation.1 | async-start | bytes 262144 | tf_op jit(solution)/shard_map/all_to_all | solution.py:714
  69.5 1.0 %copy-start = (bf16[128,4096]{1,0:T(8,128)(2,1)}, bf16[128,4096]{1,0:T(8,128)(2,1)S(1)}, u32[]{:S(2)}) copy-start(bf16[128,4096]{1,0:T(8,128)(2,1)S(1)} %collective-permute-done.1.x_ref) | copy-start | bytes 3145732

commit v5 on v4

--- a/solution.py
+++ b/solution.py
@@ -11,8 +11,8 @@
 MODES = 16
 LANES = 128
 DOCS = 16
-SPAN = 8
-PARTS = 4
+SPAN = 4
+PARTS = 2
 PART = MODES // PARTS
 PER_TILE = LANES // GROUP
 FLAT = ("ctx", "ts")
@@ -82,7 +82,7 @@
 def front_kernel(
     place_ref, docs_ref, taps_ref, rates_ref, raw_ref,
     srel_ref, live_ref, tapsx_ref, tail_ref, product_ref, head_ref,
-    stack_ref, pieces_ref, raws_ref, wk_ref, wv_ref, rel_ref, near_ref, sems,
+    stack_ref, raws_ref, wk_ref, wv_ref, rel_ref, near_ref, sems,
 ):
     width = product_ref.shape[1]
     copies = [
@@ -110,17 +110,16 @@
     for p in range(3):
         stack_ref[8 * p : 8 * p + SHORT] = taps_ref[p]
     stack_ref[24:40] = rates_ref[...]
-    split_into(pieces_ref, stack_ref[...])
     own_mode = iota((MODES, LANES), 0) == iota((MODES, LANES), 1) % MODES
     behind = (BLOCK - 1 - row).astype(f32)
 
-    def expand(j, k):
-        spread = expanded(pieces_ref, j)
+    def expand(j, k, half):
+        spread = expanded(stack_ref, j, half)
         tapsx_ref[:, tile(j)] = spread[0:24]
         rate = jnp.sum(jnp.where(own_mode, spread[24:40], 0.0), axis=0, keepdims=True)
         tail_ref[tile(j), :] = jnp.exp(-rate * behind).astype(bf16).T
 
-    for_tiles(width // LANES, expand)
+    for_halves(stack_ref.shape[1], expand)
     for copy in copies:
         copy.wait()
     rel_ref[...] = row - (starts - base)
@@ -145,22 +144,23 @@
     head_ref[1] = raws_ref[1, 0:8]
 
 
-def split_into(pieces_ref, whole):
-    upper = whole.astype(bf16)
-    rest = whole - upper.astype(f32)
-    middle = rest.astype(bf16)
-    pieces_ref[0] = upper
-    pieces_ref[1] = middle
-    pieces_ref[2] = (rest - middle.astype(f32)).astype(bf16)
-
-
-def expanded(pieces_ref, j):
-    _, lines, groups = pieces_ref.shape
-    pieces = jnp.concatenate([pieces_ref[0], pieces_ref[1], pieces_ref[2]], axis=0)
-    ahead = iota((groups, LANES), 0) - iota((groups, LANES), 1) // GROUP
-    hot = jnp.where(ahead == j * PER_TILE, 1.0, 0.0).astype(bf16)
-    spread = jnp.dot(pieces, hot, preferred_element_type=f32)
-    return spread[0:lines] + spread[lines : 2 * lines] + spread[2 * lines :]
+def expanded(lines_ref, j, half):
+    lines = lines_ref[:, tile(half)]
+    first = (j - half * (LANES // PER_TILE)) * PER_TILE
+    at = first + iota(lines.shape, 1) // GROUP
+    return jnp.take_along_axis(lines, at, axis=1, mode="promise_in_bounds")
+
+
+def for_halves(groups, body, unroll=TILES):
+    each = LANES // PER_TILE
+    for half in range(groups // LANES):
+
+        def step(i, carry):
+            for k in range(unroll):
+                body(half * each + i * unroll + k, k, half)
+            return carry
+
+        lax.fori_loop(0, each // unroll, step, 0)
 
 
 def make_front(place, doc_lengths, short_taps, decay_rates, projected, size):
@@ -187,8 +187,7 @@
         ],
         out_specs=tuple([in_vmem()] * 6),
         scratch_shapes=[
-            pltpu.VMEM((48, groups), f32),
-            pltpu.VMEM((3, 48, groups), bf16),
+            pltpu.VMEM((40, groups), f32),
             pltpu.VMEM((2, BLOCK, width), bf16),
             pltpu.VMEM((TILES, 8 + ROWS, LANES), f32),
             pltpu.VMEM((TILES, 8 + ROWS, LANES), f32),
@@ -301,7 +300,7 @@
 def tables_kernel(
     srel_ref, rates_ref, scaled_ref, medium_ref,
     dec_ref, own_ref, med_ref, ratesx_ref,
-    long_ref, pieces_ref,
+    long_ref, lines_ref,
 ):
     row = iota((BLOCK, LANES), 0)
     lane = iota((BLOCK, LANES), 1)
@@ -309,34 +308,30 @@
     own_mode = iota((MODES, LANES), 0) == iota((MODES, LANES), 1) % MODES
     ahead = (row + 1).astype(f32)
     behind = (BLOCK - 1 - row).astype(f32)
-    each = LANES // PER_TILE
-    split_into(pieces_ref, jnp.concatenate([rates_ref[...], scaled_ref[...]], axis=0))
+    lines_ref[0:MODES] = rates_ref[...]
+    lines_ref[MODES:] = scaled_ref[...]
     long_ref[...] = jnp.zeros(long_ref.shape, f32)
-
-    def step(i, carry):
-        total = long_ref[(i * TILES) // each]
-        for k in range(TILES):
-            j = i * TILES + k
-            spread = expanded(pieces_ref, j)
-            ratesx_ref[:, tile(j)] = spread[0:MODES]
-            rate = jnp.sum(jnp.where(own_mode, spread[0:MODES], 0.0), axis=0, keepdims=True)
-            scale = jnp.sum(jnp.where(own_mode, spread[MODES:], 0.0), axis=0, keepdims=True)
-            decay = jnp.where(old, scale * jnp.exp(-rate * ahead), 0.0)
-            dec_ref[:, tile(j)] = decay.astype(bf16)
-            power = scale * jnp.exp(-rate * behind)
-            upper = power.astype(bf16)
-            lower = (power - upper.astype(f32)).astype(bf16)
-            first = lax.rem(j, each) * PER_TILE
-            hot = jnp.where(lane - row // MODES == first, 1.0, 0.0).astype(bf16)
-            total = total + jnp.dot(
-                jnp.concatenate([upper, lower], axis=1),
-                jnp.concatenate([hot, hot], axis=0),
-                preferred_element_type=f32,
-            )
-        long_ref[(i * TILES) // each] = total
-        return carry
-
-    lax.fori_loop(0, dec_ref.shape[1] // (LANES * TILES), step, 0)
+    ahead_of = lane - row // MODES
+
+    def body(j, k, half):
+        spread = expanded(lines_ref, j, half)
+        ratesx_ref[:, tile(j)] = spread[0:MODES]
+        rate = jnp.sum(jnp.where(own_mode, spread[0:MODES], 0.0), axis=0, keepdims=True)
+        scale = jnp.sum(jnp.where(own_mode, spread[MODES:], 0.0), axis=0, keepdims=True)
+        decay = jnp.where(old, scale * jnp.exp(-rate * ahead), 0.0)
+        dec_ref[:, tile(j)] = decay.astype(bf16)
+        power = scale * jnp.exp(-rate * behind)
+        upper = power.astype(bf16)
+        lower = (power - upper.astype(f32)).astype(bf16)
+        first = (j - half * (LANES // PER_TILE)) * PER_TILE
+        hot = jnp.where(ahead_of == first, 1.0, 0.0).astype(bf16)
+        long_ref[half] += jnp.dot(
+            jnp.concatenate([upper, lower], axis=1),
+            jnp.concatenate([hot, hot], axis=0),
+            preferred_element_type=f32,
+        )
+
+    for_halves(medium_ref.shape[1], body)
     flip = jnp.where(row + lane == BLOCK - 1, 1.0, 0.0)
     for h in range(long_ref.shape[0]):
         medium = jnp.dot(
@@ -367,7 +362,7 @@
         out_specs=tuple([in_vmem()] * 4),
         scratch_shapes=[
             pltpu.VMEM((groups // LANES, BLOCK, LANES), f32),
-            pltpu.VMEM((3, 2 * MODES, groups), bf16),
+            pltpu.VMEM((2 * MODES, groups), f32),
         ],
         compiler_params=params(),
         name="tables",
@@ -433,9 +428,9 @@
 
 
 def own_kernel(
-    which_ref, q_ref, hq_ref, taps_ref, srel_ref, x_ref, own_ref, skip_ref, rates_ref, live_ref,
-    query_ref, acc_ref, decay_ref, live_out,
-    wq_ref, mask_ref, rel_ref, near_ref,
+    which_ref, srel_ref, x_ref, own_ref, skip_ref, rates_ref, live_ref,
+    acc_ref, decay_ref, live_out,
+    mask_ref,
 ):
     row = iota((BLOCK, LANES), 0)
     lane = iota((BLOCK, LANES), 1)
@@ -444,24 +439,8 @@
     def _():
         mask = (lane <= row) & (lane >= srel_ref[...])
         mask_ref[...] = jnp.where(mask, 1.0, 0.0).astype(bf16)
-        tiles = pl.num_programs(0) * CHUNK
-        upper = lax.rem(which_ref[0] // tiles, 2) == 1
-        rates = jnp.where(upper, rates_ref[PART:8], rates_ref[0:PART])
-        decay_ref[...] = jnp.exp(-rates * float(BLOCK))
+        decay_ref[...] = jnp.exp(-rates_ref[...] * float(BLOCK))
         live_out[...] = live_ref[...]
-        rel_ref[...] = row - srel_ref[...]
-        find_near(rel_ref, near_ref)
-
-    def rows_of_query(at, masked):
-        def ask(j, k):
-            past = hq_ref[:, tile(j)].astype(f32)
-            query_ref[at : at + ROWS, tile(j)] = feature_of(
-                q_ref, past, taps_ref, 0, j, at, rel_ref, wq_ref.at[k], masked
-            )
-
-        for_tiles(CHUNK, ask, CHUNK)
-
-    by_rows(near_ref, rows_of_query)
 
     def body(j, k):
         acc = skip_ref[:, tile(j)] * x_ref[:, tile(j)].astype(f32)
@@ -478,14 +457,13 @@
     return pl.BlockSpec(shape, lambda *_: (0,) * len(shape))
 
 
-def make_own(which, projected, edge, tapsq, srel, product, own, skip, ratesx, live):
+def make_own(which, srel, product, own, skip, ratesx, live):
     width = product.shape[1]
     tiles = width // LANES
     shape = jax.ShapeDtypeStruct
     return pl.pallas_call(
         own_kernel,
         out_shape=(
-            pltpu.HBM((BLOCK, width), f32),
             pltpu.HBM((BLOCK, width), f32),
             shape((PART, LANES), f32),
             shape(live.shape, f32),
@@ -494,38 +472,25 @@
             num_scalar_prefetch=1,
             grid=(width // WIDE,),
             in_specs=[
-                cols(BLOCK),
-                cols(8),
-                cols(8),
                 whole((BLOCK, LANES)),
                 cols(BLOCK),
                 pl.BlockSpec((WIDE // GROUP, LANES), lambda j, *_: (j, 0)),
                 cols(1),
-                pl.BlockSpec((8, LANES), lambda _, at: (at[0] // (2 * tiles), at[0] % tiles)),
+                pl.BlockSpec((8, LANES), lambda _, at: (at[0] // tiles, at[0] % tiles)),
                 whole(live.shape),
             ],
-            out_specs=(
-                cols(BLOCK),
-                cols(BLOCK),
-                whole((PART, LANES)),
-                whole(live.shape),
-            ),
-            scratch_shapes=[
-                pltpu.VMEM((CHUNK, 8 + ROWS, LANES), f32),
-                pltpu.VMEM((BLOCK, LANES), bf16),
-                pltpu.VMEM((BLOCK, LANES), i32),
-                pltpu.SMEM((BLOCK // ROWS,), i32),
-            ],
+            out_specs=(cols(BLOCK), whole((PART, LANES)), whole(live.shape)),
+            scratch_shapes=[pltpu.VMEM((BLOCK, LANES), bf16)],
         ),
         compiler_params=params(20),
         name="own",
-    )(which, *hbm(projected, edge, tapsq, srel, product), own, *hbm(skip), ratesx, *hbm(live))
+    )(which, *hbm(srel, product), own, *hbm(skip), ratesx, *hbm(live))
 
 
 def earlier_kernel(
-    x_ref, taps_ref, srel_ref, acc_ref, dec_ref,
-    out_ref, dec_out,
-    mask_ref,
+    q_ref, hq_ref, tapsq_ref, x_ref, taps_ref, srel_ref, acc_ref, dec_ref,
+    out_ref, dec_out, query_ref,
+    mask_ref, wq_ref, rel_ref, near_ref,
 ):
     row = iota((BLOCK, LANES), 0)
     lane = iota((BLOCK, LANES), 1)
@@ -535,6 +500,19 @@
     def _():
         inside = (lane > row) & (lane - BLOCK >= srel_ref[...])
         mask_ref[...] = jnp.where(inside, 1.0, 0.0).astype(bf16)
+        rel_ref[...] = row - srel_ref[...]
+        find_near(rel_ref, near_ref)
+
+    def rows_of_query(at, masked):
+        def ask(j, k):
+            past = hq_ref[:, tile(j)].astype(f32)
+            query_ref[at : at + ROWS, tile(j)] = feature_of(
+                q_ref, past, tapsq_ref, 0, j, at, rel_ref, wq_ref.at[k], masked
+            )
+
+        for_tiles(CHUNK, ask, CHUNK)
+
+    by_rows(near_ref, rows_of_query)
 
     def body(j, k):
         out_ref[:, tile(j)] = band_sum(j, x_ref, taps_ref, mask_ref, acc_ref[:, tile(j)])
@@ -542,7 +520,7 @@
     for_tiles(CHUNK, body, CHUNK)
 
 
-def make_earlier(before, med, srel, acc, dec):
+def make_earlier(projected, edge, tapsq, before, med, srel, acc, dec):
     width = acc.shape[1]
     shape = jax.ShapeDtypeStruct
     return pl.pallas_call(
@@ -551,33 +529,46 @@
         out_shape=(
             shape(acc.shape, f32),
             shape(acc.shape, bf16),
+            pltpu.HBM(acc.shape, f32),
         ),
         in_specs=[
+            columns(BLOCK),
+            columns(8),
+            columns(8),
             columns(BLOCK),
             rows_of(WIDE // GROUP),
             fixed((BLOCK, LANES)),
             columns(BLOCK),
             columns(BLOCK),
         ],
-        out_specs=(columns(BLOCK), columns(BLOCK)),
-        scratch_shapes=[pltpu.VMEM((BLOCK, LANES), bf16)],
+        out_specs=(columns(BLOCK), columns(BLOCK), columns(BLOCK)),
+        scratch_shapes=[
+            pltpu.VMEM((BLOCK, LANES), bf16),
+            pltpu.VMEM((CHUNK, 8 + ROWS, LANES), f32),
+            pltpu.VMEM((BLOCK, LANES), i32),
+            pltpu.SMEM((BLOCK // ROWS,), i32),
+        ],
         compiler_params=params(20),
         name="earlier",
-    )(*hbm(before, med, srel, acc, dec))
+    )(*hbm(projected, edge, tapsq, before, med, srel, acc, dec))
 
 
 def totals_kernel(terms_ref, decay_ref, live_ref, out_ref):
     decay = decay_ref[...]
     state = jnp.zeros((PART, LANES), f32)
+    kept = jnp.ones((PART, LANES), f32)
     for b in range(terms_ref.shape[0]):
-        state = live_ref[b : b + 1] * decay * state + terms_ref[b].astype(f32)
-    out_ref[...] = state
+        factor = live_ref[b : b + 1] * decay
+        state = factor * state + terms_ref[b].astype(f32)
+        kept = factor * kept
+    out_ref[0] = state
+    out_ref[1] = kept
 
 
 def make_totals(terms, decay, live):
     return pl.pallas_call(
         totals_kernel,
-        out_shape=jax.ShapeDtypeStruct((PART, LANES), f32),
+        out_shape=jax.ShapeDtypeStruct((2, PART, LANES), f32),
         in_specs=[in_vmem()] * 3,
         out_specs=in_vmem(),
         compiler_params=params(),
@@ -585,23 +576,23 @@
     )(terms, decay, live)
 
 
-def states_kernel(terms_ref, decay_ref, live_ref, enter_ref, out_ref):
+def states_kernel(terms_ref, decay_ref, live_ref, one_ref, two_ref, out_ref):
     decay = decay_ref[...]
-    state = enter_ref[...]
+    state = one_ref[0] + one_ref[1] * two_ref[0]
     for b in range(terms_ref.shape[0]):
         out_ref[b] = state.astype(bf16)
         state = live_ref[b : b + 1] * decay * state + terms_ref[b].astype(f32)
 
 
-def make_states(terms, decay, live, enter):
+def make_states(terms, decay, live, one, two):
     return pl.pallas_call(
         states_kernel,
         out_shape=pltpu.HBM(terms.shape, bf16),
-        in_specs=[in_vmem()] * 4,
+        in_specs=[in_vmem()] * 5,
         out_specs=in_vmem(),
         compiler_params=params(),
         name="states",
-    )(terms, decay, live, enter)
+    )(terms, decay, live, one, two)
 
 
 def final_kernel(
@@ -630,8 +621,7 @@
     keep = jnp.where(same, 1.0, 0.0).astype(bf16)
 
     def carry_in(j, k):
-        parts = [state_ref[p, j].astype(f32) for p in range(PARTS)]
-        one = jnp.concatenate(parts, axis=0).astype(bf16)
+        one = jnp.concatenate([state_ref[p, j] for p in range(PARTS)], axis=0)
         spread = jnp.concatenate([one] * PER_TILE, axis=0) * keep
         carried = jnp.dot(dec_ref[:, tile(j)], spread, preferred_element_type=f32)
         filtered_ref[:, tile(j)] = (acc_ref[:, tile(j)] + carried).astype(bf16)
@@ -641,13 +631,12 @@
     def chunk(c, carry):
         fetch(c).wait()
 
-        def inner(i, more):
-            at = tile(c * CHUNK + i)
+        def inner(j, k):
+            at = tile(c * CHUNK + j)
             filtered = filtered_ref[:, at].astype(f32)
             out_ref[:, at] = (query_ref[:, at] * filtered).astype(bf16)
-            return more
-
-        lax.fori_loop(0, CHUNK, inner, 0)
+
+        for_tiles(CHUNK, inner)
         send(c).start()
         return carry
 
@@ -704,17 +693,17 @@
     )
     scaled = residues * jnp.sqrt(-jnp.expm1(-2.0 * decay_rates))
     dec, own, med, ratesx = make_tables(srel, decay_rates, scaled, medium_taps, width)
-    query, acc, decay, near = make_own(
-        which.reshape(1), projected, edge, tapsq, srel, product, own,
-        skip_gain.reshape(1, -1), ratesx, live,
+    acc, decay, near = make_own(
+        which.reshape(1), srel, product, own, skip_gain.reshape(1, -1), ratesx, live
     )
     totals = make_totals(terms, decay, near)
-    enter = from_ctx(totals, SPAN)
-    states = make_states(terms, decay, near, enter)
+    one = from_ctx(totals, SPAN)
+    two = from_ctx(totals, 2 * SPAN)
+    states = make_states(terms, decay, near, one, two)
     back = lax.all_to_all(
         states, FLAT, split_axis=0, concat_axis=0, tiled=True, axis_index_groups=groups
     )
-    acc, dec = make_earlier(before, med, srel, acc, dec)
+    acc, dec, query = make_earlier(projected, edge, tapsq, before, med, srel, acc, dec)
     return make_final(acc, query, dec, back.reshape(PARTS, width // LANES, PART, LANES))
 
 

time: 85.5 us -> 82.2 us (0.961)
  the two profiles are of different devices: /device:TPU:1 before, /device:TPU:57 now
where the time goes in v5:
time: 82.2 us; the launch traced here: 81.6 us
  starting transfers between devices  41.2 us (50%)
  Pallas kernels  33.8 us (41%)
  waiting for transfers between devices  3.83 us (5%)
  local copies, waits for them, and re-layouts  1.92 us (2%)
    all_to_all x1, starting transfers between devices, per_device(): lax.all_to_all(items, FLAT, split_axis=0, concat_axis=0, tiled=True, axis...  15 us
    all_to_all x1, starting transfers between devices, per_device(): lax.all_to_all(states, FLAT, split_axis=0, concat_axis=0, tiled=True, axi...  12.2 us
    pallas_call x1, Pallas kernels, make_earlier(): pl.pallas_call(earlier_kernel, grid=(width // WIDE,), out_shape=(shape(ac...  9.07 us
    ppermute x2, starting transfers between devices, from_ctx(): lax.ppermute(value, 'ctx', [(i, i + by) for i in range(ctx_count - by)])  7.57 us
    pallas_call x1, Pallas kernels, make_own(): pl.pallas_call(own_kernel, out_shape=(pltpu.HBM((BLOCK, width), f32), sha...  6.8 us
    pallas_call x1, Pallas kernels, make_front(): pl.pallas_call(front_kernel, grid=(1,), out_shape=(shape((BLOCK, LANES),...  5.56 us
    pallas_call x1, Pallas kernels, make_tables(): pl.pallas_call(tables_kernel, grid=(1,), out_shape=(pltpu.HBM((BLOCK, wid...  5.07 us
    ppermute x1, starting transfers between devices, per_device(): halo = lax.ppermute(projected[BLOCK - 8:], FLAT, onward)  4.56 us
  transfers between devices with their start and end apart: 6, of which 1 were waited for; matrix products, arithmetic and copies ran while one was open for 1% of the time, Pallas kernels for 34%

profile of v5, /device:TPU:57, one launch (start us, length us, event | category | flops | bytes accessed | tf_op | source)
XLA Modules:
  0.0 81.6 jit_solution(9813874264064179849)
XLA Ops:
  0.0 0.9 %slice.3 = bf16[8,12288]{1,0:T(8,128)(2,1)S(1)} slice(bf16[128,12288]{1,0:T(8,128)(2,1)} %q_ref.1), slice={[120:128], [0:12288]} | slice | bytes 393216 | tf_op jit(solution)/shard_map/slice | solution.py:681
  0.9 4.6 %collective-permute-start = (bf16[8,12288]{1,0:T(8,128)(2,1)S(1)}, bf16[8,12288]{1,0:T(8,128)(2,1)S(1)}, u32[]{:S(2)}, u32[]{:S(2)}) collective-permute-start(bf16[8,12288]{1,0:T(8,128)(2,1)S(1)} %slice.3), channel_id=1, source_target_pairs={{0,1},{1,2},{2,3},{3,4},{4,5},{5,6},{6,7},{7,8},{8,9},{9,10},{10,1... | collective-permute-start | bytes 589832 | tf_op jit(solution)/shard_map/ppermute | solution.py:681
  5.5 0.1 pad_add_fusion.place_ref
  5.6 5.6 %front.1 = (s32[128,128]{1,0:T(8,128)S(1)}, f32[64,128]{1,0:T(8,128)S(1)}, f32[24,4096]{1,0:T(8,128)S(1)}, bf16[4096,128]{1,0:T(8,128)(2,1)S(1)}, bf16[128,4096]...) custom-call(s32[2]{0:T(128)S(1)} %pad_add_fusion.place_ref, s32[16]{0:T(128)} %docs_ref.1, f32[3,7,256]{2,1,0:T(8,128)} %taps_ref.1, ...), custom_call_target="tpu_custom_call" | custom-call | tf_op jit(solution)/shard_map/front/pallas_call | solution.py:170
  11.2 0.0 copy-start.1
  11.2 0.0 copy-start.2
  11.2 0.0 collective-permute-done.halo_ref
  11.2 3.4 %edge.1 = (bf16[128,4096]{1,0:T(8,128)(2,1)}, bf16[2,32,8,128]{3,2,1,0:T(8,128)(2,1)}, bf16[8,4096]{1,0:T(8,128)(2,1)}, f32[8,4096]{1,0:T(8,128)}, s32[128,128]{1,0:T(8,128)}, /*index=5*/f32[64,128]{1,0:T(8,128)}) custom-call(bf16[128,4096]{1,0:T(8,128)(2,1)S(1)} %get-tuple-element.27.main_ref, bf16[2,8,4096]{2,1,0:T(8,128)(2,1)S(1)} %get-tuple-element.28.head_ref, ...), custom_call_target="tpu_custom_call" | custom-call | tf_op jit(solution)/shard_map/edge/pallas_call | solution.py:277
  14.6 1.9 %collective-permute-start.1 = (bf16[128,4096]{1,0:T(8,128)(2,1)}, bf16[128,4096]{1,0:T(8,128)(2,1)S(1)}, u32[]{:S(2)}, u32[]{:S(2)}) collective-permute-start(bf16[128,4096]{1,0:T(8,128)(2,1)} %get-tuple-element.35.x_ref), channel_id=1, source_target_pairs={{0,1},{1,2},{2,3},{3,4},{4,5},{5,6},{6,7},{7,8},{8,9},{9,10},{10,1... | collective-permute-start | bytes 3145736 | tf_op jit(solution)/shard_map/ppermute | solution.py:689
  16.5 15.0 %all-to-all-start = ((bf16[64,8,128]{2,1,0:T(8,128)(2,1)}), bf16[64,8,128]{2,1,0:T(8,128)(2,1)S(1)}, u32[]{:S(2)}, u32[]{:S(2)}) async-start(bf16[64,8,128]{2,1,0:T(8,128)(2,1)} %bitcast.7), calls=%async_computation | async-start | bytes 262144 | tf_op jit(solution)/shard_map/all_to_all | solution.py:691
  31.5 0.0 copy-done.1
  31.6 0.0 copy-done.2
  31.6 0.6 sqrt_multiply_fusion.scaled_ref
  32.2 5.1 %tables.1 = (bf16[128,4096]{1,0:T(8,128)(2,1)}, f32[256,128]{1,0:T(8,128)S(1)}, f32[256,128]{1,0:T(8,128)}, f32[16,4096]{1,0:T(8,128)S(1)}) custom-call(s32[128,128]{1,0:T(8,128)} %get-tuple-element.36.srel_ref, f32[16,256]{1,0:T(8,128)} %rates_ref.3, f32[16,256]{1,0:T(8,128)} %sqrt_multiply_fusion.scaled_ref, f32[128,256]{1,0:T(8,128)} %medium_ref.1), custom_call_target="tpu_custom_call" | custom-call | tf_op jit(solution)/shard_map/tables/pallas_call | solution.py:347
  37.3 6.8 %own.1 = (f32[128,4096]{1,0:T(8,128)}, f32[8,128]{1,0:T(8,128)S(1)}, f32[64,128]{1,0:T(8,128)S(1)}) custom-call(s32[1]{0:T(128)} %bitcast.2.which_ref, s32[128,128]{1,0:T(8,128)} %get-tuple-element.36.srel_ref, bf16[128,4096]{1,0:T(8,128)(2,1)} %get-tuple-element.35.x_ref, f32[256,128]{1,0:T(8,128)S(1)} %get-tuple-element.38.own_ref, f32[1,4096]{1,0:T(1,128)} %bitcast.8, ...), custom_call_target="tpu_custom_call" | custom-call | tf_op jit(solution)/shard_map/own/pallas_call | solution.py:464
  44.1 0.0 all-to-all-done.terms_ref
  44.1 0.1 totals.1
  44.2 3.1 %collective-permute-start.3 = (f32[2,8,128]{2,1,0:T(8,128)S(1)}, f32[2,8,128]{2,1,0:T(8,128)S(1)}, u32[]{:S(2)}, u32[]{:S(2)}) collective-permute-start(f32[2,8,128]{2,1,0:T(8,128)S(1)} %totals.1), channel_id=1, source_target_pairs={{0,128},{16,144},{32,160},{48,176},{64,192},{80,208},{96,224},{112... | collective-permute-start | bytes 24584 | tf_op jit(solution)/shard_map/ppermute | solution.py:679
  47.3 4.5 %collective-permute-start.2 = (f32[2,8,128]{2,1,0:T(8,128)S(1)}, f32[2,8,128]{2,1,0:T(8,128)S(1)}, u32[]{:S(2)}, u32[]{:S(2)}) collective-permute-start(f32[2,8,128]{2,1,0:T(8,128)S(1)} %totals.1), channel_id=1, source_target_pairs={{0,64},{16,80},{32,96},{48,112},{64,128},{80,144},{96,160},{112,17... | collective-permute-start | bytes 24584 | tf_op jit(solution)/shard_map/ppermute | solution.py:679
  51.8 0.0 collective-permute-done.3.two_ref
  51.8 3.8 %collective-permute-done.2.one_ref = f32[2,8,128]{2,1,0:T(8,128)S(1)} collective-permute-done((f32[2,8,128]{2,1,0:T(8,128)S(1)}, f32[2,8,128]{2,1,0:T(8,128)S(1)}, u32[]{:S(2)}, u32[]{:S(2)}) %collective-permute-start.2) | collective-permute-done | bytes 8224 | tf_op jit(solution)/shard_map/ppermute | solution.py:679
  55.6 0.8 states.1
  56.4 12.2 %all-to-all-start.1 = ((bf16[64,8,128]{2,1,0:T(8,128)(2,1)}), bf16[64,8,128]{2,1,0:T(8,128)(2,1)S(1)}, u32[]{:S(2)}, u32[]{:S(2)}) async-start(bf16[64,8,128]{2,1,0:T(8,128)(2,1)} %states.1), calls=%async_computation.1 | async-start | bytes 262144 | tf_op jit(solution)/shard_map/all_to_all | solution.py:703
  68.6 0.0 collective-permute-done.1.x_ref
  68.6 0.0 copy-start
  68.6 1.0 %copy-done = bf16[128,4096]{1,0:T(8,128)(2,1)} copy-done((bf16[128,4096]{1,0:T(8,128)(2,1)}, bf16[128,4096]{1,0:T(8,128)(2,1)S(1)}, u32[]{:S(2)}) %copy-start) | copy-done | bytes 1048600
  69.5 9.1 %earlier.1 = (f32[128,4096]{1,0:T(8,128)S(1)}, bf16[128,4096]{1,0:T(8,128)(2,1)S(1)}, f32[128,4096]{1,0:T(8,128)}) custom-call(bf16[128,12288]{1,0:T(8,128)(2,1)} %q_ref.1, bf16[8,4096]{1,0:T(8,128)(2,1)} %get-tuple-element.33.hq_ref, f32[8,4096]{1,0:T(8,128)} %get-tuple-element.34.tapsq_ref, bf16[128,4096]{1,0:T(8,128)(2,1)} %copy-done, ...), custom_call_target="tpu_custom_call" | custom-call | tf_op jit(solution)/shard_map/earlier/pallas_call | solution.py:526
  78.6 0.0 all-to-all-done.1
  78.6 3.0 %final.1 = bf16[128,4096]{1,0:T(8,128)(2,1)} custom-call(f32[128,4096]{1,0:T(8,128)S(1)} %get-tuple-element.43.acc_ref, f32[128,4096]{1,0:T(8,128)} %get-tuple-element.44.query_hbm, bf16[128,4096]{1,0:T(8,128)(2,1)S(1)} %get-tuple-element.45.dec_ref, bf16[2,32,8,128]{3,2,1,0:T(8,128)(2,1)S(1)} %bitcast.6), custom_call_target="tpu_custom_call" | custom-call | tf_op jit(solution)/shard_map/final/pallas_call | solution.py:650
Async XLA Ops:
  0.9 10.3 %collective-permute-start = (bf16[8,12288]{1,0:T(8,128)(2,1)S(1)}, bf16[8,12288]{1,0:T(8,128)(2,1)S(1)}, u32[]{:S(2)}, u32[]{:S(2)}) collective-permute-start(bf16[8,12288]{1,0:T(8,128)(2,1)S(1)} %slice.3), channel_id=1, source_target_pairs={{0,1},{1,2},{2,3},{3,4},{4,5},{5,6},{6,7},{7,8},{8,9},{9,10},{10,1... | collective-permute-start | bytes 589832 | tf_op jit(solution)/shard_map/ppermute | solution.py:681
  11.2 20.4 %copy-start.1 = (f32[16,256]{1,0:T(8,128)S(1)}, f32[16,256]{1,0:T(8,128)}, u32[]{:S(2)}) copy-start(f32[16,256]{1,0:T(8,128)} %rates_ref.3) | copy-start | bytes 49156
  11.2 20.4 %copy-start.2 = (f32[16,256]{1,0:T(8,128)S(1)}, f32[16,256]{1,0:T(8,128)}, u32[]{:S(2)}) copy-start(f32[16,256]{1,0:T(8,128)} %param.12) | copy-start | bytes 49156
  14.6 54.0 %collective-permute-start.1 = (bf16[128,4096]{1,0:T(8,128)(2,1)}, bf16[128,4096]{1,0:T(8,128)(2,1)S(1)}, u32[]{:S(2)}, u32[]{:S(2)}) collective-permute-start(bf16[128,4096]{1,0:T(8,128)(2,1)} %get-tuple-element.35.x_ref), channel_id=1, source_target_pairs={{0,1},{1,2},{2,3},{3,4},{4,5},{5,6},{6,7},{7,8},{8,9},{9,10},{10,1... | collective-permute-start | bytes 3145736 | tf_op jit(solution)/shard_map/ppermute | solution.py:689
  16.5 27.5 %all-to-all-start = ((bf16[64,8,128]{2,1,0:T(8,128)(2,1)}), bf16[64,8,128]{2,1,0:T(8,128)(2,1)S(1)}, u32[]{:S(2)}, u32[]{:S(2)}) async-start(bf16[64,8,128]{2,1,0:T(8,128)(2,1)} %bitcast.7), calls=%async_computation | async-start | bytes 262144 | tf_op jit(solution)/shard_map/all_to_all | solution.py:691
  44.2 7.6 %collective-permute-start.3 = (f32[2,8,128]{2,1,0:T(8,128)S(1)}, f32[2,8,128]{2,1,0:T(8,128)S(1)}, u32[]{:S(2)}, u32[]{:S(2)}) collective-permute-start(f32[2,8,128]{2,1,0:T(8,128)S(1)} %totals.1), channel_id=1, source_target_pairs={{0,128},{16,144},{32,160},{48,176},{64,192},{80,208},{96,224},{112... | collective-permute-start | bytes 24584 | tf_op jit(solution)/shard_map/ppermute | solution.py:679
  47.3 8.3 %collective-permute-start.2 = (f32[2,8,128]{2,1,0:T(8,128)S(1)}, f32[2,8,128]{2,1,0:T(8,128)S(1)}, u32[]{:S(2)}, u32[]{:S(2)}) collective-permute-start(f32[2,8,128]{2,1,0:T(8,128)S(1)} %totals.1), channel_id=1, source_target_pairs={{0,64},{16,80},{32,96},{48,112},{64,128},{80,144},{96,160},{112,17... | collective-permute-start | bytes 24584 | tf_op jit(solution)/shard_map/ppermute | solution.py:679
  56.4 22.2 %all-to-all-start.1 = ((bf16[64,8,128]{2,1,0:T(8,128)(2,1)}), bf16[64,8,128]{2,1,0:T(8,128)(2,1)S(1)}, u32[]{:S(2)}, u32[]{:S(2)}) async-start(bf16[64,8,128]{2,1,0:T(8,128)(2,1)} %states.1), calls=%async_computation.1 | async-start | bytes 262144 | tf_op jit(solution)/shard_map/all_to_all | solution.py:703
  68.6 1.0 %copy-start = (bf16[128,4096]{1,0:T(8,128)(2,1)}, bf16[128,4096]{1,0:T(8,128)(2,1)S(1)}, u32[]{:S(2)}) copy-start(bf16[128,4096]{1,0:T(8,128)(2,1)S(1)} %collective-permute-done.1.x_ref) | copy-start | bytes 3145732

commit v6 on v5

--- a/solution.py
+++ b/solution.py
@@ -202,18 +202,22 @@
 
 def edge_kernel(
     main_ref, head_ref, halo_ref, taps_ref, srel_ref, live_ref, tail_ref,
-    product_out, contrib_out, edge_ref, tapsq_ref, srel_out, live_out,
-    window_ref, product_ref, contrib_ref, sems,
+    product_out, contrib_out, edge_out, tapsq_out, srel_out, live_out,
+    window_ref, product_ref, contrib_ref, sems, pass_sems,
 ):
     width = main_ref.shape[1]
     row = iota((BLOCK, LANES), 0)
     kept = jnp.where(row >= srel_ref[BLOCK - 1 : BLOCK], 1.0, 0.0).astype(bf16)
     rel = (row - srel_ref[...])[0:8]
     lane_group = iota((MODES, LANES), 1) // GROUP
-    edge_ref[...] = halo_ref[:, 0:width]
-    tapsq_ref[...] = taps_ref[0:8]
-    srel_out[...] = srel_ref[...]
-    live_out[...] = live_ref[...]
+    passed = [
+        pltpu.make_async_copy(halo_ref.at[:, 0:width], edge_out, pass_sems.at[0]),
+        pltpu.make_async_copy(taps_ref.at[0:8], tapsq_out, pass_sems.at[1]),
+        pltpu.make_async_copy(srel_ref, srel_out, pass_sems.at[2]),
+        pltpu.make_async_copy(live_ref, live_out, pass_sems.at[3]),
+    ]
+    for copy in passed:
+        copy.start()
 
     def body(j, slot):
         values = []
@@ -266,6 +270,8 @@
 
     chunks = width // WIDE
     lax.fori_loop(0, chunks, chunk, 0)
+    for copy in passed:
+        copy.wait()
     for c in range(chunks):
         for copy in copies(c):
             copy.wait()
@@ -285,12 +291,13 @@
             shape(live.shape, f32),
         ),
         in_specs=[in_vmem()] * 7,
-        out_specs=(in_hbm(), in_hbm(), in_vmem(), in_vmem(), in_vmem(), in_vmem()),
+        out_specs=tuple([in_hbm()] * 6),
         scratch_shapes=[
             pltpu.VMEM((TILES, 2, 16, LANES), f32),
             pltpu.VMEM((BLOCK, width), bf16),
             pltpu.VMEM((PARTS, width // LANES, PART, LANES), bf16),
             pltpu.SemaphoreType.DMA((2, width // WIDE)),
+            pltpu.SemaphoreType.DMA((4,)),
         ],
         compiler_params=params(),
         name="edge",
@@ -686,11 +693,11 @@
     product, contrib, edge, tapsq, srel, live = make_edge(
         main, head, halo, tapsx, srel, live, tail
     )
-    before = lax.ppermute(product, FLAT, onward)
     items = contrib.reshape(size, PART, LANES)
     terms = lax.all_to_all(
         items, FLAT, split_axis=0, concat_axis=0, tiled=True, axis_index_groups=groups
     )
+    before = lax.ppermute(product, FLAT, onward)
     scaled = residues * jnp.sqrt(-jnp.expm1(-2.0 * decay_rates))
     dec, own, med, ratesx = make_tables(srel, decay_rates, scaled, medium_taps, width)
     acc, decay, near = make_own(

time: 82.2 us -> 81.5 us (level)
  the two profiles are of different devices: /device:TPU:57 before, /device:TPU:2 now
where the time goes in v6:
time: 81.5 us; the launch traced here: 81 us
  Pallas kernels  33.1 us (41%)
  starting transfers between devices  31.3 us (38%)
  waiting for transfers between devices  13.8 us (17%)
  local copies, waits for them, and re-layouts  1.92 us (2%)
    all_to_all x1, starting transfers between devices, per_device(): lax.all_to_all(states, FLAT, split_axis=0, concat_axis=0, tiled=True, axi...  10.6 us
    ppermute x2, starting transfers between devices, from_ctx(): lax.ppermute(value, 'ctx', [(i, i + by) for i in range(ctx_count - by)])  9.33 us
    pallas_call x1, Pallas kernels, make_earlier(): pl.pallas_call(earlier_kernel, grid=(width // WIDE,), out_shape=(shape(ac...  9.08 us
    ppermute x1, waiting for transfers between devices, per_device(): halo = lax.ppermute(projected[BLOCK - 8:], FLAT, onward)  8.99 us
    all_to_all x1, starting transfers between devices, per_device(): lax.all_to_all(items, FLAT, split_axis=0, concat_axis=0, tiled=True, axis...  7.51 us
    pallas_call x1, Pallas kernels, make_own(): pl.pallas_call(own_kernel, out_shape=(pltpu.HBM((BLOCK, width), f32), sha...  6.79 us
    pallas_call x1, Pallas kernels, make_front(): pl.pallas_call(front_kernel, grid=(1,), out_shape=(shape((BLOCK, LANES),...  5.56 us
    pallas_call x1, Pallas kernels, make_tables(): pl.pallas_call(tables_kernel, grid=(1,), out_shape=(pltpu.HBM((BLOCK, wid...  5.07 us
  transfers between devices with their start and end apart: 6, of which 3 were waited for; matrix products, arithmetic and copies ran while one was open for 1% of the time, Pallas kernels for 34%

profile of v6, /device:TPU:2, one launch (start us, length us, event | category | flops | bytes accessed | tf_op | source)
XLA Modules:
  0.0 81.0 jit_solution(4825049517407070463)
XLA Ops:
  0.0 0.9 %slice.3 = bf16[8,12288]{1,0:T(8,128)(2,1)S(1)} slice(bf16[128,12288]{1,0:T(8,128)(2,1)} %q_ref.1), slice={[120:128], [0:12288]} | slice | bytes 393216 | tf_op jit(solution)/shard_map/slice | solution.py:688
  0.9 1.9 %collective-permute-start = (bf16[8,12288]{1,0:T(8,128)(2,1)S(1)}, bf16[8,12288]{1,0:T(8,128)(2,1)S(1)}, u32[]{:S(2)}, u32[]{:S(2)}) collective-permute-start(bf16[8,12288]{1,0:T(8,128)(2,1)S(1)} %slice.3), channel_id=1, source_target_pairs={{0,1},{1,2},{2,3},{3,4},{4,5},{5,6},{6,7},{7,8},{8,9},{9,10},{10,1... | collective-permute-start | bytes 589832 | tf_op jit(solution)/shard_map/ppermute | solution.py:688
  2.9 0.1 pad_add_fusion.place_ref
  3.0 5.6 %front.1 = (s32[128,128]{1,0:T(8,128)S(1)}, f32[64,128]{1,0:T(8,128)S(1)}, f32[24,4096]{1,0:T(8,128)S(1)}, bf16[4096,128]{1,0:T(8,128)(2,1)S(1)}, bf16[128,4096]...) custom-call(s32[2]{0:T(128)S(1)} %pad_add_fusion.place_ref, s32[16]{0:T(128)} %docs_ref.1, f32[3,7,256]{2,1,0:T(8,128)} %taps_ref.1, ...), custom_call_target="tpu_custom_call" | custom-call | tf_op jit(solution)/shard_map/front/pallas_call | solution.py:170
  8.5 0.0 copy-start.1
  8.5 0.0 copy-start.2
  8.6 9.0 %collective-permute-done.halo_ref = bf16[8,12288]{1,0:T(8,128)(2,1)S(1)} collective-permute-done((bf16[8,12288]{1,0:T(8,128)(2,1)S(1)}, bf16[8,12288]{1,0:T(8,128)(2,1)S(1)}, u32[]{:S(2)}, u32[]{:S(2)}) %collective-permute-start) | collective-permute-done | bytes 196640 | tf_op jit(solution)/shard_map/ppermute | solution.py:688
  17.6 2.7 %edge.1 = (bf16[128,4096]{1,0:T(8,128)(2,1)}, bf16[2,32,8,128]{3,2,1,0:T(8,128)(2,1)}, bf16[8,4096]{1,0:T(8,128)(2,1)}, f32[8,4096]{1,0:T(8,128)}, s32[128,128]{1,0:T(8,128)}, /*index=5*/f32[64,128]{1,0:T(8,128)}) custom-call(bf16[128,4096]{1,0:T(8,128)(2,1)S(1)} %get-tuple-element.27.main_ref, bf16[2,8,4096]{2,1,0:T(8,128)(2,1)S(1)} %get-tuple-element.28.head_ref, ...), custom_call_target="tpu_custom_call" | custom-call | tf_op jit(solution)/shard_map/edge/pallas_call | solution.py:283
  20.2 1.9 %collective-permute-start.1 = (bf16[128,4096]{1,0:T(8,128)(2,1)}, bf16[128,4096]{1,0:T(8,128)(2,1)S(1)}, u32[]{:S(2)}, u32[]{:S(2)}) collective-permute-start(bf16[128,4096]{1,0:T(8,128)(2,1)} %get-tuple-element.35.x_ref), channel_id=1, source_target_pairs={{0,1},{1,2},{2,3},{3,4},{4,5},{5,6},{6,7},{7,8},{8,9},{9,10},{10,1... | collective-permute-start | bytes 3145736 | tf_op jit(solution)/shard_map/ppermute | solution.py:700
  22.2 7.5 %all-to-all-start = ((bf16[64,8,128]{2,1,0:T(8,128)(2,1)}), bf16[64,8,128]{2,1,0:T(8,128)(2,1)S(1)}, u32[]{:S(2)}, u32[]{:S(2)}) async-start(bf16[64,8,128]{2,1,0:T(8,128)(2,1)} %bitcast.7), calls=%async_computation | async-start | bytes 262144 | tf_op jit(solution)/shard_map/all_to_all | solution.py:697
  29.7 0.0 copy-done.1
  29.7 0.0 copy-done.2
  29.7 0.6 sqrt_multiply_fusion.scaled_ref
  30.3 5.1 %tables.1 = (bf16[128,4096]{1,0:T(8,128)(2,1)}, f32[256,128]{1,0:T(8,128)S(1)}, f32[256,128]{1,0:T(8,128)}, f32[16,4096]{1,0:T(8,128)S(1)}) custom-call(s32[128,128]{1,0:T(8,128)} %get-tuple-element.36.srel_ref, f32[16,256]{1,0:T(8,128)} %rates_ref.3, f32[16,256]{1,0:T(8,128)} %sqrt_multiply_fusion.scaled_ref, f32[128,256]{1,0:T(8,128)} %medium_ref.1), custom_call_target="tpu_custom_call" | custom-call | tf_op jit(solution)/shard_map/tables/pallas_call | solution.py:354
  35.4 6.8 %own.1 = (f32[128,4096]{1,0:T(8,128)}, f32[8,128]{1,0:T(8,128)S(1)}, f32[64,128]{1,0:T(8,128)S(1)}) custom-call(s32[1]{0:T(128)} %bitcast.2.which_ref, s32[128,128]{1,0:T(8,128)} %get-tuple-element.36.srel_ref, bf16[128,4096]{1,0:T(8,128)(2,1)} %get-tuple-element.35.x_ref, f32[256,128]{1,0:T(8,128)S(1)} %get-tuple-element.38.own_ref, f32[1,4096]{1,0:T(1,128)} %bitcast.8, ...), custom_call_target="tpu_custom_call" | custom-call | tf_op jit(solution)/shard_map/own/pallas_call | solution.py:471
  42.2 0.0 all-to-all-done.terms_ref
  42.2 0.1 totals.1
  42.3 3.4 %collective-permute-start.3 = (f32[2,8,128]{2,1,0:T(8,128)S(1)}, f32[2,8,128]{2,1,0:T(8,128)S(1)}, u32[]{:S(2)}, u32[]{:S(2)}) collective-permute-start(f32[2,8,128]{2,1,0:T(8,128)S(1)} %totals.1), channel_id=1, source_target_pairs={{0,128},{16,144},{32,160},{48,176},{64,192},{80,208},{96,224},{112... | collective-permute-start | bytes 24584 | tf_op jit(solution)/shard_map/ppermute | solution.py:686
  45.7 5.9 %collective-permute-start.2 = (f32[2,8,128]{2,1,0:T(8,128)S(1)}, f32[2,8,128]{2,1,0:T(8,128)S(1)}, u32[]{:S(2)}, u32[]{:S(2)}) collective-permute-start(f32[2,8,128]{2,1,0:T(8,128)S(1)} %totals.1), channel_id=1, source_target_pairs={{0,64},{16,80},{32,96},{48,112},{64,128},{80,144},{96,160},{112,17... | collective-permute-start | bytes 24584 | tf_op jit(solution)/shard_map/ppermute | solution.py:686
  51.7 0.0 collective-permute-done.3.two_ref
  51.7 4.5 %collective-permute-done.2.one_ref = f32[2,8,128]{2,1,0:T(8,128)S(1)} collective-permute-done((f32[2,8,128]{2,1,0:T(8,128)S(1)}, f32[2,8,128]{2,1,0:T(8,128)S(1)}, u32[]{:S(2)}, u32[]{:S(2)}) %collective-permute-start.2) | collective-permute-done | bytes 8224 | tf_op jit(solution)/shard_map/ppermute | solution.py:686
  56.2 0.8 states.1
  57.0 10.6 %all-to-all-start.1 = ((bf16[64,8,128]{2,1,0:T(8,128)(2,1)}), bf16[64,8,128]{2,1,0:T(8,128)(2,1)S(1)}, u32[]{:S(2)}, u32[]{:S(2)}) async-start(bf16[64,8,128]{2,1,0:T(8,128)(2,1)} %states.1), calls=%async_computation.1 | async-start | bytes 262144 | tf_op jit(solution)/shard_map/all_to_all | solution.py:710
  67.6 0.0 collective-permute-done.1.x_ref
  67.6 0.0 copy-start
  67.6 1.0 %copy-done = bf16[128,4096]{1,0:T(8,128)(2,1)} copy-done((bf16[128,4096]{1,0:T(8,128)(2,1)}, bf16[128,4096]{1,0:T(8,128)(2,1)S(1)}, u32[]{:S(2)}) %copy-start) | copy-done | bytes 1048600
  68.6 9.1 %earlier.1 = (f32[128,4096]{1,0:T(8,128)S(1)}, bf16[128,4096]{1,0:T(8,128)(2,1)S(1)}, f32[128,4096]{1,0:T(8,128)}) custom-call(bf16[128,12288]{1,0:T(8,128)(2,1)} %q_ref.1, bf16[8,4096]{1,0:T(8,128)(2,1)} %get-tuple-element.33.hq_ref, f32[8,4096]{1,0:T(8,128)} %get-tuple-element.34.tapsq_ref, bf16[128,4096]{1,0:T(8,128)(2,1)} %copy-done, ...), custom_call_target="tpu_custom_call" | custom-call | tf_op jit(solution)/shard_map/earlier/pallas_call | solution.py:533
  77.7 0.4 all-to-all-done.1
  78.0 3.0 %final.1 = bf16[128,4096]{1,0:T(8,128)(2,1)} custom-call(f32[128,4096]{1,0:T(8,128)S(1)} %get-tuple-element.43.acc_ref, f32[128,4096]{1,0:T(8,128)} %get-tuple-element.44.query_hbm, bf16[128,4096]{1,0:T(8,128)(2,1)S(1)} %get-tuple-element.45.dec_ref, bf16[2,32,8,128]{3,2,1,0:T(8,128)(2,1)S(1)} %bitcast.6), custom_call_target="tpu_custom_call" | custom-call | tf_op jit(solution)/shard_map/final/pallas_call | solution.py:657
Async XLA Ops:
  0.9 16.6 %collective-permute-start = (bf16[8,12288]{1,0:T(8,128)(2,1)S(1)}, bf16[8,12288]{1,0:T(8,128)(2,1)S(1)}, u32[]{:S(2)}, u32[]{:S(2)}) collective-permute-start(bf16[8,12288]{1,0:T(8,128)(2,1)S(1)} %slice.3), channel_id=1, source_target_pairs={{0,1},{1,2},{2,3},{3,4},{4,5},{5,6},{6,7},{7,8},{8,9},{9,10},{10,1... | collective-permute-start | bytes 589832 | tf_op jit(solution)/shard_map/ppermute | solution.py:688
  8.5 21.1 %copy-start.1 = (f32[16,256]{1,0:T(8,128)S(1)}, f32[16,256]{1,0:T(8,128)}, u32[]{:S(2)}) copy-start(f32[16,256]{1,0:T(8,128)} %rates_ref.3) | copy-start | bytes 49156
  8.5 21.1 %copy-start.2 = (f32[16,256]{1,0:T(8,128)S(1)}, f32[16,256]{1,0:T(8,128)}, u32[]{:S(2)}) copy-start(f32[16,256]{1,0:T(8,128)} %param.12) | copy-start | bytes 49156
  20.2 47.4 %collective-permute-start.1 = (bf16[128,4096]{1,0:T(8,128)(2,1)}, bf16[128,4096]{1,0:T(8,128)(2,1)S(1)}, u32[]{:S(2)}, u32[]{:S(2)}) collective-permute-start(bf16[128,4096]{1,0:T(8,128)(2,1)} %get-tuple-element.35.x_ref), channel_id=1, source_target_pairs={{0,1},{1,2},{2,3},{3,4},{4,5},{5,6},{6,7},{7,8},{8,9},{9,10},{10,1... | collective-permute-start | bytes 3145736 | tf_op jit(solution)/shard_map/ppermute | solution.py:700
  22.2 20.0 %all-to-all-start = ((bf16[64,8,128]{2,1,0:T(8,128)(2,1)}), bf16[64,8,128]{2,1,0:T(8,128)(2,1)S(1)}, u32[]{:S(2)}, u32[]{:S(2)}) async-start(bf16[64,8,128]{2,1,0:T(8,128)(2,1)} %bitcast.7), calls=%async_computation | async-start | bytes 262144 | tf_op jit(solution)/shard_map/all_to_all | solution.py:697
  42.3 9.3 %collective-permute-start.3 = (f32[2,8,128]{2,1,0:T(8,128)S(1)}, f32[2,8,128]{2,1,0:T(8,128)S(1)}, u32[]{:S(2)}, u32[]{:S(2)}) collective-permute-start(f32[2,8,128]{2,1,0:T(8,128)S(1)} %totals.1), channel_id=1, source_target_pairs={{0,128},{16,144},{32,160},{48,176},{64,192},{80,208},{96,224},{112... | collective-permute-start | bytes 24584 | tf_op jit(solution)/shard_map/ppermute | solution.py:686
  45.7 10.4 %collective-permute-start.2 = (f32[2,8,128]{2,1,0:T(8,128)S(1)}, f32[2,8,128]{2,1,0:T(8,128)S(1)}, u32[]{:S(2)}, u32[]{:S(2)}) collective-permute-start(f32[2,8,128]{2,1,0:T(8,128)S(1)} %totals.1), channel_id=1, source_target_pairs={{0,64},{16,80},{32,96},{48,112},{64,128},{80,144},{96,160},{112,17... | collective-permute-start | bytes 24584 | tf_op jit(solution)/shard_map/ppermute | solution.py:686
  57.0 21.1 %all-to-all-start.1 = ((bf16[64,8,128]{2,1,0:T(8,128)(2,1)}), bf16[64,8,128]{2,1,0:T(8,128)(2,1)S(1)}, u32[]{:S(2)}, u32[]{:S(2)}) async-start(bf16[64,8,128]{2,1,0:T(8,128)(2,1)} %states.1), calls=%async_computation.1 | async-start | bytes 262144 | tf_op jit(solution)/shard_map/all_to_all | solution.py:710
  67.6 1.0 %copy-start = (bf16[128,4096]{1,0:T(8,128)(2,1)}, bf16[128,4096]{1,0:T(8,128)(2,1)S(1)}, u32[]{:S(2)}) copy-start(bf16[128,4096]{1,0:T(8,128)(2,1)S(1)} %collective-permute-done.1.x_ref) | copy-start | bytes 3145732

commit v7 on v6

--- a/solution.py
+++ b/solution.py
@@ -77,6 +77,13 @@
 
 def params(mib=12):
     return pltpu.CompilerParams(vmem_limit_bytes=mib << 20)
+
+
+def run_of(first, step, falling):
+    blocks = [first]
+    for _ in range(BLOCK // 8 - 1):
+        blocks.append(blocks[-1] * step)
+    return jnp.concatenate(blocks[::-1] if falling else blocks, axis=0)
 
 
 def front_kernel(
@@ -111,13 +118,14 @@
         stack_ref[8 * p : 8 * p + SHORT] = taps_ref[p]
     stack_ref[24:40] = rates_ref[...]
     own_mode = iota((MODES, LANES), 0) == iota((MODES, LANES), 1) % MODES
-    behind = (BLOCK - 1 - row).astype(f32)
+    behind = (7 - iota((8, LANES), 0)).astype(f32)
 
     def expand(j, k, half):
         spread = expanded(stack_ref, j, half)
         tapsx_ref[:, tile(j)] = spread[0:24]
         rate = jnp.sum(jnp.where(own_mode, spread[24:40], 0.0), axis=0, keepdims=True)
-        tail_ref[tile(j), :] = jnp.exp(-rate * behind).astype(bf16).T
+        power = run_of(jnp.exp(-rate * behind), jnp.exp(-8.0 * rate), True)
+        tail_ref[tile(j), :] = power.astype(bf16).T
 
     for_halves(stack_ref.shape[1], expand)
     for copy in copies:
@@ -313,8 +321,8 @@
     lane = iota((BLOCK, LANES), 1)
     old = srel_ref[...] < 0
     own_mode = iota((MODES, LANES), 0) == iota((MODES, LANES), 1) % MODES
-    ahead = (row + 1).astype(f32)
-    behind = (BLOCK - 1 - row).astype(f32)
+    ahead = (iota((8, LANES), 0) + 1).astype(f32)
+    behind = (7 - iota((8, LANES), 0)).astype(f32)
     lines_ref[0:MODES] = rates_ref[...]
     lines_ref[MODES:] = scaled_ref[...]
     long_ref[...] = jnp.zeros(long_ref.shape, f32)
@@ -325,9 +333,10 @@
         ratesx_ref[:, tile(j)] = spread[0:MODES]
         rate = jnp.sum(jnp.where(own_mode, spread[0:MODES], 0.0), axis=0, keepdims=True)
         scale = jnp.sum(jnp.where(own_mode, spread[MODES:], 0.0), axis=0, keepdims=True)
-        decay = jnp.where(old, scale * jnp.exp(-rate * ahead), 0.0)
-        dec_ref[:, tile(j)] = decay.astype(bf16)
-        power = scale * jnp.exp(-rate * behind)
+        by_eight = jnp.exp(-8.0 * rate)
+        decay = run_of(scale * jnp.exp(-rate * ahead), by_eight, False)
+        dec_ref[:, tile(j)] = jnp.where(old, decay, 0.0).astype(bf16)
+        power = run_of(scale * jnp.exp(-rate * behind), by_eight, True)
         upper = power.astype(bf16)
         lower = (power - upper.astype(f32)).astype(bf16)
         first = (j - half * (LANES // PER_TILE)) * PER_TILE
@@ -409,49 +418,108 @@
     return summed
 
 
-def band_sum(j, x_ref, taps_ref, mask_ref, acc):
+HALF = BLOCK // 2
+
+
+def set_masks(srel_ref, mask_ref, left_ref, right_ref, lower):
+    row = iota((BLOCK, LANES), 0)
+    lane = iota((BLOCK, LANES), 1)
+    near = slice(0, HALF) if lower else slice(HALF, BLOCK)
+
+    def within(rows, column):
+        if lower:
+            return (column <= row[rows]) & (column >= srel_ref[rows])
+        return (column > row[rows]) & (column - BLOCK >= srel_ref[rows])
+
+    every = slice(0, BLOCK)
+    mask_ref[...] = jnp.where(within(every, lane), 1.0, 0.0).astype(bf16)
+    side = lane[near]
+    valid = within(near, side % HALF + (0 if lower else HALF))
+    left_ref[...] = jnp.where(valid & (side < HALF), 1.0, 0.0).astype(bf16)
+    right_ref[...] = jnp.where(valid & (side >= HALF), 1.0, 0.0).astype(bf16)
+
+
+def mask_scratch():
+    return [
+        pltpu.VMEM((BLOCK, LANES), bf16),
+        pltpu.VMEM((HALF, LANES), bf16),
+        pltpu.VMEM((HALF, LANES), bf16),
+    ]
+
+
+def band_sum(j, x_ref, taps_ref, masks, lower):
+    mask_ref, left_ref, right_ref = masks
     lane_group = iota((1, LANES), 1) // GROUP
-    even = jnp.where(lane_group % 2 == 0, 1.0, 0.0).astype(bf16)
-    odd = jnp.where(lane_group % 2 == 1, 1.0, 0.0).astype(bf16)
+
+    def only(values, count):
+        return jnp.concatenate(
+            [
+                values * jnp.where(lane_group % count == i, 1.0, 0.0).astype(bf16)
+                for i in range(count)
+            ],
+            axis=0,
+        )
+
     x = x_ref[:, tile(j)]
-    both = jnp.concatenate([x * even, x * odd], axis=0)
-    pair_of = iota((BLOCK, LANES), 1) // (2 * GROUP)
+    near = 0 if lower else HALF
+    far = HALF - near
+    both = only(x, 2)
+    four = only(x[near : near + HALF], 4)
     taps = taps_ref[pl.ds(pl.multiple_of(j * PER_TILE, PER_TILE), PER_TILE), :]
-    pairs = []
-    for pair in range(PER_TILE // 2):
-        bands = []
-        for side in range(2):
-            g = 2 * pair + side
-            line = jnp.broadcast_to(taps[g : g + 1], (16, BLOCK))
-            ring = pltpu.roll(line, 1, 1, stride=1, stride_axis=0).astype(bf16)
-            parts = [ring] + [pltpu.roll(ring, 16 * k, 1) for k in range(1, BLOCK // 16)]
-            bands.append(jnp.concatenate(parts, axis=0) * mask_ref[...])
-        pairs.append(jnp.concatenate(bands, axis=1))
+    rings = []
+    for g in range(PER_TILE):
+        line = jnp.broadcast_to(taps[g : g + 1], (16, BLOCK))
+        rings.append(pltpu.roll(line, 1, 1, stride=1, stride_axis=0).astype(bf16))
+
+    def rows_from(g, first, shift):
+        parts = []
+        for k in range(HALF // 16):
+            amount = (first + 16 * k + shift) % BLOCK
+            parts.append(pltpu.roll(rings[g], amount, 1) if amount else rings[g])
+        return jnp.concatenate(parts, axis=0)
+
+    full_mask = mask_ref[far : far + HALF]
+    pairs = [
+        jnp.concatenate(
+            [rows_from(2 * p + i, far, 0) * full_mask for i in range(2)], axis=1
+        )
+        for p in range(PER_TILE // 2)
+    ]
     out = jnp.dot(jnp.concatenate(pairs, axis=0), both, preferred_element_type=f32)
-    picked = out[0:BLOCK]
-    for pair in range(1, PER_TILE // 2):
-        picked = jnp.where(pair_of == pair, out[pair * BLOCK : (pair + 1) * BLOCK], picked)
-    return acc + picked
+    pair_of = iota((HALF, LANES), 1) // (2 * GROUP)
+    full = out[0:HALF]
+    for p in range(1, PER_TILE // 2):
+        full = jnp.where(pair_of == p, out[p * HALF : (p + 1) * HALF], full)
+    left_shift, right_shift = (0, HALF) if lower else (HALF, 0)
+    quads = []
+    for q in range(PER_TILE // 4):
+        sides = []
+        for g in (4 * q, 4 * q + 2):
+            left = rows_from(g, near, left_shift) * left_ref[...]
+            right = rows_from(g + 1, near, right_shift) * right_ref[...]
+            sides.append(left + right)
+        quads.append(jnp.concatenate(sides, axis=1))
+    out = jnp.dot(jnp.concatenate(quads, axis=0), four, preferred_element_type=f32)
+    partial = jnp.where(pair_of >= 2, out[HALF:], out[0:HALF])
+    return jnp.concatenate([partial, full] if lower else [full, partial], axis=0)
 
 
 def own_kernel(
     which_ref, srel_ref, x_ref, own_ref, skip_ref, rates_ref, live_ref,
     acc_ref, decay_ref, live_out,
-    mask_ref,
+    mask_ref, left_ref, right_ref,
 ):
-    row = iota((BLOCK, LANES), 0)
-    lane = iota((BLOCK, LANES), 1)
+    masks = (mask_ref, left_ref, right_ref)
 
     @pl.when(pl.program_id(0) == 0)
     def _():
-        mask = (lane <= row) & (lane >= srel_ref[...])
-        mask_ref[...] = jnp.where(mask, 1.0, 0.0).astype(bf16)
+        set_masks(srel_ref, *masks, True)
         decay_ref[...] = jnp.exp(-rates_ref[...] * float(BLOCK))
         live_out[...] = live_ref[...]
 
     def body(j, k):
         acc = skip_ref[:, tile(j)] * x_ref[:, tile(j)].astype(f32)
-        acc_ref[:, tile(j)] = band_sum(j, x_ref, own_ref, mask_ref, acc)
+        acc_ref[:, tile(j)] = acc + band_sum(j, x_ref, own_ref, masks, True)
 
     for_tiles(CHUNK, body, CHUNK)
 
@@ -487,7 +555,7 @@
                 whole(live.shape),
             ],
             out_specs=(cols(BLOCK), whole((PART, LANES)), whole(live.shape)),
-            scratch_shapes=[pltpu.VMEM((BLOCK, LANES), bf16)],
+            scratch_shapes=mask_scratch(),
         ),
         compiler_params=params(20),
         name="own",
@@ -497,16 +565,15 @@
 def earlier_kernel(
     q_ref, hq_ref, tapsq_ref, x_ref, taps_ref, srel_ref, acc_ref, dec_ref,
     out_ref, dec_out, query_ref,
-    mask_ref, wq_ref, rel_ref, near_ref,
+    mask_ref, left_ref, right_ref, wq_ref, rel_ref, near_ref,
 ):
+    masks = (mask_ref, left_ref, right_ref)
     row = iota((BLOCK, LANES), 0)
-    lane = iota((BLOCK, LANES), 1)
     dec_out[...] = dec_ref[...]
 
     @pl.when(pl.program_id(0) == 0)
     def _():
-        inside = (lane > row) & (lane - BLOCK >= srel_ref[...])
-        mask_ref[...] = jnp.where(inside, 1.0, 0.0).astype(bf16)
+        set_masks(srel_ref, *masks, False)
         rel_ref[...] = row - srel_ref[...]
         find_near(rel_ref, near_ref)
 
@@ -522,7 +589,8 @@
     by_rows(near_ref, rows_of_query)
 
     def body(j, k):
-        out_ref[:, tile(j)] = band_sum(j, x_ref, taps_ref, mask_ref, acc_ref[:, tile(j)])
+        band = band_sum(j, x_ref, taps_ref, masks, False)
+        out_ref[:, tile(j)] = acc_ref[:, tile(j)] + band
 
     for_tiles(CHUNK, body, CHUNK)
 
@@ -549,8 +617,8 @@
             columns(BLOCK),
         ],
         out_specs=(columns(BLOCK), columns(BLOCK), columns(BLOCK)),
-        scratch_shapes=[
-            pltpu.VMEM((BLOCK, LANES), bf16),
+        scratch_shapes=mask_scratch()
+        + [
             pltpu.VMEM((CHUNK, 8 + ROWS, LANES), f32),
             pltpu.VMEM((BLOCK, LANES), i32),
             pltpu.SMEM((BLOCK // ROWS,), i32),

time: 81.5 us -> 80.6 us (0.989)
  Pallas kernels: 33.1 us -> 31.5 us
  waiting for transfers between devices: 13.8 us -> 14.8 us
  transfers between devices with their start and end apart: 6 -> 6, of which waited for: 3 -> 4; matrix products, arithmetic and copies ran while one was open for 1% -> 1% of each run, Pallas kernels for 34% -> 32%
where the time goes in v7:
time: 80.6 us; the launch traced here: 80 us
  Pallas kernels  31.5 us (39%)
  starting transfers between devices  30.9 us (38%)
  waiting for transfers between devices  14.8 us (18%)
  local copies, waits for them, and re-layouts  1.92 us (2%)
    all_to_all x1, starting transfers between devices, per_device(): lax.all_to_all(states, FLAT, split_axis=0, concat_axis=0, tiled=True, axi...  10.4 us
    ppermute x2, starting transfers between devices, from_ctx(): lax.ppermute(value, 'ctx', [(i, i + by) for i in range(ctx_count - by)])  9.13 us
    ppermute x1, waiting for transfers between devices, per_device(): halo = lax.ppermute(projected[BLOCK - 8:], FLAT, onward)  9.01 us
    pallas_call x1, Pallas kernels, make_earlier(): pl.pallas_call(earlier_kernel, grid=(width // WIDE,), out_shape=(shape(ac...  8.52 us
    all_to_all x1, starting transfers between devices, per_device(): lax.all_to_all(items, FLAT, split_axis=0, concat_axis=0, tiled=True, axis...  7.51 us
    pallas_call x1, Pallas kernels, make_own(): pl.pallas_call(own_kernel, out_shape=(pltpu.HBM((BLOCK, width), f32), sha...  6.11 us
    pallas_call x1, Pallas kernels, make_front(): pl.pallas_call(front_kernel, grid=(1,), out_shape=(shape((BLOCK, LANES),...  5.55 us
    pallas_call x1, Pallas kernels, make_tables(): pl.pallas_call(tables_kernel, grid=(1,), out_shape=(pltpu.HBM((BLOCK, wid...  4.73 us
  transfers between devices with their start and end apart: 6, of which 4 were waited for; matrix products, arithmetic and copies ran while one was open for 1% of the time, Pallas kernels for 32%

profile of v7, /device:TPU:2, one launch (start us, length us, event | category | flops | bytes accessed | tf_op | source)
XLA Modules:
  0.0 80.0 jit_solution(16407885541181957341)
XLA Ops:
  0.0 0.9 %slice.3 = bf16[8,12288]{1,0:T(8,128)(2,1)S(1)} slice(bf16[128,12288]{1,0:T(8,128)(2,1)} %q_ref.1), slice={[120:128], [0:12288]} | slice | bytes 393216 | tf_op jit(solution)/shard_map/slice | solution.py:756
  0.9 1.9 %collective-permute-start = (bf16[8,12288]{1,0:T(8,128)(2,1)S(1)}, bf16[8,12288]{1,0:T(8,128)(2,1)S(1)}, u32[]{:S(2)}, u32[]{:S(2)}) collective-permute-start(bf16[8,12288]{1,0:T(8,128)(2,1)S(1)} %slice.3), channel_id=1, source_target_pairs={{0,1},{1,2},{2,3},{3,4},{4,5},{5,6},{6,7},{7,8},{8,9},{9,10},{10,1... | collective-permute-start | bytes 589832 | tf_op jit(solution)/shard_map/ppermute | solution.py:756
  2.9 0.1 pad_add_fusion.place_ref
  3.0 5.5 %front.1 = (s32[128,128]{1,0:T(8,128)S(1)}, f32[64,128]{1,0:T(8,128)S(1)}, f32[24,4096]{1,0:T(8,128)S(1)}, bf16[4096,128]{1,0:T(8,128)(2,1)S(1)}, bf16[128,4096]...) custom-call(s32[2]{0:T(128)S(1)} %pad_add_fusion.place_ref, s32[16]{0:T(128)} %docs_ref.1, f32[3,7,256]{2,1,0:T(8,128)} %taps_ref.1, ...), custom_call_target="tpu_custom_call" | custom-call | tf_op jit(solution)/shard_map/front/pallas_call | solution.py:178
  8.5 0.0 copy-start.1
  8.5 0.0 copy-start.2
  8.5 9.0 %collective-permute-done.halo_ref = bf16[8,12288]{1,0:T(8,128)(2,1)S(1)} collective-permute-done((bf16[8,12288]{1,0:T(8,128)(2,1)S(1)}, bf16[8,12288]{1,0:T(8,128)(2,1)S(1)}, u32[]{:S(2)}, u32[]{:S(2)}) %collective-permute-start) | collective-permute-done | bytes 196640 | tf_op jit(solution)/shard_map/ppermute | solution.py:756
  17.6 2.7 %edge.1 = (bf16[128,4096]{1,0:T(8,128)(2,1)}, bf16[2,32,8,128]{3,2,1,0:T(8,128)(2,1)}, bf16[8,4096]{1,0:T(8,128)(2,1)}, f32[8,4096]{1,0:T(8,128)}, s32[128,128]{1,0:T(8,128)}, /*index=5*/f32[64,128]{1,0:T(8,128)}) custom-call(bf16[128,4096]{1,0:T(8,128)(2,1)S(1)} %get-tuple-element.27.main_ref, bf16[2,8,4096]{2,1,0:T(8,128)(2,1)S(1)} %get-tuple-element.28.head_ref, ...), custom_call_target="tpu_custom_call" | custom-call | tf_op jit(solution)/shard_map/edge/pallas_call | solution.py:291
  20.2 1.9 %collective-permute-start.1 = (bf16[128,4096]{1,0:T(8,128)(2,1)}, bf16[128,4096]{1,0:T(8,128)(2,1)S(1)}, u32[]{:S(2)}, u32[]{:S(2)}) collective-permute-start(bf16[128,4096]{1,0:T(8,128)(2,1)} %get-tuple-element.35.x_ref), channel_id=1, source_target_pairs={{0,1},{1,2},{2,3},{3,4},{4,5},{5,6},{6,7},{7,8},{8,9},{9,10},{10,1... | collective-permute-start | bytes 3145736 | tf_op jit(solution)/shard_map/ppermute | solution.py:768
  22.2 7.5 %all-to-all-start = ((bf16[64,8,128]{2,1,0:T(8,128)(2,1)}), bf16[64,8,128]{2,1,0:T(8,128)(2,1)S(1)}, u32[]{:S(2)}, u32[]{:S(2)}) async-start(bf16[64,8,128]{2,1,0:T(8,128)(2,1)} %bitcast.7), calls=%async_computation | async-start | bytes 262144 | tf_op jit(solution)/shard_map/all_to_all | solution.py:765
  29.7 0.0 copy-done.1
  29.7 0.0 copy-done.2
  29.7 0.6 sqrt_multiply_fusion.scaled_ref
  30.3 4.7 %tables.1 = (bf16[128,4096]{1,0:T(8,128)(2,1)}, f32[256,128]{1,0:T(8,128)S(1)}, f32[256,128]{1,0:T(8,128)}, f32[16,4096]{1,0:T(8,128)S(1)}) custom-call(s32[128,128]{1,0:T(8,128)} %get-tuple-element.36.srel_ref, f32[16,256]{1,0:T(8,128)} %rates_ref.3, f32[16,256]{1,0:T(8,128)} %sqrt_multiply_fusion.scaled_ref, f32[128,256]{1,0:T(8,128)} %medium_ref.1), custom_call_target="tpu_custom_call" | custom-call | tf_op jit(solution)/shard_map/tables/pallas_call | solution.py:363
  35.1 6.1 %own.1 = (f32[128,4096]{1,0:T(8,128)}, f32[8,128]{1,0:T(8,128)S(1)}, f32[64,128]{1,0:T(8,128)S(1)}) custom-call(s32[1]{0:T(128)} %bitcast.2.which_ref, s32[128,128]{1,0:T(8,128)} %get-tuple-element.36.srel_ref, bf16[128,4096]{1,0:T(8,128)(2,1)} %get-tuple-element.35.x_ref, f32[256,128]{1,0:T(8,128)S(1)} %get-tuple-element.38.own_ref, f32[1,4096]{1,0:T(1,128)} %bitcast.8, ...), custom_call_target="tpu_custom_call" | custom-call | tf_op jit(solution)/shard_map/own/pallas_call | solution.py:539
  41.2 0.3 all-to-all-done.terms_ref
  41.5 0.1 totals.1
  41.6 3.4 %collective-permute-start.3 = (f32[2,8,128]{2,1,0:T(8,128)S(1)}, f32[2,8,128]{2,1,0:T(8,128)S(1)}, u32[]{:S(2)}, u32[]{:S(2)}) collective-permute-start(f32[2,8,128]{2,1,0:T(8,128)S(1)} %totals.1), channel_id=1, source_target_pairs={{0,128},{16,144},{32,160},{48,176},{64,192},{80,208},{96,224},{112... | collective-permute-start | bytes 24584 | tf_op jit(solution)/shard_map/ppermute | solution.py:754
  45.0 5.7 %collective-permute-start.2 = (f32[2,8,128]{2,1,0:T(8,128)S(1)}, f32[2,8,128]{2,1,0:T(8,128)S(1)}, u32[]{:S(2)}, u32[]{:S(2)}) collective-permute-start(f32[2,8,128]{2,1,0:T(8,128)S(1)} %totals.1), channel_id=1, source_target_pairs={{0,64},{16,80},{32,96},{48,112},{64,128},{80,144},{96,160},{112,17... | collective-permute-start | bytes 24584 | tf_op jit(solution)/shard_map/ppermute | solution.py:754
  50.7 0.0 collective-permute-done.3.two_ref
  50.8 4.6 %collective-permute-done.2.one_ref = f32[2,8,128]{2,1,0:T(8,128)S(1)} collective-permute-done((f32[2,8,128]{2,1,0:T(8,128)S(1)}, f32[2,8,128]{2,1,0:T(8,128)S(1)}, u32[]{:S(2)}, u32[]{:S(2)}) %collective-permute-start.2) | collective-permute-done | bytes 8224 | tf_op jit(solution)/shard_map/ppermute | solution.py:754
  55.4 0.8 states.1
  56.1 10.4 %all-to-all-start.1 = ((bf16[64,8,128]{2,1,0:T(8,128)(2,1)}), bf16[64,8,128]{2,1,0:T(8,128)(2,1)S(1)}, u32[]{:S(2)}, u32[]{:S(2)}) async-start(bf16[64,8,128]{2,1,0:T(8,128)(2,1)} %states.1), calls=%async_computation.1 | async-start | bytes 262144 | tf_op jit(solution)/shard_map/all_to_all | solution.py:778
  66.6 0.0 collective-permute-done.1.x_ref
  66.6 0.0 copy-start
  66.6 1.0 %copy-done = bf16[128,4096]{1,0:T(8,128)(2,1)} copy-done((bf16[128,4096]{1,0:T(8,128)(2,1)}, bf16[128,4096]{1,0:T(8,128)(2,1)S(1)}, u32[]{:S(2)}) %copy-start) | copy-done | bytes 1048600
  67.6 8.5 %earlier.1 = (f32[128,4096]{1,0:T(8,128)S(1)}, bf16[128,4096]{1,0:T(8,128)(2,1)S(1)}, f32[128,4096]{1,0:T(8,128)}) custom-call(bf16[128,12288]{1,0:T(8,128)(2,1)} %q_ref.1, bf16[8,4096]{1,0:T(8,128)(2,1)} %get-tuple-element.33.hq_ref, f32[8,4096]{1,0:T(8,128)} %get-tuple-element.34.tapsq_ref, bf16[128,4096]{1,0:T(8,128)(2,1)} %copy-done, ...), custom_call_target="tpu_custom_call" | custom-call | tf_op jit(solution)/shard_map/earlier/pallas_call | solution.py:601
  76.1 0.9 %all-to-all-done.1 = bf16[64,8,128]{2,1,0:T(8,128)(2,1)S(1)} async-done(((bf16[64,8,128]{2,1,0:T(8,128)(2,1)}), bf16[64,8,128]{2,1,0:T(8,128)(2,1)S(1)}, u32[]{:S(2)}, u32[]{:S(2)}) %all-to-all-start.1) | async-done | bytes 131104 | tf_op jit(solution)/shard_map/all_to_all | solution.py:778
  77.0 3.0 %final.1 = bf16[128,4096]{1,0:T(8,128)(2,1)} custom-call(f32[128,4096]{1,0:T(8,128)S(1)} %get-tuple-element.43.acc_ref, f32[128,4096]{1,0:T(8,128)} %get-tuple-element.44.query_hbm, bf16[128,4096]{1,0:T(8,128)(2,1)S(1)} %get-tuple-element.45.dec_ref, bf16[2,32,8,128]{3,2,1,0:T(8,128)(2,1)S(1)} %bitcast.6), custom_call_target="tpu_custom_call" | custom-call | tf_op jit(solution)/shard_map/final/pallas_call | solution.py:725
Async XLA Ops:
  0.9 16.6 %collective-permute-start = (bf16[8,12288]{1,0:T(8,128)(2,1)S(1)}, bf16[8,12288]{1,0:T(8,128)(2,1)S(1)}, u32[]{:S(2)}, u32[]{:S(2)}) collective-permute-start(bf16[8,12288]{1,0:T(8,128)(2,1)S(1)} %slice.3), channel_id=1, source_target_pairs={{0,1},{1,2},{2,3},{3,4},{4,5},{5,6},{6,7},{7,8},{8,9},{9,10},{10,1... | collective-permute-start | bytes 589832 | tf_op jit(solution)/shard_map/ppermute | solution.py:756
  8.5 21.2 %copy-start.1 = (f32[16,256]{1,0:T(8,128)S(1)}, f32[16,256]{1,0:T(8,128)}, u32[]{:S(2)}) copy-start(f32[16,256]{1,0:T(8,128)} %rates_ref.3) | copy-start | bytes 49156
  8.5 21.2 %copy-start.2 = (f32[16,256]{1,0:T(8,128)S(1)}, f32[16,256]{1,0:T(8,128)}, u32[]{:S(2)}) copy-start(f32[16,256]{1,0:T(8,128)} %param.12) | copy-start | bytes 49156
  20.2 46.4 %collective-permute-start.1 = (bf16[128,4096]{1,0:T(8,128)(2,1)}, bf16[128,4096]{1,0:T(8,128)(2,1)S(1)}, u32[]{:S(2)}, u32[]{:S(2)}) collective-permute-start(bf16[128,4096]{1,0:T(8,128)(2,1)} %get-tuple-element.35.x_ref), channel_id=1, source_target_pairs={{0,1},{1,2},{2,3},{3,4},{4,5},{5,6},{6,7},{7,8},{8,9},{9,10},{10,1... | collective-permute-start | bytes 3145736 | tf_op jit(solution)/shard_map/ppermute | solution.py:768
  22.2 19.3 %all-to-all-start = ((bf16[64,8,128]{2,1,0:T(8,128)(2,1)}), bf16[64,8,128]{2,1,0:T(8,128)(2,1)S(1)}, u32[]{:S(2)}, u32[]{:S(2)}) async-start(bf16[64,8,128]{2,1,0:T(8,128)(2,1)} %bitcast.7), calls=%async_computation | async-start | bytes 262144 | tf_op jit(solution)/shard_map/all_to_all | solution.py:765
  41.6 9.1 %collective-permute-start.3 = (f32[2,8,128]{2,1,0:T(8,128)S(1)}, f32[2,8,128]{2,1,0:T(8,128)S(1)}, u32[]{:S(2)}, u32[]{:S(2)}) collective-permute-start(f32[2,8,128]{2,1,0:T(8,128)S(1)} %totals.1), channel_id=1, source_target_pairs={{0,128},{16,144},{32,160},{48,176},{64,192},{80,208},{96,224},{112... | collective-permute-start | bytes 24584 | tf_op jit(solution)/shard_map/ppermute | solution.py:754
  45.0 10.4 %collective-permute-start.2 = (f32[2,8,128]{2,1,0:T(8,128)S(1)}, f32[2,8,128]{2,1,0:T(8,128)S(1)}, u32[]{:S(2)}, u32[]{:S(2)}) collective-permute-start(f32[2,8,128]{2,1,0:T(8,128)S(1)} %totals.1), channel_id=1, source_target_pairs={{0,64},{16,80},{32,96},{48,112},{64,128},{80,144},{96,160},{112,17... | collective-permute-start | bytes 24584 | tf_op jit(solution)/shard_map/ppermute | solution.py:754
  56.1 20.8 %all-to-all-start.1 = ((bf16[64,8,128]{2,1,0:T(8,128)(2,1)}), bf16[64,8,128]{2,1,0:T(8,128)(2,1)S(1)}, u32[]{:S(2)}, u32[]{:S(2)}) async-start(bf16[64,8,128]{2,1,0:T(8,128)(2,1)} %states.1), calls=%async_computation.1 | async-start | bytes 262144 | tf_op jit(solution)/shard_map/all_to_all | solution.py:778
  66.6 1.0 %copy-start = (bf16[128,4096]{1,0:T(8,128)(2,1)}, bf16[128,4096]{1,0:T(8,128)(2,1)S(1)}, u32[]{:S(2)}) copy-start(bf16[128,4096]{1,0:T(8,128)(2,1)S(1)} %collective-permute-done.1.x_ref) | copy-start | bytes 3145732
